TPU v7x, 32 devices: a whole 2x2x4 slice. The times are simulated.
32 devices in a mesh: seq: 8 (over y, x, core), emb: 4 (over z).
Axes of the slice: x: 2, y: 2, z: 4, core: 2. Of those that a mesh axis runs over, the one named last changes fastest.
Arguments:
- item_ids: int32 [16384], P('seq'), may hold values from 0 to 32767
- domains: int32 [16384], P(('seq', 'emb')), may hold values from 0 to 3, as said below
- live_counts: int32 [32], P(('seq', 'emb')), may hold values from 128 to 512, as said below
- table: bfloat16 [32768, 512], P(None, 'emb'), may hold values from -30 to 30
- norm_gains: float32 [3, 512], replicated, may hold values from 0.25 to 1.75
- proj_in: bfloat16 [512, 2048], replicated, may hold values from -0.25 to 0.25
- proj_out: bfloat16 [512, 512], replicated, may hold values from -0.25 to 0.25
- expert_in: bfloat16 [4, 512, 4096], P('emb'), may hold values from -0.25 to 0.25
- expert_out: bfloat16 [4, 2048, 512], P('emb'), may hold values from -0.125 to 0.125
Outputs:
- mixed: bfloat16 [16384, 512], P(('seq', 'emb'))
Inputs may be any that keep to these rules, and one draw needn't show every extreme that they name: `domains`: in the 512 events of one block no domain appears more than 256 times; in every group of 4 consecutive blocks some domain appears exactly 256 times in each block. `live_counts`: some block has all 512 events live.
All inputs are finite; a program needn't handle non-finite values.
Results may differ from a plain program's by a relative error of at most 0.006.
Values may be sent and summed in bfloat16 or wider, within the bound.
No kernel may reach another device: no remote copies, remote signals or barrier semaphores. Data moves between devices by JAX's collectives and lax.ppermute only.
A program may use at most 128 MiB of HBM per device.

v0:
```python
import math

import jax
import jax.numpy as jnp
from jax import lax
from jax.experimental import pallas as pl
from jax.experimental.pallas import tpu as pltpu
from jax.sharding import PartitionSpec as P


HEADS = 8
HEAD_DIM = 64
SPAN = 4
NORM_EPS = 1e-06
CHUNKS = (0.5, 0.25, 0.25)
KEY_TILE = 256
TAIL = 16
MIB = 1 << 20

F32 = jnp.float32
BF16 = jnp.bfloat16
I32 = jnp.int32


def shifted(value, axis, steps):
    count = lax.axis_size(axis)
    first, last = (max(0, -steps), min(count, count - steps))
    return lax.ppermute(value, axis, [(source, source + steps) for source in range(first, last)])


def rotated(value, axis, steps):
    count = lax.axis_size(axis)
    return lax.ppermute(value, axis, [(source, (source + steps) % count) for source in range(count)])


def rms_norm(values, gain):
    return values * lax.rsqrt(jnp.mean(values * values, axis=-1, keepdims=True) + NORM_EPS) * gain


def half_silu(half):
    return half + half * jnp.tanh(half)


VMEM_SPEC = pl.BlockSpec(memory_space=pltpu.VMEM)
SMEM_SPEC = pl.BlockSpec(memory_space=pltpu.SMEM)


def cost(flops, nbytes):
    return pl.CostEstimate(flops=int(flops), bytes_accessed=int(nbytes), transcendentals=0)


def limit(mib):
    return pltpu.CompilerParams(vmem_limit_bytes=mib * MIB)


def make_weights(model_width, width):
    def kernel(me, w_q, w_k, w_v, out):
        queries = w_q[...]
        low = lax.broadcasted_iota(I32, queries.shape, 1) < HEAD_DIM
        zero = jnp.zeros_like(queries)
        out[:, :width] = jnp.where(low, queries, zero)
        out[:, width : 2 * width] = jnp.where(low, zero, queries)
        out[:, 2 * width : 3 * width] = w_k[...]
        out[:, 3 * width :] = w_v[...]

    per = model_width // width
    block = lambda index: pl.BlockSpec(
        (model_width, width), lambda i, me: (0, index * per + me[0])
    )
    return pl.pallas_call(
        kernel,
        grid_spec=pltpu.PrefetchScalarGridSpec(
            num_scalar_prefetch=1,
            grid=(1,),
            in_specs=[block(1), block(2), block(3)],
            out_specs=pl.BlockSpec((model_width, 4 * width), lambda i, me: (0, 0)),
        ),
        out_shape=jax.ShapeDtypeStruct((model_width, 4 * width), BF16),
        compiler_params=limit(4),
        cost_estimate=cost(0, 16 * model_width * width),
        name="weights",
    )


def make_project(group, blocks, block_rows, width, model_width):
    lane = model_width // group
    first, past = blocks
    per = past - first
    rows = per * block_rows
    opening = first == 0

    def kernel(me_ref, *refs):
        refs = list(refs)
        take = lambda number: [refs.pop(0) for _ in range(number)]
        known = None if opening else take(1)[0]
        pieces = take(group)
        gains, weights = take(2)
        q_ref, kv_ref, own_ref = take(3)
        lives_ref = take(1)[0] if opening else None
        emb_ref = take(1)[0]
        me = me_ref[0]
        offsets = (0, group - 1, 1, 2)
        for piece, offset in zip(pieces, offsets):
            column = lax.rem(me + offset, group)
            emb_ref[:, pl.ds(pl.multiple_of(column * lane, lane), lane)] = piece[pl.ds(0, rows), :]
            if opening:
                code = piece[rows : rows + TAIL, :].astype(F32)
                high, low = jnp.max(code[: TAIL // 2]), jnp.max(code[TAIL // 2 :])
                lives_ref[column] = (high * TAIL + low).astype(I32)
        lives = [(lives_ref if opening else known)[b] for b in range(group)]
        for part in range(per):
            here = pl.ds(part * block_rows, block_rows)
            position = lax.broadcasted_iota(I32, (block_rows, 1), 0)
            mask = (position < lives[first + part]).astype(F32)
            embedded = emb_ref[here, :].astype(F32)
            normed = (rms_norm(embedded, gains[0:1, :]) * mask).astype(BF16)
            projected = jnp.dot(normed, weights[...], preferred_element_type=F32)
            scale = 0.5 / math.sqrt(HEAD_DIM)
            q_ref[here, :] = projected[:, : 2 * width].astype(BF16) * jnp.asarray(scale, BF16)
            kv_ref[here, :] = projected[:, 2 * width :].astype(BF16)
        if opening:
            row = lax.broadcasted_iota(I32, (TAIL, 2 * width), 0)
            code = jnp.zeros((TAIL, 2 * width), F32)
            for b in range(group):
                high = lax.div(lives[b], TAIL)
                code = jnp.where(row == b, high.astype(F32), code)
                code = jnp.where(row == group + b, (lives[b] - high * TAIL).astype(F32), code)
            kv_ref[pl.ds(rows, TAIL), :] = code.astype(BF16)
        at = jnp.clip(me - first, 0, per - 1) * block_rows
        own_ref[...] = emb_ref[pl.ds(pl.multiple_of(at, block_rows), block_rows), :]

    more = TAIL if opening else 0
    out_shape = (
        jax.ShapeDtypeStruct((rows, 2 * width), BF16),
        jax.ShapeDtypeStruct((rows + more, 2 * width), BF16),
        jax.ShapeDtypeStruct((block_rows, model_width), BF16),
    )
    out_specs = (VMEM_SPEC,) * 3
    if opening:
        out_shape += (jax.ShapeDtypeStruct((group,), I32),)
        out_specs += (SMEM_SPEC,)
    return pl.pallas_call(
        kernel,
        out_shape=out_shape,
        in_specs=[SMEM_SPEC] * (1 if opening else 2) + [VMEM_SPEC] * (group + 2),
        out_specs=out_specs,
        scratch_shapes=[pltpu.VMEM((rows, model_width), BF16)],
        compiler_params=limit(16),
        cost_estimate=cost(2 * rows * model_width * 4 * width, 4 * rows * model_width),
    )


def pair(queries, q_at, q_pos, kv_ref, k_at, k_pos, acc_ref, acc_at, rows, keep, live, width):
    tiles = lax.div(live + (KEY_TILE - 1), KEY_TILE)

    def step(tile, carry):
        at = pl.ds(pl.multiple_of(k_at + tile * KEY_TILE, KEY_TILE), KEY_TILE)
        keys = kv_ref[at, :width]
        values = kv_ref[at, width:]
        low = lax.broadcasted_iota(I32, values.shape, 1) < HEAD_DIM
        zero = jnp.zeros_like(values)
        total = None
        for head in range(2):
            half = lax.dot_general(
                queries[pl.ds(q_at, rows), head * width : (head + 1) * width],
                keys,
                (((1,), (1,)), ((), ())),
                preferred_element_type=F32,
            )
            weights = half_silu(half)
            if keep is not None:
                query = lax.broadcasted_iota(I32, weights.shape, 0) + q_pos
                key = lax.broadcasted_iota(I32, weights.shape, 1) + (k_pos + tile * KEY_TILE)
                weights = jnp.where(keep(query, key), weights, 0.0)
            held = jnp.where(low, values, zero) if head == 0 else jnp.where(low, zero, values)
            term = jnp.dot(weights.astype(BF16), held, preferred_element_type=F32)
            total = term if total is None else total + term
        acc_ref[pl.ds(acc_at, rows), :] += total
        return carry

    lax.fori_loop(0, tiles, step, 0)


def from_before(query, key):
    return key >= query


def from_after(query, key):
    return key <= query


def read_lives(kv_ref, rows, group):
    code = kv_ref[pl.ds(rows, TAIL), :].astype(F32)
    return [
        (jnp.max(code[b : b + 1]) * TAIL + jnp.max(code[group + b : group + b + 1])).astype(I32)
        for b in range(group)
    ]


def spans(first, past, chunks):
    for index, (start, end) in enumerate(chunks):
        low, high = max(first, start), min(past, end)
        if low < high:
            yield index, low, high


def make_own(chunks, opening, block_rows, width):
    count = 1 if opening else len(chunks)
    group = chunks[-1][1]
    first_end = chunks[0][1]
    total = (first_end if opening else group) * block_rows

    def kernel(lives_ref, *refs):
        refs = list(refs)
        take = lambda number: [refs.pop(0) for _ in range(number)]
        queries = take(count)
        keys = take(count)
        if opening:
            (acc,) = take(1)
            acc[...] = jnp.zeros_like(acc)
        else:
            (old,) = take(1)
            acc, q_all = take(2)
            done = first_end * block_rows
            acc[pl.ds(0, done), :] = old[...]
            acc[pl.ds(done, total - done), :] = jnp.zeros((total - done, width), F32)
            for (low, high), ref in zip(chunks, queries):
                q_all[pl.ds(low * block_rows, (high - low) * block_rows), :] = ref[...]
        for k in range(first_end if opening else group):
            home = next(spans(k, k + 1, chunks))[0]
            start = 0 if opening or k >= first_end else first_end
            end = first_end if opening else group
            held = queries[0] if opening else q_all
            while start < end:
                past = min(start + 2, end)
                pair(
                    held,
                    start * block_rows,
                    start * block_rows,
                    keys[home],
                    (k - chunks[home][0]) * block_rows,
                    k * block_rows,
                    acc,
                    start * block_rows,
                    (past - start) * block_rows,
                    None,
                    lives_ref[k],
                    width,
                )
                start = past

    out = (jax.ShapeDtypeStruct((total, width), F32),)
    if not opening:
        out += (jax.ShapeDtypeStruct((total, 2 * width), BF16),)
    pairs = first_end**2 if opening else group**2 - first_end**2
    return pl.pallas_call(
        kernel,
        out_shape=out,
        in_specs=[SMEM_SPEC] + [VMEM_SPEC] * (2 * count + (0 if opening else 1)),
        out_specs=(VMEM_SPEC,) * len(out),
        compiler_params=limit(24),
        cost_estimate=cost(pairs * block_rows**2 * 2048, total * width * 8),
        name="own0" if opening else "own1",
    )


def make_turn(turn, chunks, block_rows, width):
    count = len(chunks)
    blocks = chunks[-1][1]
    head_rows = chunks[0][1] * block_rows

    def kernel(me_ref, *refs):
        before, after = refs[:count], refs[count : 2 * count]
        queries, old, out, acc = refs[2 * count :]
        q = lax.rem(me_ref[0] + 1 + turn, blocks)
        at = pl.multiple_of(q * block_rows, block_rows)
        lives_before = read_lives(before[0], head_rows, blocks)
        lives_after = read_lives(after[0], head_rows, blocks)
        acc[...] = old[pl.ds(at, block_rows), :]
        for k in range(blocks):
            home = next(spans(k, k + 1, chunks))[0]
            for held, keep, live in (
                (before, from_before, jnp.where(q <= k, lives_before[k], 0)),
                (after, from_after, jnp.where(q >= k, lives_after[k], 0)),
            ):
                pair(
                    queries,
                    at,
                    at,
                    held[home],
                    (k - chunks[home][0]) * block_rows,
                    k * block_rows,
                    acc,
                    0,
                    block_rows,
                    keep,
                    live,
                    width,
                )
        out[...] = acc[...].astype(BF16)

    return pl.pallas_call(
        kernel,
        out_shape=jax.ShapeDtypeStruct((block_rows, width), BF16),
        in_specs=[SMEM_SPEC] + [VMEM_SPEC] * (2 * count + 2),
        out_specs=VMEM_SPEC,
        scratch_shapes=[pltpu.VMEM((block_rows, width), F32)],
        compiler_params=limit(20),
        cost_estimate=cost(5 * block_rows**2 * 2048, block_rows * width * 8),
    )


def make_gate(group, chunks, rows, model_width, capacity):
    count = len(chunks)

    def kernel(me_ref, live_ref, *refs):
        candidates = refs[:count]
        gains, weights, domains, gating, emb_ref, slot_row, slot_col = refs[count:]
        me, live = me_ref[0], live_ref[0]
        for c in range(count):

            @pl.when((me >= chunks[c][0]) & (me < chunks[c][1]))
            def _():
                emb_ref[...] = candidates[c][...]

        position = lax.broadcasted_iota(I32, (rows, 1), 0)
        mask = (position < live).astype(F32)
        normed = (rms_norm(emb_ref[...].astype(F32), gains[0:1, :]) * mask).astype(BF16)
        gate = jnp.dot(normed, weights[...], preferred_element_type=F32)
        gating[...] = half_silu(gate * 0.5)
        turn = lax.rem(domains[...] - me + group, group)
        alive = lax.broadcasted_iota(I32, (1, rows), 1) < live
        expert = lax.broadcasted_iota(I32, (8, rows), 0)
        onehot = jnp.where((expert == turn) & alive, 1.0, 0.0)
        earlier = lax.broadcasted_iota(I32, (rows, rows), 0) < lax.broadcasted_iota(
            I32, (rows, rows), 1
        )
        rank = jnp.dot(
            onehot.astype(BF16),
            jnp.where(earlier, 1.0, 0.0).astype(BF16),
            preferred_element_type=F32,
        )
        slot = jnp.sum(onehot * (rank + (expert * capacity).astype(F32)), axis=0, keepdims=True)
        slot = jnp.where(alive, slot, -1.0)
        slot_row[...] = slot.astype(I32)
        slot_col[...] = jnp.transpose(jnp.broadcast_to(slot, (128, rows))).astype(I32)

    return pl.pallas_call(
        kernel,
        grid=(1,),
        out_shape=(
            jax.ShapeDtypeStruct((rows, model_width), F32),
            jax.ShapeDtypeStruct((rows, model_width), BF16),
            jax.ShapeDtypeStruct((1, rows), I32),
            jax.ShapeDtypeStruct((rows, 128), I32),
        ),
        in_specs=[SMEM_SPEC] * 2
        + [VMEM_SPEC] * (count + 1)
        + [pl.BlockSpec((model_width, model_width), lambda i: (0, 0)), VMEM_SPEC],
        out_specs=(VMEM_SPEC,) * 4,
        compiler_params=limit(12),
        cost_estimate=cost(2 * rows * model_width**2, 8 * rows * model_width),
        name="gate",
    )


def make_route(group, rows, width, model_width, capacity):
    def kernel(me_ref, *refs):
        pieces = refs[:group]
        gating, emb, gains, proj_out, slot = refs[group : group + 5]
        hidden_ref = refs[group + 5]
        sent = refs[group + 6 : group + 6 + group]
        att = refs[group + 6 + group]
        me = me_ref[0]
        for turn, piece in enumerate(pieces):
            column = lax.rem(me + group - 1 - turn, group)
            att[:, pl.ds(pl.multiple_of(column * width, width), width)] = piece[...].astype(F32)
        gated = (rms_norm(att[...], gains[1:2, :]) * gating[...]).astype(BF16)
        hidden = emb[...].astype(F32) + jnp.dot(
            gated, proj_out[...], preferred_element_type=F32
        )
        hidden_ref[...] = hidden
        routed = rms_norm(hidden, gains[2:3, :]).astype(BF16)
        for turn in range(group):
            place = lax.broadcasted_iota(I32, (capacity, rows), 0) + turn * capacity
            pick = jnp.where(place == slot[...], 1.0, 0.0).astype(BF16)
            sent[turn][...] = jnp.dot(pick, routed, preferred_element_type=F32).astype(BF16)

    return pl.pallas_call(
        kernel,
        out_shape=(jax.ShapeDtypeStruct((rows, model_width), F32),)
        + (jax.ShapeDtypeStruct((capacity, model_width), BF16),) * group,
        in_specs=[SMEM_SPEC] + [VMEM_SPEC] * (group + 5),
        out_specs=(VMEM_SPEC,) * (group + 1),
        scratch_shapes=[pltpu.VMEM((rows, model_width), F32)],
        compiler_params=limit(16),
        cost_estimate=cost(6 * rows * model_width**2, 8 * rows * model_width),
        name="route",
    )


def make_expert(rows, model_width, hidden):
    tile = hidden // 4

    def kernel(x, w_in, w_out, out):
        total = None
        for at in range(0, hidden, tile):
            gate = jnp.dot(x[...], w_in[0, :, at : at + tile], preferred_element_type=F32)
            up = jnp.dot(
                x[...], w_in[0, :, hidden + at : hidden + at + tile], preferred_element_type=F32
            )
            activated = (half_silu(gate * 0.5) * up).astype(BF16)
            term = jnp.dot(activated, w_out[0, at : at + tile, :], preferred_element_type=F32)
            total = term if total is None else total + term
        out[...] = total.astype(BF16)

    return pl.pallas_call(
        kernel,
        out_shape=jax.ShapeDtypeStruct((rows, model_width), BF16),
        in_specs=[VMEM_SPEC] * 3,
        out_specs=VMEM_SPEC,
        compiler_params=limit(16),
        cost_estimate=cost(6 * rows * model_width * hidden, 4 * rows * model_width),
        name="expert",
    )


def make_mix(group, rows, model_width, capacity):
    def kernel(live_ref, *refs):
        pieces = refs[:group]
        hidden, slot, out = refs[group:]
        total = hidden[...]
        where = slot[:, 0:1]
        for turn, piece in enumerate(pieces):
            place = lax.broadcasted_iota(I32, (rows, capacity), 1) + turn * capacity
            pick = jnp.where(place == where, 1.0, 0.0).astype(BF16)
            total = total + jnp.dot(pick, piece[...], preferred_element_type=F32)
        position = lax.broadcasted_iota(I32, (rows, 1), 0)
        mask = (position < live_ref[0]).astype(F32)
        out[...] = (mask * total).astype(BF16)

    return pl.pallas_call(
        kernel,
        out_shape=jax.ShapeDtypeStruct((rows, model_width), BF16),
        in_specs=[SMEM_SPEC] + [VMEM_SPEC] * (group + 2),
        out_specs=VMEM_SPEC,
        compiler_params=limit(12),
        cost_estimate=cost(2 * rows * rows * model_width * 2, 8 * rows * model_width),
        name="mix",
    )


def by_heads(
    item_ids, domains, live_counts, table, norm_gains, proj_in, proj_out, expert_in, expert_out
):
    group = lax.axis_size("emb")
    me = lax.axis_index("emb").astype(I32)[None]
    rows = domains.shape[0]
    model_width = proj_out.shape[0]
    hidden_units = expert_out.shape[1]
    width = model_width // group
    capacity = 2 * rows // group
    ends = [round(group * sum(CHUNKS[: c + 1])) for c in range(len(CHUNKS))]
    chunks = list(zip([0, *ends[:-1]], ends))

    high = lax.div(live_counts[0], TAIL)
    code = jnp.where(jnp.arange(TAIL, dtype=I32) < TAIL // 2, high, live_counts[0] - high * TAIL)
    code = jnp.broadcast_to(code.astype(BF16)[:, None], (TAIL, width))
    cut = chunks[0][1] * rows
    opening = jnp.concatenate((table[item_ids[:cut]], code))
    rest = table[item_ids[cut:]]
    mine = [opening] + [rest[a * rows - cut : b * rows - cut] for a, b in chunks[1:]]
    low, high, far = [], [], []
    for c, piece in enumerate(mine):
        low.append(rotated(piece, "emb", 1))
        high.append(rotated(piece, "emb", -1))
        far.append(rotated(low[c], "emb", 1))

    weights = make_weights(model_width, width)(me, proj_in, proj_in, proj_in)
    queries, own, before, after, candidates = [], [], [], [], []
    lives = acc = None
    for c, blocks in enumerate(chunks):
        project = make_project(group, blocks, rows, width, model_width)
        known = () if c == 0 else (lives,)
        pieces = (mine[c], low[c], high[c], far[c])
        if c == 1:
            pieces, acc = lax.optimization_barrier((pieces, acc))
        q, kv, emb, *more = project(me, *known, *pieces, norm_gains, weights)
        lives = more[0] if c == 0 else lives
        queries.append(q)
        own.append(kv)
        candidates.append(emb)
        before.append(shifted(kv, "seq", 1))
        after.append(shifted(kv, "seq", -1))
        if c == 0:
            (acc,) = make_own(chunks, True, rows, width)(lives, q, kv)
    acc, q_all = make_own(chunks, False, rows, width)(lives, *queries, *own, acc)

    gating, own_embedded, slot_row, slot_col = make_gate(
        group, chunks, rows, model_width, capacity
    )(me, live_counts, *candidates, norm_gains, proj_in, domains[None, :])

    pieces = []
    for t in range(group):
        turn = make_turn(t, chunks, rows, width)
        heads = turn(me, *before, *after, q_all, acc)
        if t < group - 1:
            heads = rotated(heads, "emb", t + 1)
        pieces.append(heads)
    route = make_route(group, rows, width, model_width, capacity)
    hidden, *sent = route(me, *pieces, gating, own_embedded, norm_gains, proj_out, slot_row)
    expert = make_expert(capacity, model_width, hidden_units)
    arrived = [sent[0]]
    for k in range(1, group):
        arrived.append(rotated(sent[k], "emb", k))
    returned = []
    for k in range(group):
        made = expert(arrived[k], expert_in, expert_out)
        if k > 0:
            made = rotated(made, "emb", -k)
        returned.append(made)
    mix = make_mix(group, rows, model_width, capacity)
    return mix(live_counts, *returned, hidden, slot_col)


def by_rows(
    item_ids, domains, live_counts, table, norm_gains, proj_in, proj_out, expert_in, expert_out
):
    rows_dev = domains.shape[0]
    model_width = proj_out.shape[0]
    hidden_units = expert_out.shape[1]
    group_size = lax.axis_size("emb")
    capacity = 2 * rows_dev // group_size
    columns = table[item_ids]
    embedded = lax.all_to_all(columns, "emb", split_axis=0, concat_axis=1, tiled=True).astype(
        jnp.float32
    )
    positions = jnp.arange(rows_dev, dtype=jnp.int32)
    live_mask = (positions < live_counts[0]).astype(jnp.float32)
    normed = (rms_norm(embedded, norm_gains[0]) * live_mask[:, None]).astype(jnp.bfloat16)
    projected = jnp.dot(normed, proj_in, preferred_element_type=jnp.float32)
    gating = jax.nn.silu(projected[:, :model_width])
    queries = (
        projected[:, model_width : 2 * model_width]
        .astype(jnp.bfloat16)
        .reshape(rows_dev, HEADS, HEAD_DIM)
    )
    own_pair = jnp.stack(
        (
            projected[:, 2 * model_width : 3 * model_width].astype(jnp.bfloat16),
            projected[:, 3 * model_width :].astype(jnp.bfloat16),
        )
    )
    key_weights = proj_in[:, 2 * model_width :]
    upper_band = positions[None, :] >= positions[:, None]
    lower_band = positions[None, :] <= positions[:, None]
    score_scale = 1.0 / math.sqrt(HEAD_DIM)

    def unpack(piece):
        rebuilt = jnp.dot(piece[0], key_weights, preferred_element_type=jnp.float32)
        return jnp.stack(
            (
                rebuilt[:, :model_width].astype(jnp.bfloat16),
                rebuilt[:, model_width:].astype(jnp.bfloat16),
            )
        )

    def attend(both, band_mask):
        key_heads = both[0].reshape(rows_dev, HEADS, HEAD_DIM)
        value_heads = both[1].reshape(rows_dev, HEADS, HEAD_DIM)
        scores = (
            jnp.einsum("qhd,khd->hqk", queries, key_heads, preferred_element_type=jnp.float32)
            * score_scale
        )
        weights = jax.nn.silu(scores)
        if band_mask is not None:
            weights = jnp.where(band_mask[None], weights, 0.0)
        weights = weights.astype(jnp.bfloat16)
        return jnp.einsum(
            "hqk,khd->qhd", weights, value_heads, preferred_element_type=jnp.float32
        ).reshape(rows_dev, model_width)

    outgoing = normed[None]
    attended = attend(own_pair, None)
    for distance in range(1, SPAN + 1):
        band_before = upper_band if distance == SPAN else None
        band_after = lower_band if distance == SPAN else None
        earlier = shifted(outgoing, ("seq", "emb"), distance)
        following = shifted(outgoing, ("seq", "emb"), -distance)
        attended = (
            attended + attend(unpack(earlier), band_before) + attend(unpack(following), band_after)
        )
    gated = (rms_norm(attended, norm_gains[1]) * gating).astype(jnp.bfloat16)
    hidden = embedded + jnp.dot(gated, proj_out, preferred_element_type=jnp.float32)
    routed = rms_norm(hidden, norm_gains[2]).astype(jnp.bfloat16)
    onehot_domain = (domains[:, None] == jnp.arange(group_size, dtype=jnp.int32)[None, :]).astype(
        jnp.int32
    )
    slot_rank = jnp.sum((jnp.cumsum(onehot_domain, axis=0) - onehot_domain) * onehot_domain, axis=1)
    slot_index = domains * capacity + slot_rank
    outgoing_rows = (
        jnp.zeros((group_size * capacity, model_width), jnp.bfloat16).at[slot_index].set(routed)
    )
    outgoing_rows = outgoing_rows.reshape(group_size, capacity, model_width)
    inbox = lax.all_to_all(outgoing_rows, "emb", split_axis=0, concat_axis=0, tiled=True)
    sources, slot_count, _ = inbox.shape
    flattened = inbox.reshape(sources * slot_count, model_width)
    gate_up = jnp.dot(flattened, expert_in[0], preferred_element_type=jnp.float32)
    activated = (jax.nn.silu(gate_up[:, :hidden_units]) * gate_up[:, hidden_units:]).astype(
        jnp.bfloat16
    )
    produced = jnp.dot(activated, expert_out[0], preferred_element_type=jnp.float32).astype(
        jnp.bfloat16
    )
    finished = produced.reshape(sources, slot_count, model_width)
    returned = lax.all_to_all(finished, "emb", split_axis=0, concat_axis=0, tiled=True).reshape(
        group_size * capacity, model_width
    )
    expert_rows = returned[slot_index].astype(jnp.float32)
    return (live_mask[:, None] * (hidden + expert_rows)).astype(jnp.bfloat16)


def solution(mesh):
    group = mesh.shape["emb"]
    split_heads = group == SPAN and HEADS == 2 * group

    def body(*arrays):
        return (by_heads if split_heads else by_rows)(*arrays)

    in_specs = (
        P("seq"),
        P(("seq", "emb")),
        P(("seq", "emb")),
        P(None, "emb"),
        P(),
        P(),
        P(),
        P("emb", None, None),
        P("emb", None, None),
    )
    out_specs = P(("seq", "emb"), None)
    return jax.shard_map(body, mesh=mesh, in_specs=in_specs, out_specs=out_specs, check_vma=False)
```

profile of v0, /device:TPU:2, one launch (start us, length us, event | category | flops | bytes accessed | tf_op | source)
XLA Modules:
  0.0 154.1 jit_solution(17682025559872520113)
XLA Ops:
  0.7 0.7 fusion.1
  1.4 7.3 %gather_fusion = bf16[1024,128]{1,0:T(8,128)(2,1)S(1)} fusion(bf16[32768,128]{1,0:T(8,128)(2,1)} %param.12, s32[1024]{0:T(1024)S(1)} %get-tuple-element.60), kind=kCustom, calls=%fused_computation | custom fusion | bytes 528384 | tf_op jit(solution)/shard_map/gather | solution.py:470
  8.8 0.2 pad_maximum_fusion.refs_0_
  9.0 1.6 %collective-permute-start = (bf16[1040,128]{1,0:T(8,128)(2,1)S(1)}, bf16[1040,128]{1,0:T(8,128)(2,1)S(1)}, u32[]{:S(2)}, u32[]{:S(2)}) collective-permute-start(bf16[1040,128]{1,0:T(8,128)(2,1)S(1)} %pad_maximum_fusion.refs_0_), channel_id=1, source_target_pairs={{0,1},{1,2},{2,3},{3,0},{4,5},{5,6},{6,7},{7,4},{8,9},{9,10},{10,1... | collective-permute-start | bytes 798728 | tf_op jit(solution)/shard_map/ppermute | solution.py:33
  10.6 2.2 %collective-permute-start.1 = (bf16[1040,128]{1,0:T(8,128)(2,1)S(1)}, bf16[1040,128]{1,0:T(8,128)(2,1)S(1)}, u32[]{:S(2)}, u32[]{:S(2)}) collective-permute-start(bf16[1040,128]{1,0:T(8,128)(2,1)S(1)} %pad_maximum_fusion.refs_0_), channel_id=1, source_target_pairs={{0,3},{1,0},{2,1},{3,2},{4,7},{5,4},{6,5},{7,6},{8,11},{9,8},{10,9... | collective-permute-start | bytes 798728 | tf_op jit(solution)/shard_map/ppermute | solution.py:33
  12.8 7.3 %gather_fusion.1 = bf16[1024,128]{1,0:T(8,128)(2,1)S(1)} fusion(bf16[32768,128]{1,0:T(8,128)(2,1)} %param.12, s32[1024]{0:T(1024)S(1)} %get-tuple-element.59), kind=kCustom, calls=%fused_computation.1 | custom fusion | bytes 528384 | tf_op jit(solution)/shard_map/gather | solution.py:471
  20.3 4.7 %collective-permute-start.8 = (bf16[512,128]{1,0:T(8,128)(2,1)S(1)}, bf16[512,128]{1,0:T(8,128)(2,1)S(1)}, u32[]{:S(2)}, u32[]{:S(2)}) collective-permute-start(bf16[512,128]{1,0:T(8,128)(2,1)S(1)} %get-tuple-element.57.refs_1_), channel_id=1, source_target_pairs={{0,1},{1,2},{2,3},{3,0},{4,5},{5,6},{6,7},{7,4},{8,9},{9,10},{10,1... | collective-permute-start | bytes 393224 | tf_op jit(solution)/shard_map/ppermute | solution.py:33
  25.0 0.8 collective-permute-start.9
  25.9 8.8 %collective-permute-done.8.refs_2_ = bf16[512,128]{1,0:T(8,128)(2,1)S(1)} collective-permute-done((bf16[512,128]{1,0:T(8,128)(2,1)S(1)}, bf16[512,128]{1,0:T(8,128)(2,1)S(1)}, u32[]{:S(2)}, u32[]{:S(2)}) %collective-permute-start.8) | collective-permute-done | bytes 131104 | tf_op jit(solution)/shard_map/ppermute | solution.py:33
  34.7 2.4 %collective-permute-start.4 = (bf16[512,128]{1,0:T(8,128)(2,1)S(1)}, bf16[512,128]{1,0:T(8,128)(2,1)S(1)}, u32[]{:S(2)}, u32[]{:S(2)}) collective-permute-start(bf16[512,128]{1,0:T(8,128)(2,1)S(1)} %get-tuple-element.34.refs_1_), channel_id=1, source_target_pairs={{0,1},{1,2},{2,3},{3,0},{4,5},{5,6},{6,7},{7,4},{8,9},{9,10},{10,1... | collective-permute-start | bytes 393224 | tf_op jit(solution)/shard_map/ppermute | solution.py:33
  37.1 1.6 %copy-done.1 = bf16[512,2048]{1,0:T(8,128)(2,1)S(1)} copy-done((bf16[512,2048]{1,0:T(8,128)(2,1)S(1)}, bf16[512,2048]{1,0:T(8,128)(2,1)}, u32[]{:S(2)}) %copy-start.1) | copy-done | bytes 2097176
  38.7 0.2 weights.1.refs_5_.refs_6_
  38.9 1.5 shard_map.91
  40.4 1.1 collective-permute-done.10.refs_4_
  41.5 1.2 shard_map.93
  42.8 1.9 %collective-permute-start.11 = (bf16[512,256]{1,0:T(8,128)(2,1)S(1)}, bf16[512,256]{1,0:T(8,128)(2,1)S(1)}, u32[]{:S(2)}, u32[]{:S(2)}) collective-permute-start(bf16[512,256]{1,0:T(8,128)(2,1)S(1)} %get-tuple-element.39.refs_5_), channel_id=1, source_target_pairs={{0,4},{4,8},{8,12},{12,16},{16,20},{20,24},{24,28},{1,5},{5,9},{9,... | collective-permute-start | bytes 786440 | tf_op jit(solution)/shard_map/ppermute | solution.py:28
  44.7 1.8 %collective-permute-start.5 = (bf16[512,128]{1,0:T(8,128)(2,1)S(1)}, bf16[512,128]{1,0:T(8,128)(2,1)S(1)}, u32[]{:S(2)}, u32[]{:S(2)}) collective-permute-start(bf16[512,128]{1,0:T(8,128)(2,1)S(1)} %get-tuple-element.34.refs_1_), channel_id=1, source_target_pairs={{0,3},{1,0},{2,1},{3,2},{4,7},{5,4},{6,5},{7,6},{8,11},{9,8},{10,9... | collective-permute-start | bytes 393224 | tf_op jit(solution)/shard_map/ppermute | solution.py:33
  46.5 0.3 collective-permute-start.6
  46.8 3.1 %collective-permute-start.14 = (bf16[512,256]{1,0:T(8,128)(2,1)S(1)}, bf16[512,256]{1,0:T(8,128)(2,1)S(1)}, u32[]{:S(2)}, u32[]{:S(2)}) collective-permute-start(bf16[512,256]{1,0:T(8,128)(2,1)S(1)} %get-tuple-element.39.refs_5_), channel_id=1, source_target_pairs={{4,0},{8,4},{12,8},{16,12},{20,16},{24,20},{28,24},{5,1},{9,5},{13... | collective-permute-start | bytes 786440 | tf_op jit(solution)/shard_map/ppermute | solution.py:28
  49.8 3.5 %own0.1.refs_6_ = f32[1024,128]{1,0:T(8,128)S(1)} custom-call(s32[4]{0:T(128)S(1)} %get-tuple-element.32.lives_ref.refs_0_, bf16[1024,256]{1,0:T(8,128)(2,1)S(1)} %get-tuple-element.33.refs_0_, bf16[1040,256]{1,0:T(8,128)(2,1)S(1)} %get-tuple-element.31.refs_1_.refs_3_), custom_call_target="tpu_custom_call" | custom-call | flops 2147483648 | bytes 1048576 | tf_op jit(solution)/shard_map/own0/pallas_call | solution.py:496
  53.3 1.0 collective-permute-done.6.refs_4_
  54.3 1.2 shard_map.92
  55.6 1.9 %collective-permute-start.13 = (bf16[512,256]{1,0:T(8,128)(2,1)S(1)}, bf16[512,256]{1,0:T(8,128)(2,1)S(1)}, u32[]{:S(2)}, u32[]{:S(2)}) collective-permute-start(bf16[512,256]{1,0:T(8,128)(2,1)S(1)} %get-tuple-element.38.refs_4_), channel_id=1, source_target_pairs={{4,0},{8,4},{12,8},{16,12},{20,16},{24,20},{28,24},{5,1},{9,5},{13... | collective-permute-start | bytes 786440 | tf_op jit(solution)/shard_map/ppermute | solution.py:28
  57.5 2.4 %collective-permute-start.7 = (bf16[512,256]{1,0:T(8,128)(2,1)S(1)}, bf16[512,256]{1,0:T(8,128)(2,1)S(1)}, u32[]{:S(2)}, u32[]{:S(2)}) collective-permute-start(bf16[512,256]{1,0:T(8,128)(2,1)S(1)} %get-tuple-element.38.refs_4_), channel_id=1, source_target_pairs={{0,4},{4,8},{8,12},{12,16},{16,20},{20,24},{24,28},{1,5},{5,9},{9,... | collective-permute-start | bytes 786440 | tf_op jit(solution)/shard_map/ppermute | solution.py:28
  59.9 3.2 %collective-permute-start.12 = (bf16[1040,256]{1,0:T(8,128)(2,1)S(1)}, bf16[1040,256]{1,0:T(8,128)(2,1)S(1)}, u32[]{:S(2)}, u32[]{:S(2)}) collective-permute-start(bf16[1040,256]{1,0:T(8,128)(2,1)S(1)} %get-tuple-element.31.refs_1_.refs_3_), channel_id=1, source_target_pairs={{4,0},{8,4},{12,8},{16,12},{20,16},{24,20},{28,24},{5,1},{9,5},{13... | collective-permute-start | bytes 1597448 | tf_op jit(solution)/shard_map/ppermute | solution.py:28
  63.1 3.0 %collective-permute-start.3 = (bf16[1040,256]{1,0:T(8,128)(2,1)S(1)}, bf16[1040,256]{1,0:T(8,128)(2,1)S(1)}, u32[]{:S(2)}, u32[]{:S(2)}) collective-permute-start(bf16[1040,256]{1,0:T(8,128)(2,1)S(1)} %get-tuple-element.31.refs_1_.refs_3_), channel_id=1, source_target_pairs={{0,4},{4,8},{8,12},{12,16},{16,20},{20,24},{24,28},{1,5},{5,9},{9,... | collective-permute-start | bytes 1597448 | tf_op jit(solution)/shard_map/ppermute | solution.py:28
  66.1 8.0 %own1.1 = (f32[2048,128]{1,0:T(8,128)S(1)}, bf16[2048,256]{1,0:T(8,128)(2,1)S(1)}) custom-call(s32[4]{0:T(128)S(1)} %get-tuple-element.32.lives_ref.refs_0_, bf16[1024,256]{1,0:T(8,128)(2,1)S(1)} %get-tuple-element.33.refs_0_, bf16[512,256]{1,0:T(8,128)(2,1)S(1)} %get-tuple-element.40.refs_1_, bf16[512,256]{1,0:T(8,128)(2,1)S(1)} %get-tuple-element.41.refs_2_, ...), custom_call_target="tpu_custom_call" | custom-call | flops 6442450944 | bytes 2097152 | tf_op jit(solution)/shard_map/own1/pallas_call | solution.py:497
  74.1 0.8 gate.1
  75.0 4.7 %shard_map.96 = bf16[512,128]{1,0:T(8,128)(2,1)S(1)} custom-call(s32[1]{0:T(128)} %bitcast.me.me_ref, bf16[1040,256]{1,0:T(8,128)(2,1)S(1)} %collective-permute-done.3.refs_0_, bf16[512,256]{1,0:T(8,128)(2,1)S(1)} %collective-permute-done.7.refs_1_, bf16[512,256]{1,0:T(8,128)(2,1)S(1)} %collective-permute-done.11.refs_2_, ...), custom_call_target="tpu_custom_call" | custom-call | flops 2684354560 | bytes 524288 | tf_op jit(solution)/shard_map/pallas_call | solution.py:506
  79.7 1.9 %collective-permute-start.17 = (bf16[512,128]{1,0:T(8,128)(2,1)S(1)}, bf16[512,128]{1,0:T(8,128)(2,1)S(1)}, u32[]{:S(2)}, u32[]{:S(2)}) collective-permute-start(bf16[512,128]{1,0:T(8,128)(2,1)S(1)} %shard_map.96), channel_id=1, source_target_pairs={{0,3},{1,0},{2,1},{3,2},{4,7},{5,4},{6,5},{7,6},{8,11},{9,8},{10,9... | collective-permute-start | bytes 393224 | tf_op jit(solution)/shard_map/ppermute | solution.py:33
  81.6 4.3 %shard_map.95 = bf16[512,128]{1,0:T(8,128)(2,1)S(1)} custom-call(s32[1]{0:T(128)} %bitcast.me.me_ref, bf16[1040,256]{1,0:T(8,128)(2,1)S(1)} %collective-permute-done.3.refs_0_, bf16[512,256]{1,0:T(8,128)(2,1)S(1)} %collective-permute-done.7.refs_1_, bf16[512,256]{1,0:T(8,128)(2,1)S(1)} %collective-permute-done.11.refs_2_, ...), custom_call_target="tpu_custom_call" | custom-call | flops 2684354560 | bytes 524288 | tf_op jit(solution)/shard_map/pallas_call | solution.py:506
  85.9 4.3 %shard_map.94 = bf16[512,128]{1,0:T(8,128)(2,1)S(1)} custom-call(s32[1]{0:T(128)} %bitcast.me.me_ref, bf16[1040,256]{1,0:T(8,128)(2,1)S(1)} %collective-permute-done.3.refs_0_, bf16[512,256]{1,0:T(8,128)(2,1)S(1)} %collective-permute-done.7.refs_1_, bf16[512,256]{1,0:T(8,128)(2,1)S(1)} %collective-permute-done.11.refs_2_, ...), custom_call_target="tpu_custom_call" | custom-call | flops 2684354560 | bytes 524288 | tf_op jit(solution)/shard_map/pallas_call | solution.py:506
  90.2 1.9 %collective-permute-start.15 = (bf16[512,128]{1,0:T(8,128)(2,1)S(1)}, bf16[512,128]{1,0:T(8,128)(2,1)S(1)}, u32[]{:S(2)}, u32[]{:S(2)}) collective-permute-start(bf16[512,128]{1,0:T(8,128)(2,1)S(1)} %shard_map.94), channel_id=1, source_target_pairs={{0,1},{1,2},{2,3},{3,0},{4,5},{5,6},{6,7},{7,4},{8,9},{9,10},{10,1... | collective-permute-start | bytes 393224 | tf_op jit(solution)/shard_map/ppermute | solution.py:33
  92.2 4.0 %shard_map.97.refs_3_ = bf16[512,128]{1,0:T(8,128)(2,1)S(1)} custom-call(s32[1]{0:T(128)} %bitcast.me.me_ref, bf16[1040,256]{1,0:T(8,128)(2,1)S(1)} %collective-permute-done.3.refs_0_, bf16[512,256]{1,0:T(8,128)(2,1)S(1)} %collective-permute-done.7.refs_1_, bf16[512,256]{1,0:T(8,128)(2,1)S(1)} %collective-permute-done.11.refs_2_, ...), custom_call_target="tpu_custom_call" | custom-call | flops 2684354560 | bytes 524288 | tf_op jit(solution)/shard_map/pallas_call | solution.py:506
  96.2 2.4 %collective-permute-done.16.refs_1_ = bf16[512,128]{1,0:T(8,128)(2,1)S(1)} collective-permute-done((bf16[512,128]{1,0:T(8,128)(2,1)S(1)}, bf16[512,128]{1,0:T(8,128)(2,1)S(1)}, u32[]{:S(2)}, u32[]{:S(2)}) %collective-permute-start.16) | collective-permute-done | bytes 131104 | tf_op jit(solution)/shard_map/ppermute | solution.py:33
  98.6 1.5 route.1
  100.1 0.2 collective-permute-start.18
  100.3 0.9 collective-permute-start.20
  101.2 2.8 %collective-permute-start.22 = (bf16[256,512]{1,0:T(8,128)(2,1)S(1)}, bf16[256,512]{1,0:T(8,128)(2,1)S(1)}, u32[]{:S(2)}, u32[]{:S(2)}) collective-permute-start(bf16[256,512]{1,0:T(8,128)(2,1)S(1)} %get-tuple-element.54), channel_id=1, source_target_pairs={{0,3},{1,0},{2,1},{3,2},{4,7},{5,4},{6,5},{7,6},{8,11},{9,8},{10,9... | collective-permute-start | bytes 786440 | tf_op jit(solution)/shard_map/ppermute | solution.py:33
  104.0 7.3 %collective-permute-done.18.x = bf16[256,512]{1,0:T(8,128)(2,1)S(1)} collective-permute-done((bf16[256,512]{1,0:T(8,128)(2,1)S(1)}, bf16[256,512]{1,0:T(8,128)(2,1)S(1)}, u32[]{:S(2)}, u32[]{:S(2)}) %collective-permute-start.18) | collective-permute-done | bytes 262176 | tf_op jit(solution)/shard_map/ppermute | solution.py:33
  111.3 2.1 %expert.5 = bf16[256,512]{1,0:T(8,128)(2,1)S(1)} custom-call(bf16[256,512]{1,0:T(8,128)(2,1)S(1)} %collective-permute-done.18.x, bf16[1,512,4096]{2,1,0:T(8,128)(2,1)S(1)} %copy-done, bf16[1,2048,512]{2,1,0:T(8,128)(2,1)S(1)} %copy-done.3), custom_call_target="tpu_custom_call" | custom-call | flops 1610612736 | bytes 524288 | tf_op jit(solution)/shard_map/expert/pallas_call | solution.py:518
  113.5 8.2 %collective-permute-done.20.x = bf16[256,512]{1,0:T(8,128)(2,1)S(1)} collective-permute-done((bf16[256,512]{1,0:T(8,128)(2,1)S(1)}, bf16[256,512]{1,0:T(8,128)(2,1)S(1)}, u32[]{:S(2)}, u32[]{:S(2)}) %collective-permute-start.20) | collective-permute-done | bytes 262176 | tf_op jit(solution)/shard_map/ppermute | solution.py:33
  121.7 2.1 %expert.6 = bf16[256,512]{1,0:T(8,128)(2,1)S(1)} custom-call(bf16[256,512]{1,0:T(8,128)(2,1)S(1)} %collective-permute-done.20.x, bf16[1,512,4096]{2,1,0:T(8,128)(2,1)S(1)} %copy-done, bf16[1,2048,512]{2,1,0:T(8,128)(2,1)S(1)} %copy-done.3), custom_call_target="tpu_custom_call" | custom-call | flops 1610612736 | bytes 524288 | tf_op jit(solution)/shard_map/expert/pallas_call | solution.py:518
  123.9 2.1 %expert.7 = bf16[256,512]{1,0:T(8,128)(2,1)S(1)} custom-call(bf16[256,512]{1,0:T(8,128)(2,1)S(1)} %collective-permute-done.22.x, bf16[1,512,4096]{2,1,0:T(8,128)(2,1)S(1)} %copy-done, bf16[1,2048,512]{2,1,0:T(8,128)(2,1)S(1)} %copy-done.3), custom_call_target="tpu_custom_call" | custom-call | flops 1610612736 | bytes 524288 | tf_op jit(solution)/shard_map/expert/pallas_call | solution.py:518
  126.1 17.5 %collective-permute-start.23 = (bf16[256,512]{1,0:T(8,128)(2,1)S(1)}, bf16[256,512]{1,0:T(8,128)(2,1)S(1)}, u32[]{:S(2)}, u32[]{:S(2)}) collective-permute-start(bf16[256,512]{1,0:T(8,128)(2,1)S(1)} %expert.7), channel_id=1, source_target_pairs={{0,1},{1,2},{2,3},{3,0},{4,5},{5,6},{6,7},{7,4},{8,9},{9,10},{10,1... | collective-permute-start | bytes 786440 | tf_op jit(solution)/shard_map/ppermute | solution.py:33
  143.5 2.2 %expert.4.refs_0_ = bf16[256,512]{1,0:T(8,128)(2,1)S(1)} custom-call(bf16[256,512]{1,0:T(8,128)(2,1)S(1)} %get-tuple-element.51.x, bf16[1,512,4096]{2,1,0:T(8,128)(2,1)S(1)} %copy-done, bf16[1,2048,512]{2,1,0:T(8,128)(2,1)S(1)} %copy-done.3), custom_call_target="tpu_custom_call" | custom-call | flops 1610612736 | bytes 524288 | tf_op jit(solution)/shard_map/expert/pallas_call | solution.py:518
  145.7 6.8 %collective-permute-done.23.refs_3_ = bf16[256,512]{1,0:T(8,128)(2,1)S(1)} collective-permute-done((bf16[256,512]{1,0:T(8,128)(2,1)S(1)}, bf16[256,512]{1,0:T(8,128)(2,1)S(1)}, u32[]{:S(2)}, u32[]{:S(2)}) %collective-permute-start.23) | collective-permute-done | bytes 262176 | tf_op jit(solution)/shard_map/ppermute | solution.py:33
  152.5 1.5 %mix.1 = bf16[512,512]{1,0:T(8,128)(2,1)} custom-call(s32[1]{0:T(128)} %copy.10.live_ref, bf16[256,512]{1,0:T(8,128)(2,1)S(1)} %expert.4.refs_0_, bf16[256,512]{1,0:T(8,128)(2,1)S(1)} %collective-permute-done.19.refs_1_, bf16[256,512]{1,0:T(8,128)(2,1)S(1)} %collective-permute-done.21.refs_2_, bf16[256,512]{1,0:T(8,128)(2,1)S(1)} %collective-permute-done.23.refs_3_, ...), custom_call_target="tpu_custom_call" | custom-call | flops 536870912 | bytes 2097152 | tf_op jit(solution)/shard_map/mix/pallas_call | solution.py:523
  (38 shorter events, 0.4 us)
Async XLA Ops:
  0.0 38.9 %copy-start.4 = (f32[3,512]{1,0:T(4,128)S(1)}, f32[3,512]{1,0:T(4,128)}, u32[]{:S(2)}) copy-start(f32[3,512]{1,0:T(4,128)} %refs_6_.1) | copy-start | bytes 18436
  9.0 11.2 %collective-permute-start = (bf16[1040,128]{1,0:T(8,128)(2,1)S(1)}, bf16[1040,128]{1,0:T(8,128)(2,1)S(1)}, u32[]{:S(2)}, u32[]{:S(2)}) collective-permute-start(bf16[1040,128]{1,0:T(8,128)(2,1)S(1)} %pad_maximum_fusion.refs_0_), channel_id=1, source_target_pairs={{0,1},{1,2},{2,3},{3,0},{4,5},{5,6},{6,7},{7,4},{8,9},{9,10},{10,1... | collective-permute-start | bytes 798728 | tf_op jit(solution)/shard_map/ppermute | solution.py:33
  10.6 28.3 %collective-permute-start.1 = (bf16[1040,128]{1,0:T(8,128)(2,1)S(1)}, bf16[1040,128]{1,0:T(8,128)(2,1)S(1)}, u32[]{:S(2)}, u32[]{:S(2)}) collective-permute-start(bf16[1040,128]{1,0:T(8,128)(2,1)S(1)} %pad_maximum_fusion.refs_0_), channel_id=1, source_target_pairs={{0,3},{1,0},{2,1},{3,2},{4,7},{5,4},{6,5},{7,6},{8,11},{9,8},{10,9... | collective-permute-start | bytes 798728 | tf_op jit(solution)/shard_map/ppermute | solution.py:33
  20.2 18.7 %collective-permute-start.2 = (bf16[1040,128]{1,0:T(8,128)(2,1)S(1)}, bf16[1040,128]{1,0:T(8,128)(2,1)S(1)}, u32[]{:S(2)}, u32[]{:S(2)}) collective-permute-start(bf16[1040,128]{1,0:T(8,128)(2,1)S(1)} %collective-permute-done.refs_1_), channel_id=1, source_target_pairs={{0,1},{1,2},{2,3},{3,0},{4,5},{5,6},{6,7},{7,4},{8,9},{9,10},{10,1... | collective-permute-start | bytes 798728 | tf_op jit(solution)/shard_map/ppermute | solution.py:33
  20.3 14.4 %collective-permute-start.8 = (bf16[512,128]{1,0:T(8,128)(2,1)S(1)}, bf16[512,128]{1,0:T(8,128)(2,1)S(1)}, u32[]{:S(2)}, u32[]{:S(2)}) collective-permute-start(bf16[512,128]{1,0:T(8,128)(2,1)S(1)} %get-tuple-element.57.refs_1_), channel_id=1, source_target_pairs={{0,1},{1,2},{2,3},{3,0},{4,5},{5,6},{6,7},{7,4},{8,9},{9,10},{10,1... | collective-permute-start | bytes 393224 | tf_op jit(solution)/shard_map/ppermute | solution.py:33
  25.0 15.4 %collective-permute-start.9 = (bf16[512,128]{1,0:T(8,128)(2,1)S(1)}, bf16[512,128]{1,0:T(8,128)(2,1)S(1)}, u32[]{:S(2)}, u32[]{:S(2)}) collective-permute-start(bf16[512,128]{1,0:T(8,128)(2,1)S(1)} %get-tuple-element.57.refs_1_), channel_id=1, source_target_pairs={{0,3},{1,0},{2,1},{3,2},{4,7},{5,4},{6,5},{7,6},{8,11},{9,8},{10,9... | collective-permute-start | bytes 393224 | tf_op jit(solution)/shard_map/ppermute | solution.py:33
  34.7 6.8 %collective-permute-start.10 = (bf16[512,128]{1,0:T(8,128)(2,1)S(1)}, bf16[512,128]{1,0:T(8,128)(2,1)S(1)}, u32[]{:S(2)}, u32[]{:S(2)}) collective-permute-start(bf16[512,128]{1,0:T(8,128)(2,1)S(1)} %collective-permute-done.8.refs_2_), channel_id=1, source_target_pairs={{0,1},{1,2},{2,3},{3,0},{4,5},{5,6},{6,7},{7,4},{8,9},{9,10},{10,1... | collective-permute-start | bytes 393224 | tf_op jit(solution)/shard_map/ppermute | solution.py:33
  34.7 11.7 %collective-permute-start.4 = (bf16[512,128]{1,0:T(8,128)(2,1)S(1)}, bf16[512,128]{1,0:T(8,128)(2,1)S(1)}, u32[]{:S(2)}, u32[]{:S(2)}) collective-permute-start(bf16[512,128]{1,0:T(8,128)(2,1)S(1)} %get-tuple-element.34.refs_1_), channel_id=1, source_target_pairs={{0,1},{1,2},{2,3},{3,0},{4,5},{5,6},{6,7},{7,4},{8,9},{9,10},{10,1... | collective-permute-start | bytes 393224 | tf_op jit(solution)/shard_map/ppermute | solution.py:33
  37.1 1.6 %copy-start.1 = (bf16[512,2048]{1,0:T(8,128)(2,1)S(1)}, bf16[512,2048]{1,0:T(8,128)(2,1)}, u32[]{:S(2)}) copy-start(bf16[512,2048]{1,0:T(8,128)(2,1)} %refs_4_.3) | copy-start | bytes 6291460
  42.8 20.3 %collective-permute-start.11 = (bf16[512,256]{1,0:T(8,128)(2,1)S(1)}, bf16[512,256]{1,0:T(8,128)(2,1)S(1)}, u32[]{:S(2)}, u32[]{:S(2)}) collective-permute-start(bf16[512,256]{1,0:T(8,128)(2,1)S(1)} %get-tuple-element.39.refs_5_), channel_id=1, source_target_pairs={{0,4},{4,8},{8,12},{12,16},{16,20},{20,24},{24,28},{1,5},{5,9},{9,... | collective-permute-start | bytes 786440 | tf_op jit(solution)/shard_map/ppermute | solution.py:28
  44.7 8.6 %collective-permute-start.5 = (bf16[512,128]{1,0:T(8,128)(2,1)S(1)}, bf16[512,128]{1,0:T(8,128)(2,1)S(1)}, u32[]{:S(2)}, u32[]{:S(2)}) collective-permute-start(bf16[512,128]{1,0:T(8,128)(2,1)S(1)} %get-tuple-element.34.refs_1_), channel_id=1, source_target_pairs={{0,3},{1,0},{2,1},{3,2},{4,7},{5,4},{6,5},{7,6},{8,11},{9,8},{10,9... | collective-permute-start | bytes 393224 | tf_op jit(solution)/shard_map/ppermute | solution.py:33
  46.5 7.8 %collective-permute-start.6 = (bf16[512,128]{1,0:T(8,128)(2,1)S(1)}, bf16[512,128]{1,0:T(8,128)(2,1)S(1)}, u32[]{:S(2)}, u32[]{:S(2)}) collective-permute-start(bf16[512,128]{1,0:T(8,128)(2,1)S(1)} %collective-permute-done.4.refs_2_), channel_id=1, source_target_pairs={{0,1},{1,2},{2,3},{3,0},{4,5},{5,6},{6,7},{7,4},{8,9},{9,10},{10,1... | collective-permute-start | bytes 393224 | tf_op jit(solution)/shard_map/ppermute | solution.py:33
  46.8 28.1 %collective-permute-start.14 = (bf16[512,256]{1,0:T(8,128)(2,1)S(1)}, bf16[512,256]{1,0:T(8,128)(2,1)S(1)}, u32[]{:S(2)}, u32[]{:S(2)}) collective-permute-start(bf16[512,256]{1,0:T(8,128)(2,1)S(1)} %get-tuple-element.39.refs_5_), channel_id=1, source_target_pairs={{4,0},{8,4},{12,8},{16,12},{20,16},{24,20},{28,24},{5,1},{9,5},{13... | collective-permute-start | bytes 786440 | tf_op jit(solution)/shard_map/ppermute | solution.py:28
  55.6 19.4 %collective-permute-start.13 = (bf16[512,256]{1,0:T(8,128)(2,1)S(1)}, bf16[512,256]{1,0:T(8,128)(2,1)S(1)}, u32[]{:S(2)}, u32[]{:S(2)}) collective-permute-start(bf16[512,256]{1,0:T(8,128)(2,1)S(1)} %get-tuple-element.38.refs_4_), channel_id=1, source_target_pairs={{4,0},{8,4},{12,8},{16,12},{20,16},{24,20},{28,24},{5,1},{9,5},{13... | collective-permute-start | bytes 786440 | tf_op jit(solution)/shard_map/ppermute | solution.py:28
  57.5 17.4 %collective-permute-start.7 = (bf16[512,256]{1,0:T(8,128)(2,1)S(1)}, bf16[512,256]{1,0:T(8,128)(2,1)S(1)}, u32[]{:S(2)}, u32[]{:S(2)}) collective-permute-start(bf16[512,256]{1,0:T(8,128)(2,1)S(1)} %get-tuple-element.38.refs_4_), channel_id=1, source_target_pairs={{0,4},{4,8},{8,12},{12,16},{16,20},{20,24},{24,28},{1,5},{5,9},{9,... | collective-permute-start | bytes 786440 | tf_op jit(solution)/shard_map/ppermute | solution.py:28
  59.9 15.0 %collective-permute-start.12 = (bf16[1040,256]{1,0:T(8,128)(2,1)S(1)}, bf16[1040,256]{1,0:T(8,128)(2,1)S(1)}, u32[]{:S(2)}, u32[]{:S(2)}) collective-permute-start(bf16[1040,256]{1,0:T(8,128)(2,1)S(1)} %get-tuple-element.31.refs_1_.refs_3_), channel_id=1, source_target_pairs={{4,0},{8,4},{12,8},{16,12},{20,16},{24,20},{28,24},{5,1},{9,5},{13... | collective-permute-start | bytes 1597448 | tf_op jit(solution)/shard_map/ppermute | solution.py:28
  63.1 11.9 %collective-permute-start.3 = (bf16[1040,256]{1,0:T(8,128)(2,1)S(1)}, bf16[1040,256]{1,0:T(8,128)(2,1)S(1)}, u32[]{:S(2)}, u32[]{:S(2)}) collective-permute-start(bf16[1040,256]{1,0:T(8,128)(2,1)S(1)} %get-tuple-element.31.refs_1_.refs_3_), channel_id=1, source_target_pairs={{0,4},{4,8},{8,12},{12,16},{16,20},{20,24},{24,28},{1,5},{5,9},{9,... | collective-permute-start | bytes 1597448 | tf_op jit(solution)/shard_map/ppermute | solution.py:28
  66.1 8.1 %copy-start.2 = (bf16[512,2048]{1,0:T(8,128)(2,1)S(1)}, bf16[512,2048]{1,0:T(8,128)(2,1)}, u32[]{:S(2)}) copy-start(bf16[512,2048]{1,0:T(8,128)(2,1)} %refs_4_.3) | copy-start | bytes 6291460
  66.1 8.0 %copy-start.5 = (s32[512]{0:T(512)S(1)}, s32[512]{0:T(512)}, u32[]{:S(2)}) copy-start(s32[512]{0:T(512)} %param.10) | copy-start | bytes 6148
  79.7 16.5 %collective-permute-start.17 = (bf16[512,128]{1,0:T(8,128)(2,1)S(1)}, bf16[512,128]{1,0:T(8,128)(2,1)S(1)}, u32[]{:S(2)}, u32[]{:S(2)}) collective-permute-start(bf16[512,128]{1,0:T(8,128)(2,1)S(1)} %shard_map.96), channel_id=1, source_target_pairs={{0,3},{1,0},{2,1},{3,2},{4,7},{5,4},{6,5},{7,6},{8,11},{9,8},{10,9... | collective-permute-start | bytes 393224 | tf_op jit(solution)/shard_map/ppermute | solution.py:33
  85.8 12.8 %copy-start.6 = (bf16[512,512]{1,0:T(8,128)(2,1)S(1)}, bf16[512,512]{1,0:T(8,128)(2,1)}, u32[]{:S(2)}) copy-start(bf16[512,512]{1,0:T(8,128)(2,1)} %refs_7_.1) | copy-start | bytes 1572868
  85.9 12.8 %collective-permute-start.16 = (bf16[512,128]{1,0:T(8,128)(2,1)S(1)}, bf16[512,128]{1,0:T(8,128)(2,1)S(1)}, u32[]{:S(2)}, u32[]{:S(2)}) collective-permute-start(bf16[512,128]{1,0:T(8,128)(2,1)S(1)} %shard_map.95), channel_id=1, source_target_pairs={{0,2},{1,3},{2,0},{3,1},{4,6},{5,7},{6,4},{7,5},{8,10},{9,11},{10,... | collective-permute-start | bytes 393224 | tf_op jit(solution)/shard_map/ppermute | solution.py:33
  90.2 21.1 %copy-start = (bf16[1,512,4096]{2,1,0:T(8,128)(2,1)S(1)}, bf16[1,512,4096]{2,1,0:T(8,128)(2,1)}, u32[]{:S(2)}) copy-start(bf16[1,512,4096]{2,1,0:T(8,128)(2,1)} %w_in.7) | copy-start | bytes 12582916
  90.2 21.1 %copy-start.3 = (bf16[1,2048,512]{2,1,0:T(8,128)(2,1)S(1)}, bf16[1,2048,512]{2,1,0:T(8,128)(2,1)}, u32[]{:S(2)}) copy-start(bf16[1,2048,512]{2,1,0:T(8,128)(2,1)} %w_out.7) | copy-start | bytes 6291460
  90.2 8.4 %collective-permute-start.15 = (bf16[512,128]{1,0:T(8,128)(2,1)S(1)}, bf16[512,128]{1,0:T(8,128)(2,1)S(1)}, u32[]{:S(2)}, u32[]{:S(2)}) collective-permute-start(bf16[512,128]{1,0:T(8,128)(2,1)S(1)} %shard_map.94), channel_id=1, source_target_pairs={{0,1},{1,2},{2,3},{3,0},{4,5},{5,6},{6,7},{7,4},{8,9},{9,10},{10,1... | collective-permute-start | bytes 393224 | tf_op jit(solution)/shard_map/ppermute | solution.py:33
  100.1 11.2 %collective-permute-start.18 = (bf16[256,512]{1,0:T(8,128)(2,1)S(1)}, bf16[256,512]{1,0:T(8,128)(2,1)S(1)}, u32[]{:S(2)}, u32[]{:S(2)}) collective-permute-start(bf16[256,512]{1,0:T(8,128)(2,1)S(1)} %get-tuple-element.52), channel_id=1, source_target_pairs={{0,1},{1,2},{2,3},{3,0},{4,5},{5,6},{6,7},{7,4},{8,9},{9,10},{10,1... | collective-permute-start | bytes 786440 | tf_op jit(solution)/shard_map/ppermute | solution.py:33
  100.3 21.4 %collective-permute-start.20 = (bf16[256,512]{1,0:T(8,128)(2,1)S(1)}, bf16[256,512]{1,0:T(8,128)(2,1)S(1)}, u32[]{:S(2)}, u32[]{:S(2)}) collective-permute-start(bf16[256,512]{1,0:T(8,128)(2,1)S(1)} %get-tuple-element.53), channel_id=1, source_target_pairs={{0,2},{1,3},{2,0},{3,1},{4,6},{5,7},{6,4},{7,5},{8,10},{9,11},{10,... | collective-permute-start | bytes 786440 | tf_op jit(solution)/shard_map/ppermute | solution.py:33
  101.2 22.7 %collective-permute-start.22 = (bf16[256,512]{1,0:T(8,128)(2,1)S(1)}, bf16[256,512]{1,0:T(8,128)(2,1)S(1)}, u32[]{:S(2)}, u32[]{:S(2)}) collective-permute-start(bf16[256,512]{1,0:T(8,128)(2,1)S(1)} %get-tuple-element.54), channel_id=1, source_target_pairs={{0,3},{1,0},{2,1},{3,2},{4,7},{5,4},{6,5},{7,6},{8,11},{9,8},{10,9... | collective-permute-start | bytes 786440 | tf_op jit(solution)/shard_map/ppermute | solution.py:33
  113.5 32.3 %collective-permute-start.19 = (bf16[256,512]{1,0:T(8,128)(2,1)S(1)}, bf16[256,512]{1,0:T(8,128)(2,1)S(1)}, u32[]{:S(2)}, u32[]{:S(2)}) collective-permute-start(bf16[256,512]{1,0:T(8,128)(2,1)S(1)} %expert.5), channel_id=1, source_target_pairs={{0,3},{1,0},{2,1},{3,2},{4,7},{5,4},{6,5},{7,6},{8,11},{9,8},{10,9... | collective-permute-start | bytes 786440 | tf_op jit(solution)/shard_map/ppermute | solution.py:33
  123.8 21.9 %collective-permute-start.21 = (bf16[256,512]{1,0:T(8,128)(2,1)S(1)}, bf16[256,512]{1,0:T(8,128)(2,1)S(1)}, u32[]{:S(2)}, u32[]{:S(2)}) collective-permute-start(bf16[256,512]{1,0:T(8,128)(2,1)S(1)} %expert.6), channel_id=1, source_target_pairs={{0,2},{1,3},{2,0},{3,1},{4,6},{5,7},{6,4},{7,5},{8,10},{9,11},{10,... | collective-permute-start | bytes 786440 | tf_op jit(solution)/shard_map/ppermute | solution.py:33
  126.1 26.5 %collective-permute-start.23 = (bf16[256,512]{1,0:T(8,128)(2,1)S(1)}, bf16[256,512]{1,0:T(8,128)(2,1)S(1)}, u32[]{:S(2)}, u32[]{:S(2)}) collective-permute-start(bf16[256,512]{1,0:T(8,128)(2,1)S(1)} %expert.7), channel_id=1, source_target_pairs={{0,1},{1,2},{2,3},{3,0},{4,5},{5,6},{6,7},{7,4},{8,9},{9,10},{10,1... | collective-permute-start | bytes 786440 | tf_op jit(solution)/shard_map/ppermute | solution.py:33
where the time goes:
time: 155 us; the launch traced here: 154 us
  starting transfers between devices  54.8 us (35%)
  Pallas kernels  45.3 us (29%)
  waiting for transfers between devices  35.6 us (23%)
  local copies, waits for them, and re-layouts  16.3 us (11%)
    ppermute x18, starting transfers between devices, rotated(): lax.ppermute(value, axis, [(source, (source + steps) % count) for source...  39.4 us
    ppermute x18, waiting for transfers between devices, rotated(): lax.ppermute(value, axis, [(source, (source + steps) % count) for source...  35.6 us
    pallas_call x4, Pallas kernels, by_heads(): heads = turn(me, *before, *after, q_all, acc)  17.3 us
    ppermute x6, starting transfers between devices, shifted(): lax.ppermute(value, axis, [(source, source + steps) for source in range(f...  15.4 us
    pallas_call x4, Pallas kernels, by_heads(): made = expert(arrived[k], expert_in, expert_out)  8.59 us
    pallas_call x1, Pallas kernels, by_heads(): make_own(chunks, False, rows, width)(lives, *queries, *own, acc)  8.02 us
    gather x1, local copies, waits for them, and re-layouts, by_heads(): opening = jnp.concatenate((table[item_ids[:cut]], code))  7.34 us
    gather x1, local copies, waits for them, and re-layouts, by_heads(): rest = table[item_ids[cut:]]  7.34 us
  transfers between devices with their start and end apart: 24, of which 7 were waited for; matrix products, arithmetic and copies ran while one was open for 5% of the time, Pallas kernels for 24%

commit v1 on v0

--- a/solution.py
+++ b/solution.py
@@ -1,3 +1,4 @@
+import functools
 import math
 
 import jax
@@ -12,7 +13,7 @@
 HEAD_DIM = 64
 SPAN = 4
 NORM_EPS = 1e-06
-CHUNKS = (0.5, 0.25, 0.25)
+CHUNKS = (0.25, 0.25, 0.5)
 KEY_TILE = 256
 TAIL = 16
 MIB = 1 << 20
@@ -95,9 +96,8 @@
         known = None if opening else take(1)[0]
         pieces = take(group)
         gains, weights = take(2)
-        q_ref, kv_ref, own_ref = take(3)
+        q_ref, kv_ref, emb_ref = take(3)
         lives_ref = take(1)[0] if opening else None
-        emb_ref = take(1)[0]
         me = me_ref[0]
         offsets = (0, group - 1, 1, 2)
         for piece, offset in zip(pieces, offsets):
@@ -105,7 +105,7 @@
             emb_ref[:, pl.ds(pl.multiple_of(column * lane, lane), lane)] = piece[pl.ds(0, rows), :]
             if opening:
                 code = piece[rows : rows + TAIL, :].astype(F32)
-                high, low = jnp.max(code[: TAIL // 2]), jnp.max(code[TAIL // 2 :])
+                high, low = (jnp.max(code[at : at + 1]) for at in (TAIL - 2, TAIL - 1))
                 lives_ref[column] = (high * TAIL + low).astype(I32)
         lives = [(lives_ref if opening else known)[b] for b in range(group)]
         for part in range(per):
@@ -126,14 +126,12 @@
                 code = jnp.where(row == b, high.astype(F32), code)
                 code = jnp.where(row == group + b, (lives[b] - high * TAIL).astype(F32), code)
             kv_ref[pl.ds(rows, TAIL), :] = code.astype(BF16)
-        at = jnp.clip(me - first, 0, per - 1) * block_rows
-        own_ref[...] = emb_ref[pl.ds(pl.multiple_of(at, block_rows), block_rows), :]
 
     more = TAIL if opening else 0
     out_shape = (
         jax.ShapeDtypeStruct((rows, 2 * width), BF16),
         jax.ShapeDtypeStruct((rows + more, 2 * width), BF16),
-        jax.ShapeDtypeStruct((block_rows, model_width), BF16),
+        jax.ShapeDtypeStruct((rows, model_width), BF16),
     )
     out_specs = (VMEM_SPEC,) * 3
     if opening:
@@ -144,7 +142,6 @@
         out_shape=out_shape,
         in_specs=[SMEM_SPEC] * (1 if opening else 2) + [VMEM_SPEC] * (group + 2),
         out_specs=out_specs,
-        scratch_shapes=[pltpu.VMEM((rows, model_width), BF16)],
         compiler_params=limit(16),
         cost_estimate=cost(2 * rows * model_width * 4 * width, 4 * rows * model_width),
     )
@@ -205,36 +202,32 @@
 
 
 def make_own(chunks, opening, block_rows, width):
-    count = 1 if opening else len(chunks)
     group = chunks[-1][1]
-    first_end = chunks[0][1]
-    total = (first_end if opening else group) * block_rows
+    first_end = chunks[-1][0]
+    parts = chunks[:-1] if opening else [(0, first_end), chunks[-1]]
+    blocks = first_end if opening else group
+    done = 0 if opening else first_end * block_rows
+    total = blocks * block_rows
 
     def kernel(lives_ref, *refs):
         refs = list(refs)
         take = lambda number: [refs.pop(0) for _ in range(number)]
-        queries = take(count)
-        keys = take(count)
-        if opening:
-            (acc,) = take(1)
-            acc[...] = jnp.zeros_like(acc)
-        else:
-            (old,) = take(1)
-            acc, q_all = take(2)
-            done = first_end * block_rows
+        queries = take(len(parts))
+        keys = take(len(chunks) - 1 if opening else len(chunks))
+        old = None if opening else take(1)[0]
+        acc, q_all = take(2)
+        if not opening:
             acc[pl.ds(0, done), :] = old[...]
-            acc[pl.ds(done, total - done), :] = jnp.zeros((total - done, width), F32)
-            for (low, high), ref in zip(chunks, queries):
-                q_all[pl.ds(low * block_rows, (high - low) * block_rows), :] = ref[...]
-        for k in range(first_end if opening else group):
+        acc[pl.ds(done, total - done), :] = jnp.zeros((total - done, width), F32)
+        for (low, high), ref in zip(parts, queries):
+            q_all[pl.ds(low * block_rows, (high - low) * block_rows), :] = ref[...]
+        for k in range(blocks):
             home = next(spans(k, k + 1, chunks))[0]
             start = 0 if opening or k >= first_end else first_end
-            end = first_end if opening else group
-            held = queries[0] if opening else q_all
-            while start < end:
-                past = min(start + 2, end)
+            while start < blocks:
+                past = min(start + 2, blocks)
                 pair(
-                    held,
+                    q_all,
                     start * block_rows,
                     start * block_rows,
                     keys[home],
@@ -249,46 +242,93 @@
                 )
                 start = past
 
-    out = (jax.ShapeDtypeStruct((total, width), F32),)
-    if not opening:
-        out += (jax.ShapeDtypeStruct((total, 2 * width), BF16),)
+    inputs = len(parts) + (len(chunks) - 1 if opening else len(chunks) + 1)
     pairs = first_end**2 if opening else group**2 - first_end**2
     return pl.pallas_call(
         kernel,
-        out_shape=out,
-        in_specs=[SMEM_SPEC] + [VMEM_SPEC] * (2 * count + (0 if opening else 1)),
-        out_specs=(VMEM_SPEC,) * len(out),
+        out_shape=(
+            jax.ShapeDtypeStruct((total, width), F32),
+            jax.ShapeDtypeStruct((total, 2 * width), BF16),
+        ),
+        in_specs=[SMEM_SPEC] + [VMEM_SPEC] * inputs,
+        out_specs=(VMEM_SPEC,) * 2,
         compiler_params=limit(24),
         cost_estimate=cost(pairs * block_rows**2 * 2048, total * width * 8),
         name="own0" if opening else "own1",
     )
 
 
-def make_turn(turn, chunks, block_rows, width):
+def make_near(c, chunks, block_rows, width):
+    first, past = chunks[c]
+    known = chunks[-1][0]
+    head_rows = chunks[0][1] * block_rows
+
+    def kernel(*refs):
+        before, after = refs[:2]
+        heads = refs[2:-3] or (before, after)
+        queries, old, acc = refs[-3:]
+        acc[...] = old[...]
+        lives_before = read_lives(heads[0], head_rows, chunks[-1][1])
+        lives_after = read_lives(heads[1], head_rows, chunks[-1][1])
+        for k in range(first, past):
+            jobs = [(before, 0, k, None), (before, k, k + 1, from_before)]
+            jobs += [(after, k, k + 1, from_after), (after, k + 1, known, None)]
+            for held, low, high, keep in jobs:
+                if low == high:
+                    continue
+                pair(
+                    queries,
+                    low * block_rows,
+                    low * block_rows,
+                    held,
+                    (k - first) * block_rows,
+                    k * block_rows,
+                    acc,
+                    low * block_rows,
+                    (high - low) * block_rows,
+                    keep,
+                    (lives_before if held is before else lives_after)[k],
+                    width,
+                )
+
+    operands = 4 if c == 0 else 6
+    return pl.pallas_call(
+        kernel,
+        out_shape=jax.ShapeDtypeStruct((known * block_rows, width), F32),
+        in_specs=[VMEM_SPEC] * operands,
+        out_specs=VMEM_SPEC,
+        input_output_aliases={operands - 1: 0},
+        compiler_params=limit(20),
+        cost_estimate=cost(3 * block_rows**2 * 2048, known * block_rows * width * 8),
+    )
+
+
+def make_last(batch, chunks, block_rows, width, capacity):
     count = len(chunks)
-    blocks = chunks[-1][1]
+    first, blocks = chunks[-1]
     head_rows = chunks[0][1] * block_rows
-
-    def kernel(me_ref, *refs):
-        before, after = refs[:count], refs[count : 2 * count]
-        queries, old, out, acc = refs[2 * count :]
-        q = lax.rem(me_ref[0] + 1 + turn, blocks)
-        at = pl.multiple_of(q * block_rows, block_rows)
-        lives_before = read_lives(before[0], head_rows, blocks)
+    size = len(batch) * capacity
+
+    def kernel(*refs):
+        after = refs[:count]
+        before, first_before = refs[count : count + 2]
+        queries, old, slots = refs[count + 2 : count + 5]
+        out = refs[count + 5 : -1]
+        acc = refs[-1]
+        lives_before = read_lives(first_before, head_rows, blocks)
         lives_after = read_lives(after[0], head_rows, blocks)
-        acc[...] = old[pl.ds(at, block_rows), :]
-        for k in range(blocks):
-            home = next(spans(k, k + 1, chunks))[0]
-            for held, keep, live in (
-                (before, from_before, jnp.where(q <= k, lives_before[k], 0)),
-                (after, from_after, jnp.where(q >= k, lives_after[k], 0)),
-            ):
+        for order, q in enumerate(batch):
+            at = q * block_rows
+            acc[...] = old[pl.ds(at, block_rows), :]
+
+            def run(held, k, keep, live):
+                start = chunks[next(spans(k, k + 1, chunks))[0]][0]
                 pair(
                     queries,
                     at,
                     at,
-                    held[home],
-                    (k - chunks[home][0]) * block_rows,
+                    held,
+                    (k - start) * block_rows,
                     k * block_rows,
                     acc,
                     0,
@@ -297,157 +337,203 @@
                     live,
                     width,
                 )
-        out[...] = acc[...].astype(BF16)
+
+            for k in range(blocks):
+                home = next(spans(k, k + 1, chunks))[0]
+                if k >= first and q <= k:
+                    run(before, k, from_before if q == k else None, lives_before[k])
+                if q >= first and q >= k:
+                    run(after[home], k, from_after if q == k else None, lives_after[k])
+            attended = acc[...].astype(BF16)
+            for turn in range(blocks):
+                place = lax.broadcasted_iota(I32, (capacity, block_rows), 0) + turn * capacity
+                pick = jnp.where(place == slots[q : q + 1, :], 1.0, 0.0).astype(BF16)
+                out[turn][pl.ds(order * capacity, capacity), :] = jnp.dot(
+                    pick, attended, preferred_element_type=F32
+                ).astype(BF16)
 
     return pl.pallas_call(
         kernel,
-        out_shape=jax.ShapeDtypeStruct((block_rows, width), BF16),
-        in_specs=[SMEM_SPEC] + [VMEM_SPEC] * (2 * count + 2),
-        out_specs=VMEM_SPEC,
+        out_shape=(jax.ShapeDtypeStruct((size, width), BF16),) * blocks,
+        in_specs=[VMEM_SPEC] * (count + 5),
+        out_specs=(VMEM_SPEC,) * blocks,
         scratch_shapes=[pltpu.VMEM((block_rows, width), F32)],
         compiler_params=limit(20),
-        cost_estimate=cost(5 * block_rows**2 * 2048, block_rows * width * 8),
-    )
-
-
-def make_gate(group, chunks, rows, model_width, capacity):
-    count = len(chunks)
-
-    def kernel(me_ref, live_ref, *refs):
-        candidates = refs[:count]
-        gains, weights, domains, gating, emb_ref, slot_row, slot_col = refs[count:]
-        me, live = me_ref[0], live_ref[0]
-        for c in range(count):
-
-            @pl.when((me >= chunks[c][0]) & (me < chunks[c][1]))
-            def _():
-                emb_ref[...] = candidates[c][...]
-
-        position = lax.broadcasted_iota(I32, (rows, 1), 0)
-        mask = (position < live).astype(F32)
-        normed = (rms_norm(emb_ref[...].astype(F32), gains[0:1, :]) * mask).astype(BF16)
+        cost_estimate=cost(7 * block_rows**2 * 2048, block_rows * width * 16),
+    )
+
+
+def make_slots(group, block_rows, capacity):
+    lanes = 128
+    strips = block_rows // lanes
+
+    def kernel(me_ref, lives_ref, *refs):
+        pieces = refs[:group]
+        slots, slot_col = refs[group:]
+        me = me_ref[0]
+        earlier = lax.broadcasted_iota(I32, (block_rows, block_rows), 0) < lax.broadcasted_iota(
+            I32, (block_rows, block_rows), 1
+        )
+        earlier = jnp.where(earlier, 1.0, 0.0).astype(BF16)
+        position = lax.broadcasted_iota(I32, (1, block_rows), 1)
+        expert = lax.broadcasted_iota(I32, (8, block_rows), 0)
+        for piece, offset in zip(pieces, (0, group - 1, 1, 2)):
+            block = lax.rem(me + offset, group)
+            code = piece[pl.ds(block_rows, TAIL), :].astype(F32)
+            domain = jnp.concatenate([code[r : r + 1, :] for r in range(strips)], axis=1)
+            turn = domain.astype(I32) - me
+            turn = jnp.where(turn < 0, turn + group, turn)
+            alive = position < lives_ref[block]
+            onehot = jnp.where((expert == turn) & alive, 1.0, 0.0)
+            rank = jnp.dot(onehot.astype(BF16), earlier, preferred_element_type=F32)
+            slot = jnp.sum(
+                onehot * (rank + (expert * capacity).astype(F32)), axis=0, keepdims=True
+            )
+            slot = jnp.where(alive, slot, -1.0)
+            slots[pl.ds(block, 1), :] = slot.astype(I32)
+            if offset == 0:
+                slot_col[...] = jnp.transpose(jnp.broadcast_to(slot, (lanes, block_rows))).astype(
+                    I32
+                )
+
+    return pl.pallas_call(
+        kernel,
+        out_shape=(
+            jax.ShapeDtypeStruct((8, block_rows), I32),
+            jax.ShapeDtypeStruct((block_rows, lanes), I32),
+        ),
+        in_specs=[SMEM_SPEC] * 2 + [VMEM_SPEC] * group,
+        out_specs=(VMEM_SPEC,) * 2,
+        compiler_params=limit(12),
+        cost_estimate=cost(2 * 32 * block_rows**2, 8 * block_rows * lanes),
+        name="slots",
+    )
+
+
+def make_select(batch, chunks, block_rows, model_width, capacity):
+    homes = [next(spans(b, b + 1, chunks))[0] for b in batch]
+    size = len(batch) * capacity
+
+    def kernel(*refs):
+        sources = refs[: len(batch)]
+        slots, gains, weights, emb, gating = refs[len(batch) :]
+        for order, (b, home, source) in enumerate(zip(batch, homes, sources)):
+            place = lax.broadcasted_iota(I32, (capacity, block_rows), 0)
+            pick = jnp.where(place == slots[b : b + 1, :], 1.0, 0.0).astype(BF16)
+            rows = source[pl.ds((b - chunks[home][0]) * block_rows, block_rows), :]
+            emb[pl.ds(order * capacity, capacity), :] = jnp.dot(
+                pick, rows, preferred_element_type=F32
+            ).astype(BF16)
+        normed = rms_norm(emb[...].astype(F32), gains[0:1, :]).astype(BF16)
         gate = jnp.dot(normed, weights[...], preferred_element_type=F32)
         gating[...] = half_silu(gate * 0.5)
-        turn = lax.rem(domains[...] - me + group, group)
-        alive = lax.broadcasted_iota(I32, (1, rows), 1) < live
-        expert = lax.broadcasted_iota(I32, (8, rows), 0)
-        onehot = jnp.where((expert == turn) & alive, 1.0, 0.0)
-        earlier = lax.broadcasted_iota(I32, (rows, rows), 0) < lax.broadcasted_iota(
-            I32, (rows, rows), 1
-        )
-        rank = jnp.dot(
-            onehot.astype(BF16),
-            jnp.where(earlier, 1.0, 0.0).astype(BF16),
-            preferred_element_type=F32,
-        )
-        slot = jnp.sum(onehot * (rank + (expert * capacity).astype(F32)), axis=0, keepdims=True)
-        slot = jnp.where(alive, slot, -1.0)
-        slot_row[...] = slot.astype(I32)
-        slot_col[...] = jnp.transpose(jnp.broadcast_to(slot, (128, rows))).astype(I32)
-
-    return pl.pallas_call(
+
+    return homes, pl.pallas_call(
         kernel,
         grid=(1,),
         out_shape=(
-            jax.ShapeDtypeStruct((rows, model_width), F32),
-            jax.ShapeDtypeStruct((rows, model_width), BF16),
-            jax.ShapeDtypeStruct((1, rows), I32),
-            jax.ShapeDtypeStruct((rows, 128), I32),
+            jax.ShapeDtypeStruct((size, model_width), BF16),
+            jax.ShapeDtypeStruct((size, model_width), F32),
         ),
-        in_specs=[SMEM_SPEC] * 2
-        + [VMEM_SPEC] * (count + 1)
-        + [pl.BlockSpec((model_width, model_width), lambda i: (0, 0)), VMEM_SPEC],
-        out_specs=(VMEM_SPEC,) * 4,
+        in_specs=[VMEM_SPEC] * (len(batch) + 2)
+        + [pl.BlockSpec((model_width, model_width), lambda i: (0, 0))],
+        out_specs=(VMEM_SPEC,) * 2,
         compiler_params=limit(12),
-        cost_estimate=cost(2 * rows * model_width**2, 8 * rows * model_width),
-        name="gate",
-    )
-
-
-def make_route(group, rows, width, model_width, capacity):
+        cost_estimate=cost(4 * size * model_width**2, 8 * size * model_width),
+    )
+
+
+def make_serve(batch, senders, group, width, model_width, hidden_units, capacity):
+    size = len(batch) * capacity
+    tile = hidden_units // 4
+
     def kernel(me_ref, *refs):
         pieces = refs[:group]
-        gating, emb, gains, proj_out, slot = refs[group : group + 5]
-        hidden_ref = refs[group + 5]
-        sent = refs[group + 6 : group + 6 + group]
-        att = refs[group + 6 + group]
+        emb, gating, gains, proj_out, w_in, w_out = refs[group : group + 6]
+        out = refs[group + 6 : -2]
+        att, done = refs[-2:]
         me = me_ref[0]
-        for turn, piece in enumerate(pieces):
-            column = lax.rem(me + group - 1 - turn, group)
+        for k, piece in enumerate(pieces):
+            column = lax.rem(me + group - k, group)
             att[:, pl.ds(pl.multiple_of(column * width, width), width)] = piece[...].astype(F32)
         gated = (rms_norm(att[...], gains[1:2, :]) * gating[...]).astype(BF16)
         hidden = emb[...].astype(F32) + jnp.dot(
             gated, proj_out[...], preferred_element_type=F32
         )
-        hidden_ref[...] = hidden
         routed = rms_norm(hidden, gains[2:3, :]).astype(BF16)
-        for turn in range(group):
-            place = lax.broadcasted_iota(I32, (capacity, rows), 0) + turn * capacity
-            pick = jnp.where(place == slot[...], 1.0, 0.0).astype(BF16)
-            sent[turn][...] = jnp.dot(pick, routed, preferred_element_type=F32).astype(BF16)
-
-    return pl.pallas_call(
-        kernel,
-        out_shape=(jax.ShapeDtypeStruct((rows, model_width), F32),)
-        + (jax.ShapeDtypeStruct((capacity, model_width), BF16),) * group,
-        in_specs=[SMEM_SPEC] + [VMEM_SPEC] * (group + 5),
-        out_specs=(VMEM_SPEC,) * (group + 1),
-        scratch_shapes=[pltpu.VMEM((rows, model_width), F32)],
-        compiler_params=limit(16),
-        cost_estimate=cost(6 * rows * model_width**2, 8 * rows * model_width),
-        name="route",
-    )
-
-
-def make_expert(rows, model_width, hidden):
-    tile = hidden // 4
-
-    def kernel(x, w_in, w_out, out):
         total = None
-        for at in range(0, hidden, tile):
-            gate = jnp.dot(x[...], w_in[0, :, at : at + tile], preferred_element_type=F32)
+        for at in range(0, hidden_units, tile):
+            gate = jnp.dot(routed, w_in[0, :, at : at + tile], preferred_element_type=F32)
             up = jnp.dot(
-                x[...], w_in[0, :, hidden + at : hidden + at + tile], preferred_element_type=F32
+                routed,
+                w_in[0, :, hidden_units + at : hidden_units + at + tile],
+                preferred_element_type=F32,
             )
             activated = (half_silu(gate * 0.5) * up).astype(BF16)
             term = jnp.dot(activated, w_out[0, at : at + tile, :], preferred_element_type=F32)
             total = term if total is None else total + term
+        done[...] = (hidden + total.astype(BF16).astype(F32)).astype(BF16)
+        for ref, sender in zip(out, (*senders, batch[0])):
+            at = jnp.where(me == sender, 0, capacity)
+            ref[...] = done[pl.ds(pl.multiple_of(at, capacity), capacity), :]
+
+    return pl.pallas_call(
+        kernel,
+        out_shape=(jax.ShapeDtypeStruct((capacity, model_width), BF16),) * (len(senders) + 1),
+        in_specs=[SMEM_SPEC] + [VMEM_SPEC] * (group + 6),
+        out_specs=(VMEM_SPEC,) * (len(senders) + 1),
+        scratch_shapes=[
+            pltpu.VMEM((size, model_width), F32),
+            pltpu.VMEM((size, model_width), BF16),
+        ],
+        compiler_params=limit(20),
+        cost_estimate=cost(6 * size * model_width * hidden_units, 8 * size * model_width),
+    )
+
+
+def make_mix(group, exchanges, rows, model_width, capacity):
+    def kernel(me_ref, *refs):
+        pieces, (slot, out) = refs[:-2], refs[-2:]
+        me = me_ref[0]
+        where = slot[:, 0:1]
+        per = len(pieces) // 2
+        first = functools.reduce(
+            jnp.logical_or, [me == target for _, target in exchanges[0][0]]
+        )
+        total = None
+        for j in range(per):
+            piece = jnp.where(
+                lax.broadcasted_iota(I32, (capacity, model_width), 0) * 0 + first.astype(I32) > 0,
+                pieces[j][...].astype(F32),
+                pieces[per + j][...].astype(F32),
+            ).astype(BF16)
+            turn = jnp.zeros_like(me)
+            if j < per - 1:
+                for exchange in exchanges:
+                    for source, target in exchange[j]:
+                        turn = jnp.where(me == target, (source - target) % group, turn)
+            place = lax.broadcasted_iota(I32, (rows, capacity), 1) + turn * capacity
+            pick = jnp.where(place == where, 1.0, 0.0).astype(BF16)
+            term = jnp.dot(pick, piece, preferred_element_type=F32)
+            total = term if total is None else total + term
         out[...] = total.astype(BF16)
 
     return pl.pallas_call(
         kernel,
         out_shape=jax.ShapeDtypeStruct((rows, model_width), BF16),
-        in_specs=[VMEM_SPEC] * 3,
+        in_specs=[SMEM_SPEC] + [VMEM_SPEC] * (2 * (len(exchanges[0]) + 1) + 1),
         out_specs=VMEM_SPEC,
         compiler_params=limit(16),
-        cost_estimate=cost(6 * rows * model_width * hidden, 4 * rows * model_width),
-        name="expert",
-    )
-
-
-def make_mix(group, rows, model_width, capacity):
-    def kernel(live_ref, *refs):
-        pieces = refs[:group]
-        hidden, slot, out = refs[group:]
-        total = hidden[...]
-        where = slot[:, 0:1]
-        for turn, piece in enumerate(pieces):
-            place = lax.broadcasted_iota(I32, (rows, capacity), 1) + turn * capacity
-            pick = jnp.where(place == where, 1.0, 0.0).astype(BF16)
-            total = total + jnp.dot(pick, piece[...], preferred_element_type=F32)
-        position = lax.broadcasted_iota(I32, (rows, 1), 0)
-        mask = (position < live_ref[0]).astype(F32)
-        out[...] = (mask * total).astype(BF16)
-
-    return pl.pallas_call(
-        kernel,
-        out_shape=jax.ShapeDtypeStruct((rows, model_width), BF16),
-        in_specs=[SMEM_SPEC] + [VMEM_SPEC] * (group + 2),
-        out_specs=VMEM_SPEC,
-        compiler_params=limit(12),
-        cost_estimate=cost(2 * rows * rows * model_width * 2, 8 * rows * model_width),
+        cost_estimate=cost(4 * rows * rows * model_width, 8 * rows * model_width),
         name="mix",
     )
+
+
+BATCHES = ((0, 3), (1, 2))
+HOMEWARD = (
+    (((1, 0), (2, 3)), ((2, 0), (1, 3)), ((3, 0), (0, 3))),
+    (((0, 1), (3, 2)), ((2, 1), (1, 2)), ((3, 1), (0, 2))),
+)
 
 
 def by_heads(
@@ -464,8 +550,14 @@
     chunks = list(zip([0, *ends[:-1]], ends))
 
     high = lax.div(live_counts[0], TAIL)
-    code = jnp.where(jnp.arange(TAIL, dtype=I32) < TAIL // 2, high, live_counts[0] - high * TAIL)
-    code = jnp.broadcast_to(code.astype(BF16)[:, None], (TAIL, width))
+    count_code = jnp.stack((high, live_counts[0] - high * TAIL))
+    code = jnp.concatenate(
+        (
+            domains.reshape(rows // width, width),
+            jnp.zeros((TAIL - 2 - rows // width, width), I32),
+            jnp.broadcast_to(count_code[:, None], (2, width)),
+        )
+    ).astype(BF16)
     cut = chunks[0][1] * rows
     opening = jnp.concatenate((table[item_ids[:cut]], code))
     rest = table[item_ids[cut:]]
@@ -477,50 +569,50 @@
         far.append(rotated(low[c], "emb", 1))
 
     weights = make_weights(model_width, width)(me, proj_in, proj_in, proj_in)
-    queries, own, before, after, candidates = [], [], [], [], []
+    queries, own, before, after, embedded = [], [], [], [], []
     lives = acc = None
     for c, blocks in enumerate(chunks):
         project = make_project(group, blocks, rows, width, model_width)
         known = () if c == 0 else (lives,)
         pieces = (mine[c], low[c], high[c], far[c])
-        if c == 1:
-            pieces, acc = lax.optimization_barrier((pieces, acc))
         q, kv, emb, *more = project(me, *known, *pieces, norm_gains, weights)
-        lives = more[0] if c == 0 else lives
+        if c == 0:
+            lives = more[0]
+            slots, slot_col = make_slots(group, rows, capacity)(me, lives, *pieces)
         queries.append(q)
         own.append(kv)
-        candidates.append(emb)
+        embedded.append(emb)
         before.append(shifted(kv, "seq", 1))
         after.append(shifted(kv, "seq", -1))
-        if c == 0:
-            (acc,) = make_own(chunks, True, rows, width)(lives, q, kv)
-    acc, q_all = make_own(chunks, False, rows, width)(lives, *queries, *own, acc)
-
-    gating, own_embedded, slot_row, slot_col = make_gate(
-        group, chunks, rows, model_width, capacity
-    )(me, live_counts, *candidates, norm_gains, proj_in, domains[None, :])
-
-    pieces = []
-    for t in range(group):
-        turn = make_turn(t, chunks, rows, width)
-        heads = turn(me, *before, *after, q_all, acc)
-        if t < group - 1:
-            heads = rotated(heads, "emb", t + 1)
-        pieces.append(heads)
-    route = make_route(group, rows, width, model_width, capacity)
-    hidden, *sent = route(me, *pieces, gating, own_embedded, norm_gains, proj_out, slot_row)
-    expert = make_expert(capacity, model_width, hidden_units)
-    arrived = [sent[0]]
-    for k in range(1, group):
-        arrived.append(rotated(sent[k], "emb", k))
-    returned = []
-    for k in range(group):
-        made = expert(arrived[k], expert_in, expert_out)
-        if k > 0:
-            made = rotated(made, "emb", -k)
-        returned.append(made)
-    mix = make_mix(group, rows, model_width, capacity)
-    return mix(live_counts, *returned, hidden, slot_col)
+        if c == len(chunks) - 2:
+            acc, q_all = make_own(chunks, True, rows, width)(lives, *queries, *own)
+    for c in range(len(chunks) - 1):
+        heads = () if c == 0 else (before[0], after[0])
+        acc = make_near(c, chunks, rows, width)(before[c], after[c], *heads, q_all, acc)
+    acc, q_all = make_own(chunks, False, rows, width)(lives, q_all, queries[-1], *own, acc)
+
+    sent = []
+    for batch in BATCHES:
+        last = make_last(batch, chunks, rows, width, capacity)
+        shares = last(*after, before[-1], before[0], q_all, acc, slots)
+        arrived = [shares[0]]
+        for k in range(1, group):
+            arrived.append(rotated(shares[k], "emb", k))
+        sent.append(arrived)
+    finished = []
+    for n, batch in enumerate(BATCHES):
+        homes, select = make_select(batch, chunks, rows, model_width, capacity)
+        emb, gating = select(*(embedded[h] for h in homes), slots, norm_gains, proj_in)
+        senders = [source for pairs in HOMEWARD[n] for source, target in pairs[:1]]
+        serve = make_serve(batch, senders, group, width, model_width, hidden_units, capacity)
+        made = serve(
+            me, *sent[n], emb, gating, norm_gains, proj_out, expert_in, expert_out
+        )
+        for j, pairs in enumerate(HOMEWARD[n]):
+            finished.append(lax.ppermute(made[j], "emb", pairs))
+        finished.append(made[-1])
+    mix = make_mix(group, HOMEWARD, rows, model_width, capacity)
+    return mix(me, *finished, slot_col)
 
 
 def by_rows(

time: 155 us -> 140 us (0.903)
  waiting for transfers between devices: 35.6 us -> 18.5 us
  Pallas kernels: 45.3 us -> 47.8 us
  local copies, waits for them, and re-layouts: 16.3 us -> 14.4 us
    ppermute x18 -> x15, waiting for transfers between devices: 35.6 us -> 4.71 us  [rotated(): lax.ppermute(value, axis, [(source, (source + steps) % count) for source...]
    ppermute x18 -> x15, starting transfers between devices: 39.4 us -> 24.4 us  [rotated(): lax.ppermute(value, axis, [(source, (source + steps) % count) for source...]
    ppermute x0 -> x6, starting transfers between devices: none -> 14.6 us  [by_heads(): finished.append(lax.ppermute(made[j], 'emb', pairs))]
    ppermute x0 -> x6, waiting for transfers between devices: none -> 13.8 us  [by_heads(): finished.append(lax.ppermute(made[j], 'emb', pairs))]
    pallas_call x13 -> x12, Pallas kernels: 41.2 us -> 43.5 us  [the longest x2 13.2 us: by_heads(): shares = last(*after, before[-1], before[0], q_all, acc, slots)]
    gather x1, local copies, waits for them, and re-layouts: 7.34 us -> 5.51 us  [by_heads(): opening = jnp.concatenate((table[item_ids[:cut]], code))]
  transfers between devices with their start and end apart: 24 -> 27, of which waited for: 7 -> 3; matrix products, arithmetic and copies ran while one was open for 5% -> 5% of each run, Pallas kernels for 24% -> 29%
where the time goes in v1:
time: 140 us; the launch traced here: 139 us
  starting transfers between devices  54.9 us (39%)
  Pallas kernels  47.8 us (34%)
  waiting for transfers between devices  18.5 us (13%)
  local copies, waits for them, and re-layouts  14.4 us (10%)
  other arithmetic  2.39 us (2%)
    ppermute x15, starting transfers between devices, rotated(): lax.ppermute(value, axis, [(source, (source + steps) % count) for source...  24.4 us
    ppermute x6, starting transfers between devices, shifted(): lax.ppermute(value, axis, [(source, source + steps) for source in range(f...  16 us
    ppermute x6, starting transfers between devices, by_heads(): finished.append(lax.ppermute(made[j], 'emb', pairs))  14.6 us
    ppermute x6, waiting for transfers between devices, by_heads(): finished.append(lax.ppermute(made[j], 'emb', pairs))  13.8 us
    pallas_call x2, Pallas kernels, by_heads(): shares = last(*after, before[-1], before[0], q_all, acc, slots)  13.2 us
    pallas_call x2, Pallas kernels, by_heads(): serve(me, *sent[n], emb, gating, norm_gains, proj_out, expert_in, expert_...  9.41 us
    pallas_call x1, Pallas kernels, by_heads(): make_own(chunks, False, rows, width)(lives, q_all, queries[-1], *own, acc)  7.88 us
    gather x1, local copies, waits for them, and re-layouts, by_heads(): rest = table[item_ids[cut:]]  7.1 us
  transfers between devices with their start and end apart: 27, of which 3 were waited for; matrix products, arithmetic and copies ran while one was open for 5% of the time, Pallas kernels for 29%

profile of v1, /device:TPU:2, one launch (start us, length us, event | category | flops | bytes accessed | tf_op | source)
XLA Modules:
  0.0 139.1 jit_solution(8010013690227493974)
XLA Ops:
  0.0 0.7 compare_select_fusion
  0.7 7.1 %gather_fusion.1 = bf16[1536,128]{1,0:T(8,128)(2,1)S(1)} fusion(bf16[32768,128]{1,0:T(8,128)(2,1)} %param.12, s32[2048]{0:T(1024)S(1)} %pad_clamp_fusion), kind=kCustom, calls=%fused_computation.1 | custom fusion | bytes 792576 | tf_op jit(solution)/shard_map/gather | solution.py:563
  7.9 1.6 %collective-permute-start.8 = (bf16[1024,128]{1,0:T(8,128)(2,1)S(1)}, bf16[1024,128]{1,0:T(8,128)(2,1)S(1)}, u32[]{:S(2)}, u32[]{:S(2)}) collective-permute-start(bf16[1024,128]{1,0:T(8,128)(2,1)S(1)} %slice.21.refs_1_), channel_id=1, source_target_pairs={{0,1},{1,2},{2,3},{3,0},{4,5},{5,6},{6,7},{7,4},{8,9},{9,10},{10,1... | collective-permute-start | bytes 786440 | tf_op jit(solution)/shard_map/ppermute | solution.py:34
  9.5 0.7 compare_select_fusion.1
  10.8 0.7 convert_bitcast_fusion
  11.8 5.5 %gather_fusion = bf16[512,128]{1,0:T(8,128)(2,1)S(1)} fusion(bf16[32768,128]{1,0:T(8,128)(2,1)} %param.12, s32[1024]{0:T(1024)S(1)} %pad_clamp_fusion.1), kind=kCustom, calls=%fused_computation | custom fusion | bytes 264192 | tf_op jit(solution)/shard_map/gather | solution.py:562
  17.5 1.6 %collective-permute-start = (bf16[528,128]{1,0:T(8,128)(2,1)S(1)}, bf16[528,128]{1,0:T(8,128)(2,1)S(1)}, u32[]{:S(2)}, u32[]{:S(2)}) collective-permute-start(bf16[528,128]{1,0:T(8,128)(2,1)S(1)} %maximum_maximum_fusion.refs_0_), channel_id=1, source_target_pairs={{0,1},{1,2},{2,3},{3,0},{4,5},{5,6},{6,7},{7,4},{8,9},{9,10},{10,1... | collective-permute-start | bytes 405512 | tf_op jit(solution)/shard_map/ppermute | solution.py:34
  19.1 1.6 %collective-permute-start.4 = (bf16[512,128]{1,0:T(8,128)(2,1)S(1)}, bf16[512,128]{1,0:T(8,128)(2,1)S(1)}, u32[]{:S(2)}, u32[]{:S(2)}) collective-permute-start(bf16[512,128]{1,0:T(8,128)(2,1)S(1)} %slice.20.refs_1_), channel_id=1, source_target_pairs={{0,1},{1,2},{2,3},{3,0},{4,5},{5,6},{6,7},{7,4},{8,9},{9,10},{10,1... | collective-permute-start | bytes 393224 | tf_op jit(solution)/shard_map/ppermute | solution.py:34
  20.8 2.2 %collective-permute-start.1 = (bf16[528,128]{1,0:T(8,128)(2,1)S(1)}, bf16[528,128]{1,0:T(8,128)(2,1)S(1)}, u32[]{:S(2)}, u32[]{:S(2)}) collective-permute-start(bf16[528,128]{1,0:T(8,128)(2,1)S(1)} %maximum_maximum_fusion.refs_0_), channel_id=1, source_target_pairs={{0,3},{1,0},{2,1},{3,2},{4,7},{5,4},{6,5},{7,6},{8,11},{9,8},{10,9... | collective-permute-start | bytes 405512 | tf_op jit(solution)/shard_map/ppermute | solution.py:34
  23.0 2.9 %collective-permute-done.refs_1_ = bf16[528,128]{1,0:T(8,128)(2,1)S(1)} collective-permute-done((bf16[528,128]{1,0:T(8,128)(2,1)S(1)}, bf16[528,128]{1,0:T(8,128)(2,1)S(1)}, u32[]{:S(2)}, u32[]{:S(2)}) %collective-permute-start) | collective-permute-done | bytes 135200 | tf_op jit(solution)/shard_map/ppermute | solution.py:34
  25.9 3.8 %collective-permute-start.5 = (bf16[512,128]{1,0:T(8,128)(2,1)S(1)}, bf16[512,128]{1,0:T(8,128)(2,1)S(1)}, u32[]{:S(2)}, u32[]{:S(2)}) collective-permute-start(bf16[512,128]{1,0:T(8,128)(2,1)S(1)} %slice.20.refs_1_), channel_id=1, source_target_pairs={{0,3},{1,0},{2,1},{3,2},{4,7},{5,4},{6,5},{7,6},{8,11},{9,8},{10,9... | collective-permute-start | bytes 393224 | tf_op jit(solution)/shard_map/ppermute | solution.py:34
  29.7 0.2 collective-permute-start.6
  30.0 1.8 %collective-permute-done.1.refs_2_ = bf16[528,128]{1,0:T(8,128)(2,1)S(1)} collective-permute-done((bf16[528,128]{1,0:T(8,128)(2,1)S(1)}, bf16[528,128]{1,0:T(8,128)(2,1)S(1)}, u32[]{:S(2)}, u32[]{:S(2)}) %collective-permute-start.1) | collective-permute-done | bytes 135200 | tf_op jit(solution)/shard_map/ppermute | solution.py:34
  31.8 1.8 %collective-permute-start.9 = (bf16[1024,128]{1,0:T(8,128)(2,1)S(1)}, bf16[1024,128]{1,0:T(8,128)(2,1)S(1)}, u32[]{:S(2)}, u32[]{:S(2)}) collective-permute-start(bf16[1024,128]{1,0:T(8,128)(2,1)S(1)} %slice.21.refs_1_), channel_id=1, source_target_pairs={{0,3},{1,0},{2,1},{3,2},{4,7},{5,4},{6,5},{7,6},{8,11},{9,8},{10,9... | collective-permute-start | bytes 786440 | tf_op jit(solution)/shard_map/ppermute | solution.py:34
  33.8 1.6 %copy-done = bf16[512,2048]{1,0:T(8,128)(2,1)S(1)} copy-done((bf16[512,2048]{1,0:T(8,128)(2,1)S(1)}, bf16[512,2048]{1,0:T(8,128)(2,1)}, u32[]{:S(2)}) %copy-start) | copy-done | bytes 2097176
  35.6 1.0 shard_map.91
  36.5 1.9 %collective-permute-start.13 = (bf16[528,256]{1,0:T(8,128)(2,1)S(1)}, bf16[528,256]{1,0:T(8,128)(2,1)S(1)}, u32[]{:S(2)}, u32[]{:S(2)}) collective-permute-start(bf16[528,256]{1,0:T(8,128)(2,1)S(1)} %get-tuple-element.41.refs_2_), channel_id=1, source_target_pairs={{0,4},{4,8},{8,12},{12,16},{16,20},{20,24},{24,28},{1,5},{5,9},{9,... | collective-permute-start | bytes 811016 | tf_op jit(solution)/shard_map/ppermute | solution.py:29
  38.5 3.6 %collective-permute-start.3 = (bf16[528,256]{1,0:T(8,128)(2,1)S(1)}, bf16[528,256]{1,0:T(8,128)(2,1)S(1)}, u32[]{:S(2)}, u32[]{:S(2)}) collective-permute-start(bf16[528,256]{1,0:T(8,128)(2,1)S(1)} %get-tuple-element.41.refs_2_), channel_id=1, source_target_pairs={{4,0},{8,4},{12,8},{16,12},{20,16},{24,20},{28,24},{5,1},{9,5},{13... | collective-permute-start | bytes 811016 | tf_op jit(solution)/shard_map/ppermute | solution.py:29
  42.1 1.3 shard_map.92
  43.5 1.9 %collective-permute-start.14 = (bf16[512,256]{1,0:T(8,128)(2,1)S(1)}, bf16[512,256]{1,0:T(8,128)(2,1)S(1)}, u32[]{:S(2)}, u32[]{:S(2)}) collective-permute-start(bf16[512,256]{1,0:T(8,128)(2,1)S(1)} %get-tuple-element.43.refs_3_), channel_id=1, source_target_pairs={{0,4},{4,8},{8,12},{12,16},{16,20},{20,24},{24,28},{1,5},{5,9},{9,... | collective-permute-start | bytes 786440 | tf_op jit(solution)/shard_map/ppermute | solution.py:29
  45.4 0.9 slots.1
  46.3 3.5 %own0.1 = (f32[1024,128]{1,0:T(8,128)S(1)}, bf16[1024,256]{1,0:T(8,128)(2,1)S(1)}) custom-call(s32[4]{0:T(128)S(1)} %get-tuple-element.42.refs_0_.lives_ref, bf16[512,256]{1,0:T(8,128)(2,1)S(1)} %get-tuple-element.45.refs_0_, bf16[512,256]{1,0:T(8,128)(2,1)S(1)} %get-tuple-element.46.refs_1_, bf16[528,256]{1,0:T(8,128)(2,1)S(1)} %get-tuple-element.41.refs_2_, ...), custom_call_target="tpu_custom_call" | custom-call | flops 2147483648 | bytes 1048576 | tf_op jit(solution)/shard_map/own0/pallas_call | solution.py:588
  49.8 2.9 %collective-permute-start.7 = (bf16[512,256]{1,0:T(8,128)(2,1)S(1)}, bf16[512,256]{1,0:T(8,128)(2,1)S(1)}, u32[]{:S(2)}, u32[]{:S(2)}) collective-permute-start(bf16[512,256]{1,0:T(8,128)(2,1)S(1)} %get-tuple-element.43.refs_3_), channel_id=1, source_target_pairs={{4,0},{8,4},{12,8},{16,12},{20,16},{24,20},{28,24},{5,1},{9,5},{13... | collective-permute-start | bytes 786440 | tf_op jit(solution)/shard_map/ppermute | solution.py:29
  52.7 1.8 %shard_map.93 = (bf16[1024,256]{1,0:T(8,128)(2,1)S(1)}, bf16[1024,256]{1,0:T(8,128)(2,1)S(1)}, bf16[1024,512]{1,0:T(8,128)(2,1)S(1)}) custom-call(s32[1]{0:T(128)} %bitcast.me.me_ref, s32[4]{0:T(128)S(1)} %get-tuple-element.42.refs_0_.lives_ref, bf16[1024,128]{1,0:T(8,128)(2,1)S(1)} %slice.21.refs_1_, bf16[1024,128]{1,0:T(8,128)(2,1)S(1)} %collective-permute-done.8.refs_2_, ...), custom_call_target="tpu_custom_call" | custom-call | flops 536870912 | bytes 2097152 | tf_op jit(solution)/shard_map/pallas_call | solution.py:578
  54.6 3.4 %collective-permute-start.12 = (bf16[1024,256]{1,0:T(8,128)(2,1)S(1)}, bf16[1024,256]{1,0:T(8,128)(2,1)S(1)}, u32[]{:S(2)}, u32[]{:S(2)}) collective-permute-start(bf16[1024,256]{1,0:T(8,128)(2,1)S(1)} %get-tuple-element.44.refs_4_), channel_id=1, source_target_pairs={{0,4},{4,8},{8,12},{12,16},{16,20},{20,24},{24,28},{1,5},{5,9},{9,... | collective-permute-start | bytes 1572872 | tf_op jit(solution)/shard_map/ppermute | solution.py:29
  58.0 0.8 shard_map.100
  58.9 0.8 shard_map.97
  59.7 2.1 %collective-permute-start.11 = (bf16[1024,256]{1,0:T(8,128)(2,1)S(1)}, bf16[1024,256]{1,0:T(8,128)(2,1)S(1)}, u32[]{:S(2)}, u32[]{:S(2)}) collective-permute-start(bf16[1024,256]{1,0:T(8,128)(2,1)S(1)} %get-tuple-element.44.refs_4_), channel_id=1, source_target_pairs={{4,0},{8,4},{12,8},{16,12},{20,16},{24,20},{28,24},{5,1},{9,5},{13... | collective-permute-start | bytes 1572872 | tf_op jit(solution)/shard_map/ppermute | solution.py:29
  61.9 2.4 %shard_map.94.refs_5_ = f32[1024,128]{1,0:T(8,128)S(1)} custom-call(bf16[528,256]{1,0:T(8,128)(2,1)S(1)} %collective-permute-done.13.refs_0_.refs_2_.refs_4_, bf16[528,256]{1,0:T(8,128)(2,1)S(1)} %collective-permute-done.3.refs_1_.refs_3_.refs_0_, bf16[1024,256]{1,0:T(8,128)(2,1)S(1)} %get-tuple-element.47.refs_2_.refs_4_.refs_0_, ...), custom_call_target="tpu_custom_call", output_to_operand_aliasing={{}: (3, {})} | custom-call | flops 1610612736 | bytes 1048576 | tf_op jit(solution)/shard_map/pallas_call | solution.py:591
  64.3 3.0 %shard_map.95.refs_5_ = f32[1024,128]{1,0:T(8,128)S(1)} custom-call(bf16[512,256]{1,0:T(8,128)(2,1)S(1)} %collective-permute-done.14.refs_0_, bf16[512,256]{1,0:T(8,128)(2,1)S(1)} %collective-permute-done.7.refs_1_, bf16[528,256]{1,0:T(8,128)(2,1)S(1)} %collective-permute-done.13.refs_0_.refs_2_.refs_4_, ...), custom_call_target="tpu_custom_call", output_to_operand_aliasing={{}: (5, {})} | custom-call | flops 1610612736 | bytes 1048576 | tf_op jit(solution)/shard_map/pallas_call | solution.py:591
  67.3 7.9 %own1.1 = (f32[2048,128]{1,0:T(8,128)S(1)}, bf16[2048,256]{1,0:T(8,128)(2,1)S(1)}) custom-call(s32[4]{0:T(128)S(1)} %get-tuple-element.42.refs_0_.lives_ref, bf16[1024,256]{1,0:T(8,128)(2,1)S(1)} %get-tuple-element.47.refs_2_.refs_4_.refs_0_, bf16[1024,256]{1,0:T(8,128)(2,1)S(1)} %get-tuple-element.48.refs_1_, ...), custom_call_target="tpu_custom_call" | custom-call | flops 6442450944 | bytes 2097152 | tf_op jit(solution)/shard_map/own1/pallas_call | solution.py:592
  75.2 6.4 %shard_map.99 = (bf16[512,128]{1,0:T(8,128)(2,1)S(1)}, bf16[512,128]{1,0:T(8,128)(2,1)S(1)}, bf16[512,128]{1,0:T(8,128)(2,1)S(1)}, bf16[512,128]{1,0:T(8,128)(2,1)S(1)}) custom-call(bf16[528,256]{1,0:T(8,128)(2,1)S(1)} %collective-permute-done.3.refs_1_.refs_3_.refs_0_, bf16[512,256]{1,0:T(8,128)(2,1)S(1)} %collective-permute-done.7.refs_1_, ...), custom_call_target="tpu_custom_call" | custom-call | flops 3758096384 | bytes 1048576 | tf_op jit(solution)/shard_map/pallas_call | solution.py:597
  81.6 2.0 %collective-permute-start.21 = (bf16[512,128]{1,0:T(8,128)(2,1)S(1)}, bf16[512,128]{1,0:T(8,128)(2,1)S(1)}, u32[]{:S(2)}, u32[]{:S(2)}) collective-permute-start(bf16[512,128]{1,0:T(8,128)(2,1)S(1)} %get-tuple-element.66), channel_id=1, source_target_pairs={{0,1},{1,2},{2,3},{3,0},{4,5},{5,6},{6,7},{7,4},{8,9},{9,10},{10,1... | collective-permute-start | bytes 393224 | tf_op jit(solution)/shard_map/ppermute | solution.py:34
  83.6 2.4 %collective-permute-start.22 = (bf16[512,128]{1,0:T(8,128)(2,1)S(1)}, bf16[512,128]{1,0:T(8,128)(2,1)S(1)}, u32[]{:S(2)}, u32[]{:S(2)}) collective-permute-start(bf16[512,128]{1,0:T(8,128)(2,1)S(1)} %get-tuple-element.67), channel_id=1, source_target_pairs={{0,2},{1,3},{2,0},{3,1},{4,6},{5,7},{6,4},{7,5},{8,10},{9,11},{10,... | collective-permute-start | bytes 393224 | tf_op jit(solution)/shard_map/ppermute | solution.py:34
  86.0 2.8 %collective-permute-start.23 = (bf16[512,128]{1,0:T(8,128)(2,1)S(1)}, bf16[512,128]{1,0:T(8,128)(2,1)S(1)}, u32[]{:S(2)}, u32[]{:S(2)}) collective-permute-start(bf16[512,128]{1,0:T(8,128)(2,1)S(1)} %get-tuple-element.68), channel_id=1, source_target_pairs={{0,3},{1,0},{2,1},{3,2},{4,7},{5,4},{6,5},{7,6},{8,11},{9,8},{10,9... | collective-permute-start | bytes 393224 | tf_op jit(solution)/shard_map/ppermute | solution.py:34
  88.9 6.8 %shard_map.96 = (bf16[512,128]{1,0:T(8,128)(2,1)S(1)}, bf16[512,128]{1,0:T(8,128)(2,1)S(1)}, bf16[512,128]{1,0:T(8,128)(2,1)S(1)}, bf16[512,128]{1,0:T(8,128)(2,1)S(1)}) custom-call(bf16[528,256]{1,0:T(8,128)(2,1)S(1)} %collective-permute-done.3.refs_1_.refs_3_.refs_0_, bf16[512,256]{1,0:T(8,128)(2,1)S(1)} %collective-permute-done.7.refs_1_, ...), custom_call_target="tpu_custom_call" | custom-call | flops 3758096384 | bytes 1048576 | tf_op jit(solution)/shard_map/pallas_call | solution.py:597
  95.8 0.6 collective-permute-start.16
  96.3 3.3 %collective-permute-start.17 = (bf16[512,128]{1,0:T(8,128)(2,1)S(1)}, bf16[512,128]{1,0:T(8,128)(2,1)S(1)}, u32[]{:S(2)}, u32[]{:S(2)}) collective-permute-start(bf16[512,128]{1,0:T(8,128)(2,1)S(1)} %get-tuple-element.56), channel_id=1, source_target_pairs={{0,3},{1,0},{2,1},{3,2},{4,7},{5,4},{6,5},{7,6},{8,11},{9,8},{10,9... | collective-permute-start | bytes 393224 | tf_op jit(solution)/shard_map/ppermute | solution.py:34
  99.6 4.7 %shard_map.101 = (bf16[256,512]{1,0:T(8,128)(2,1)S(1)}, bf16[256,512]{1,0:T(8,128)(2,1)S(1)}, bf16[256,512]{1,0:T(8,128)(2,1)S(1)}, bf16[256,512]{1,0:T(8,128)(2,1)S(1)}) custom-call(s32[1]{0:T(128)} %bitcast.me.me_ref, bf16[512,128]{1,0:T(8,128)(2,1)S(1)} %get-tuple-element.65.refs_0_, bf16[512,128]{1,0:T(8,128)(2,1)S(1)} %collective-permute-done.21.refs_1_, ...), custom_call_target="tpu_custom_call" | custom-call | flops 3221225472 | bytes 2097152 | tf_op jit(solution)/shard_map/pallas_call | solution.py:608
  104.3 2.5 %collective-permute-start.24 = (bf16[256,512]{1,0:T(8,128)(2,1)S(1)}, bf16[256,512]{1,0:T(8,128)(2,1)S(1)}, u32[]{:S(2)}, u32[]{:S(2)}) collective-permute-start(bf16[256,512]{1,0:T(8,128)(2,1)S(1)} %get-tuple-element.72), channel_id=1, source_target_pairs={{0,1},{3,2},{4,5},{7,6},{8,9},{11,10},{12,13},{15,14},{16,17},{19,... | collective-permute-start | bytes 786440 | tf_op jit(solution)/shard_map/ppermute | solution.py:612
  106.8 0.7 collective-permute-start.25
  107.5 4.0 %collective-permute-start.26 = (bf16[256,512]{1,0:T(8,128)(2,1)S(1)}, bf16[256,512]{1,0:T(8,128)(2,1)S(1)}, u32[]{:S(2)}, u32[]{:S(2)}) collective-permute-start(bf16[256,512]{1,0:T(8,128)(2,1)S(1)} %get-tuple-element.74), channel_id=1, source_target_pairs={{3,1},{0,2},{7,5},{4,6},{11,9},{8,10},{15,13},{12,14},{19,17},{16,... | collective-permute-start | bytes 786440 | tf_op jit(solution)/shard_map/ppermute | solution.py:612
  111.5 4.7 %shard_map.98 = (bf16[256,512]{1,0:T(8,128)(2,1)S(1)}, bf16[256,512]{1,0:T(8,128)(2,1)S(1)}, bf16[256,512]{1,0:T(8,128)(2,1)S(1)}, bf16[256,512]{1,0:T(8,128)(2,1)S(1)}) custom-call(s32[1]{0:T(128)} %bitcast.me.me_ref, bf16[512,128]{1,0:T(8,128)(2,1)S(1)} %get-tuple-element.53.refs_0_, bf16[512,128]{1,0:T(8,128)(2,1)S(1)} %collective-permute-done.15.refs_1_, ...), custom_call_target="tpu_custom_call" | custom-call | flops 3221225472 | bytes 2097152 | tf_op jit(solution)/shard_map/pallas_call | solution.py:608
  116.3 1.3 collective-permute-start.18
  117.6 1.3 collective-permute-start.19
  118.9 4.8 %collective-permute-start.20 = (bf16[256,512]{1,0:T(8,128)(2,1)S(1)}, bf16[256,512]{1,0:T(8,128)(2,1)S(1)}, u32[]{:S(2)}, u32[]{:S(2)}) collective-permute-start(bf16[256,512]{1,0:T(8,128)(2,1)S(1)} %get-tuple-element.63), channel_id=1, source_target_pairs={{3,0},{0,3},{7,4},{4,7},{11,8},{8,11},{15,12},{12,15},{19,16},{16,... | collective-permute-start | bytes 786440 | tf_op jit(solution)/shard_map/ppermute | solution.py:612
  123.7 13.8 %collective-permute-done.18.refs_0_ = bf16[256,512]{1,0:T(8,128)(2,1)S(1)} collective-permute-done((bf16[256,512]{1,0:T(8,128)(2,1)S(1)}, bf16[256,512]{1,0:T(8,128)(2,1)S(1)}, u32[]{:S(2)}, u32[]{:S(2)}) %collective-permute-start.18) | collective-permute-done | bytes 262176 | tf_op jit(solution)/shard_map/ppermute | solution.py:612
  137.5 1.6 %mix.1 = bf16[512,512]{1,0:T(8,128)(2,1)} custom-call(s32[1]{0:T(128)} %bitcast.me.me_ref, bf16[256,512]{1,0:T(8,128)(2,1)S(1)} %collective-permute-done.18.refs_0_, bf16[256,512]{1,0:T(8,128)(2,1)S(1)} %collective-permute-done.19.refs_1_, bf16[256,512]{1,0:T(8,128)(2,1)S(1)} %collective-permute-done.20.refs_2_, ...), custom_call_target="tpu_custom_call" | custom-call | flops 536870912 | bytes 2097152 | tf_op jit(solution)/shard_map/mix/pallas_call | solution.py:615
  (48 shorter events, 1.0 us)
Async XLA Ops:
  0.0 35.6 %copy-start.2 = (f32[3,512]{1,0:T(4,128)S(1)}, f32[3,512]{1,0:T(4,128)}, u32[]{:S(2)}) copy-start(f32[3,512]{1,0:T(4,128)} %refs_6_.3) | copy-start | bytes 18436
  7.9 25.7 %collective-permute-start.8 = (bf16[1024,128]{1,0:T(8,128)(2,1)S(1)}, bf16[1024,128]{1,0:T(8,128)(2,1)S(1)}, u32[]{:S(2)}, u32[]{:S(2)}) collective-permute-start(bf16[1024,128]{1,0:T(8,128)(2,1)S(1)} %slice.21.refs_1_), channel_id=1, source_target_pairs={{0,1},{1,2},{2,3},{3,0},{4,5},{5,6},{6,7},{7,4},{8,9},{9,10},{10,1... | collective-permute-start | bytes 786440 | tf_op jit(solution)/shard_map/ppermute | solution.py:34
  17.5 8.4 %collective-permute-start = (bf16[528,128]{1,0:T(8,128)(2,1)S(1)}, bf16[528,128]{1,0:T(8,128)(2,1)S(1)}, u32[]{:S(2)}, u32[]{:S(2)}) collective-permute-start(bf16[528,128]{1,0:T(8,128)(2,1)S(1)} %maximum_maximum_fusion.refs_0_), channel_id=1, source_target_pairs={{0,1},{1,2},{2,3},{3,0},{4,5},{5,6},{6,7},{7,4},{8,9},{9,10},{10,1... | collective-permute-start | bytes 405512 | tf_op jit(solution)/shard_map/ppermute | solution.py:34
  19.1 10.6 %collective-permute-start.4 = (bf16[512,128]{1,0:T(8,128)(2,1)S(1)}, bf16[512,128]{1,0:T(8,128)(2,1)S(1)}, u32[]{:S(2)}, u32[]{:S(2)}) collective-permute-start(bf16[512,128]{1,0:T(8,128)(2,1)S(1)} %slice.20.refs_1_), channel_id=1, source_target_pairs={{0,1},{1,2},{2,3},{3,0},{4,5},{5,6},{6,7},{7,4},{8,9},{9,10},{10,1... | collective-permute-start | bytes 393224 | tf_op jit(solution)/shard_map/ppermute | solution.py:34
  20.8 11.0 %collective-permute-start.1 = (bf16[528,128]{1,0:T(8,128)(2,1)S(1)}, bf16[528,128]{1,0:T(8,128)(2,1)S(1)}, u32[]{:S(2)}, u32[]{:S(2)}) collective-permute-start(bf16[528,128]{1,0:T(8,128)(2,1)S(1)} %maximum_maximum_fusion.refs_0_), channel_id=1, source_target_pairs={{0,3},{1,0},{2,1},{3,2},{4,7},{5,4},{6,5},{7,6},{8,11},{9,8},{10,9... | collective-permute-start | bytes 405512 | tf_op jit(solution)/shard_map/ppermute | solution.py:34
  25.9 9.6 %collective-permute-start.2 = (bf16[528,128]{1,0:T(8,128)(2,1)S(1)}, bf16[528,128]{1,0:T(8,128)(2,1)S(1)}, u32[]{:S(2)}, u32[]{:S(2)}) collective-permute-start(bf16[528,128]{1,0:T(8,128)(2,1)S(1)} %collective-permute-done.refs_1_), channel_id=1, source_target_pairs={{0,1},{1,2},{2,3},{3,0},{4,5},{5,6},{6,7},{7,4},{8,9},{9,10},{10,1... | collective-permute-start | bytes 405512 | tf_op jit(solution)/shard_map/ppermute | solution.py:34
  25.9 12.6 %collective-permute-start.5 = (bf16[512,128]{1,0:T(8,128)(2,1)S(1)}, bf16[512,128]{1,0:T(8,128)(2,1)S(1)}, u32[]{:S(2)}, u32[]{:S(2)}) collective-permute-start(bf16[512,128]{1,0:T(8,128)(2,1)S(1)} %slice.20.refs_1_), channel_id=1, source_target_pairs={{0,3},{1,0},{2,1},{3,2},{4,7},{5,4},{6,5},{7,6},{8,11},{9,8},{10,9... | collective-permute-start | bytes 393224 | tf_op jit(solution)/shard_map/ppermute | solution.py:34
  29.7 12.4 %collective-permute-start.6 = (bf16[512,128]{1,0:T(8,128)(2,1)S(1)}, bf16[512,128]{1,0:T(8,128)(2,1)S(1)}, u32[]{:S(2)}, u32[]{:S(2)}) collective-permute-start(bf16[512,128]{1,0:T(8,128)(2,1)S(1)} %collective-permute-done.4.refs_2_), channel_id=1, source_target_pairs={{0,1},{1,2},{2,3},{3,0},{4,5},{5,6},{6,7},{7,4},{8,9},{9,10},{10,1... | collective-permute-start | bytes 393224 | tf_op jit(solution)/shard_map/ppermute | solution.py:34
  31.8 18.0 %collective-permute-start.9 = (bf16[1024,128]{1,0:T(8,128)(2,1)S(1)}, bf16[1024,128]{1,0:T(8,128)(2,1)S(1)}, u32[]{:S(2)}, u32[]{:S(2)}) collective-permute-start(bf16[1024,128]{1,0:T(8,128)(2,1)S(1)} %slice.21.refs_1_), channel_id=1, source_target_pairs={{0,3},{1,0},{2,1},{3,2},{4,7},{5,4},{6,5},{7,6},{8,11},{9,8},{10,9... | collective-permute-start | bytes 786440 | tf_op jit(solution)/shard_map/ppermute | solution.py:34
  33.6 19.1 %collective-permute-start.10 = (bf16[1024,128]{1,0:T(8,128)(2,1)S(1)}, bf16[1024,128]{1,0:T(8,128)(2,1)S(1)}, u32[]{:S(2)}, u32[]{:S(2)}) collective-permute-start(bf16[1024,128]{1,0:T(8,128)(2,1)S(1)} %collective-permute-done.8.refs_2_), channel_id=1, source_target_pairs={{0,1},{1,2},{2,3},{3,0},{4,5},{5,6},{6,7},{7,4},{8,9},{9,10},{10,1... | collective-permute-start | bytes 786440 | tf_op jit(solution)/shard_map/ppermute | solution.py:34
  33.8 1.6 %copy-start = (bf16[512,2048]{1,0:T(8,128)(2,1)S(1)}, bf16[512,2048]{1,0:T(8,128)(2,1)}, u32[]{:S(2)}) copy-start(bf16[512,2048]{1,0:T(8,128)(2,1)} %refs_4_.5) | copy-start | bytes 6291460
  35.4 22.6 %copy-start.1 = (bf16[512,2048]{1,0:T(8,128)(2,1)S(1)}, bf16[512,2048]{1,0:T(8,128)(2,1)}, u32[]{:S(2)}) copy-start(bf16[512,2048]{1,0:T(8,128)(2,1)} %refs_4_.5) | copy-start | bytes 6291460
  36.5 23.2 %collective-permute-start.13 = (bf16[528,256]{1,0:T(8,128)(2,1)S(1)}, bf16[528,256]{1,0:T(8,128)(2,1)S(1)}, u32[]{:S(2)}, u32[]{:S(2)}) collective-permute-start(bf16[528,256]{1,0:T(8,128)(2,1)S(1)} %get-tuple-element.41.refs_2_), channel_id=1, source_target_pairs={{0,4},{4,8},{8,12},{12,16},{16,20},{20,24},{24,28},{1,5},{5,9},{9,... | collective-permute-start | bytes 811016 | tf_op jit(solution)/shard_map/ppermute | solution.py:29
  38.5 23.4 %collective-permute-start.3 = (bf16[528,256]{1,0:T(8,128)(2,1)S(1)}, bf16[528,256]{1,0:T(8,128)(2,1)S(1)}, u32[]{:S(2)}, u32[]{:S(2)}) collective-permute-start(bf16[528,256]{1,0:T(8,128)(2,1)S(1)} %get-tuple-element.41.refs_2_), channel_id=1, source_target_pairs={{4,0},{8,4},{12,8},{16,12},{20,16},{24,20},{28,24},{5,1},{9,5},{13... | collective-permute-start | bytes 811016 | tf_op jit(solution)/shard_map/ppermute | solution.py:29
  43.5 20.8 %collective-permute-start.14 = (bf16[512,256]{1,0:T(8,128)(2,1)S(1)}, bf16[512,256]{1,0:T(8,128)(2,1)S(1)}, u32[]{:S(2)}, u32[]{:S(2)}) collective-permute-start(bf16[512,256]{1,0:T(8,128)(2,1)S(1)} %get-tuple-element.43.refs_3_), channel_id=1, source_target_pairs={{0,4},{4,8},{8,12},{12,16},{16,20},{20,24},{24,28},{1,5},{5,9},{9,... | collective-permute-start | bytes 786440 | tf_op jit(solution)/shard_map/ppermute | solution.py:29
  49.8 14.5 %collective-permute-start.7 = (bf16[512,256]{1,0:T(8,128)(2,1)S(1)}, bf16[512,256]{1,0:T(8,128)(2,1)S(1)}, u32[]{:S(2)}, u32[]{:S(2)}) collective-permute-start(bf16[512,256]{1,0:T(8,128)(2,1)S(1)} %get-tuple-element.43.refs_3_), channel_id=1, source_target_pairs={{4,0},{8,4},{12,8},{16,12},{20,16},{24,20},{28,24},{5,1},{9,5},{13... | collective-permute-start | bytes 786440 | tf_op jit(solution)/shard_map/ppermute | solution.py:29
  54.6 20.6 %collective-permute-start.12 = (bf16[1024,256]{1,0:T(8,128)(2,1)S(1)}, bf16[1024,256]{1,0:T(8,128)(2,1)S(1)}, u32[]{:S(2)}, u32[]{:S(2)}) collective-permute-start(bf16[1024,256]{1,0:T(8,128)(2,1)S(1)} %get-tuple-element.44.refs_4_), channel_id=1, source_target_pairs={{0,4},{4,8},{8,12},{12,16},{16,20},{20,24},{24,28},{1,5},{5,9},{9,... | collective-permute-start | bytes 1572872 | tf_op jit(solution)/shard_map/ppermute | solution.py:29
  59.7 15.5 %collective-permute-start.11 = (bf16[1024,256]{1,0:T(8,128)(2,1)S(1)}, bf16[1024,256]{1,0:T(8,128)(2,1)S(1)}, u32[]{:S(2)}, u32[]{:S(2)}) collective-permute-start(bf16[1024,256]{1,0:T(8,128)(2,1)S(1)} %get-tuple-element.44.refs_4_), channel_id=1, source_target_pairs={{4,0},{8,4},{12,8},{16,12},{20,16},{24,20},{28,24},{5,1},{9,5},{13... | collective-permute-start | bytes 1572872 | tf_op jit(solution)/shard_map/ppermute | solution.py:29
  81.6 18.0 %copy-start.3 = (bf16[1,512,4096]{2,1,0:T(8,128)(2,1)S(1)}, bf16[1,512,4096]{2,1,0:T(8,128)(2,1)}, u32[]{:S(2)}) copy-start(bf16[1,512,4096]{2,1,0:T(8,128)(2,1)} %refs_8_.3) | copy-start | bytes 12582916
  81.6 18.0 %copy-start.4 = (bf16[1,2048,512]{2,1,0:T(8,128)(2,1)S(1)}, bf16[1,2048,512]{2,1,0:T(8,128)(2,1)}, u32[]{:S(2)}) copy-start(bf16[1,2048,512]{2,1,0:T(8,128)(2,1)} %refs_9_.3) | copy-start | bytes 6291460
  81.6 18.0 %copy-start.5 = (bf16[512,512]{1,0:T(8,128)(2,1)S(1)}, bf16[512,512]{1,0:T(8,128)(2,1)}, u32[]{:S(2)}) copy-start(bf16[512,512]{1,0:T(8,128)(2,1)} %refs_7_.3) | copy-start | bytes 1572868
  81.6 14.7 %collective-permute-start.21 = (bf16[512,128]{1,0:T(8,128)(2,1)S(1)}, bf16[512,128]{1,0:T(8,128)(2,1)S(1)}, u32[]{:S(2)}, u32[]{:S(2)}) collective-permute-start(bf16[512,128]{1,0:T(8,128)(2,1)S(1)} %get-tuple-element.66), channel_id=1, source_target_pairs={{0,1},{1,2},{2,3},{3,0},{4,5},{5,6},{6,7},{7,4},{8,9},{9,10},{10,1... | collective-permute-start | bytes 393224 | tf_op jit(solution)/shard_map/ppermute | solution.py:34
  83.6 15.9 %collective-permute-start.22 = (bf16[512,128]{1,0:T(8,128)(2,1)S(1)}, bf16[512,128]{1,0:T(8,128)(2,1)S(1)}, u32[]{:S(2)}, u32[]{:S(2)}) collective-permute-start(bf16[512,128]{1,0:T(8,128)(2,1)S(1)} %get-tuple-element.67), channel_id=1, source_target_pairs={{0,2},{1,3},{2,0},{3,1},{4,6},{5,7},{6,4},{7,5},{8,10},{9,11},{10,... | collective-permute-start | bytes 393224 | tf_op jit(solution)/shard_map/ppermute | solution.py:34
  86.0 13.6 %collective-permute-start.23 = (bf16[512,128]{1,0:T(8,128)(2,1)S(1)}, bf16[512,128]{1,0:T(8,128)(2,1)S(1)}, u32[]{:S(2)}, u32[]{:S(2)}) collective-permute-start(bf16[512,128]{1,0:T(8,128)(2,1)S(1)} %get-tuple-element.68), channel_id=1, source_target_pairs={{0,3},{1,0},{2,1},{3,2},{4,7},{5,4},{6,5},{7,6},{8,11},{9,8},{10,9... | collective-permute-start | bytes 393224 | tf_op jit(solution)/shard_map/ppermute | solution.py:34
  95.7 11.8 %collective-permute-start.15 = (bf16[512,128]{1,0:T(8,128)(2,1)S(1)}, bf16[512,128]{1,0:T(8,128)(2,1)S(1)}, u32[]{:S(2)}, u32[]{:S(2)}) collective-permute-start(bf16[512,128]{1,0:T(8,128)(2,1)S(1)} %get-tuple-element.54), channel_id=1, source_target_pairs={{0,1},{1,2},{2,3},{3,0},{4,5},{5,6},{6,7},{7,4},{8,9},{9,10},{10,1... | collective-permute-start | bytes 393224 | tf_op jit(solution)/shard_map/ppermute | solution.py:34
  95.8 15.8 %collective-permute-start.16 = (bf16[512,128]{1,0:T(8,128)(2,1)S(1)}, bf16[512,128]{1,0:T(8,128)(2,1)S(1)}, u32[]{:S(2)}, u32[]{:S(2)}) collective-permute-start(bf16[512,128]{1,0:T(8,128)(2,1)S(1)} %get-tuple-element.55), channel_id=1, source_target_pairs={{0,2},{1,3},{2,0},{3,1},{4,6},{5,7},{6,4},{7,5},{8,10},{9,11},{10,... | collective-permute-start | bytes 393224 | tf_op jit(solution)/shard_map/ppermute | solution.py:34
  96.3 15.2 %collective-permute-start.17 = (bf16[512,128]{1,0:T(8,128)(2,1)S(1)}, bf16[512,128]{1,0:T(8,128)(2,1)S(1)}, u32[]{:S(2)}, u32[]{:S(2)}) collective-permute-start(bf16[512,128]{1,0:T(8,128)(2,1)S(1)} %get-tuple-element.56), channel_id=1, source_target_pairs={{0,3},{1,0},{2,1},{3,2},{4,7},{5,4},{6,5},{7,6},{8,11},{9,8},{10,9... | collective-permute-start | bytes 393224 | tf_op jit(solution)/shard_map/ppermute | solution.py:34
  104.3 14.5 %collective-permute-start.24 = (bf16[256,512]{1,0:T(8,128)(2,1)S(1)}, bf16[256,512]{1,0:T(8,128)(2,1)S(1)}, u32[]{:S(2)}, u32[]{:S(2)}) collective-permute-start(bf16[256,512]{1,0:T(8,128)(2,1)S(1)} %get-tuple-element.72), channel_id=1, source_target_pairs={{0,1},{3,2},{4,5},{7,6},{8,9},{11,10},{12,13},{15,14},{16,17},{19,... | collective-permute-start | bytes 786440 | tf_op jit(solution)/shard_map/ppermute | solution.py:612
  106.8 16.9 %collective-permute-start.25 = (bf16[256,512]{1,0:T(8,128)(2,1)S(1)}, bf16[256,512]{1,0:T(8,128)(2,1)S(1)}, u32[]{:S(2)}, u32[]{:S(2)}) collective-permute-start(bf16[256,512]{1,0:T(8,128)(2,1)S(1)} %get-tuple-element.73), channel_id=1, source_target_pairs={{2,1},{1,2},{6,5},{5,6},{10,9},{9,10},{14,13},{13,14},{18,17},{17,... | collective-permute-start | bytes 786440 | tf_op jit(solution)/shard_map/ppermute | solution.py:612
  107.5 16.2 %collective-permute-start.26 = (bf16[256,512]{1,0:T(8,128)(2,1)S(1)}, bf16[256,512]{1,0:T(8,128)(2,1)S(1)}, u32[]{:S(2)}, u32[]{:S(2)}) collective-permute-start(bf16[256,512]{1,0:T(8,128)(2,1)S(1)} %get-tuple-element.74), channel_id=1, source_target_pairs={{3,1},{0,2},{7,5},{4,6},{11,9},{8,10},{15,13},{12,14},{19,17},{16,... | collective-permute-start | bytes 786440 | tf_op jit(solution)/shard_map/ppermute | solution.py:612
  116.3 21.2 %collective-permute-start.18 = (bf16[256,512]{1,0:T(8,128)(2,1)S(1)}, bf16[256,512]{1,0:T(8,128)(2,1)S(1)}, u32[]{:S(2)}, u32[]{:S(2)}) collective-permute-start(bf16[256,512]{1,0:T(8,128)(2,1)S(1)} %get-tuple-element.61), channel_id=1, source_target_pairs={{1,0},{2,3},{5,4},{6,7},{9,8},{10,11},{13,12},{14,15},{17,16},{18,... | collective-permute-start | bytes 786440 | tf_op jit(solution)/shard_map/ppermute | solution.py:612
  117.6 19.9 %collective-permute-start.19 = (bf16[256,512]{1,0:T(8,128)(2,1)S(1)}, bf16[256,512]{1,0:T(8,128)(2,1)S(1)}, u32[]{:S(2)}, u32[]{:S(2)}) collective-permute-start(bf16[256,512]{1,0:T(8,128)(2,1)S(1)} %get-tuple-element.62), channel_id=1, source_target_pairs={{2,0},{1,3},{6,4},{5,7},{10,8},{9,11},{14,12},{13,15},{18,16},{17,... | collective-permute-start | bytes 786440 | tf_op jit(solution)/shard_map/ppermute | solution.py:612
  118.9 18.6 %collective-permute-start.20 = (bf16[256,512]{1,0:T(8,128)(2,1)S(1)}, bf16[256,512]{1,0:T(8,128)(2,1)S(1)}, u32[]{:S(2)}, u32[]{:S(2)}) collective-permute-start(bf16[256,512]{1,0:T(8,128)(2,1)S(1)} %get-tuple-element.63), channel_id=1, source_target_pairs={{3,0},{0,3},{7,4},{4,7},{11,8},{8,11},{15,12},{12,15},{19,16},{16,... | collective-permute-start | bytes 786440 | tf_op jit(solution)/shard_map/ppermute | solution.py:612

commit v2 on v1

--- a/solution.py
+++ b/solution.py
@@ -13,8 +13,7 @@
 HEAD_DIM = 64
 SPAN = 4
 NORM_EPS = 1e-06
-CHUNKS = (0.25, 0.25, 0.5)
-KEY_TILE = 256
+CHUNKS = (0.5, 0.5)
 TAIL = 16
 MIB = 1 << 20
 
@@ -147,11 +146,11 @@
     )
 
 
-def pair(queries, q_at, q_pos, kv_ref, k_at, k_pos, acc_ref, acc_at, rows, keep, live, width):
-    tiles = lax.div(live + (KEY_TILE - 1), KEY_TILE)
+def pair(queries, q_at, q_pos, kv_ref, k_at, k_pos, acc_ref, acc_at, rows, keep, live, tile_keys, width):
+    tiles = lax.div(live + (tile_keys - 1), tile_keys)
 
     def step(tile, carry):
-        at = pl.ds(pl.multiple_of(k_at + tile * KEY_TILE, KEY_TILE), KEY_TILE)
+        at = pl.ds(pl.multiple_of(k_at + tile * tile_keys, tile_keys), tile_keys)
         keys = kv_ref[at, :width]
         values = kv_ref[at, width:]
         low = lax.broadcasted_iota(I32, values.shape, 1) < HEAD_DIM
@@ -167,7 +166,7 @@
             weights = half_silu(half)
             if keep is not None:
                 query = lax.broadcasted_iota(I32, weights.shape, 0) + q_pos
-                key = lax.broadcasted_iota(I32, weights.shape, 1) + (k_pos + tile * KEY_TILE)
+                key = lax.broadcasted_iota(I32, weights.shape, 1) + (k_pos + tile * tile_keys)
                 weights = jnp.where(keep(query, key), weights, 0.0)
             held = jnp.where(low, values, zero) if head == 0 else jnp.where(low, zero, values)
             term = jnp.dot(weights.astype(BF16), held, preferred_element_type=F32)
@@ -238,6 +237,7 @@
                     (past - start) * block_rows,
                     None,
                     lives_ref[k],
+                    block_rows,
                     width,
                 )
                 start = past
@@ -288,6 +288,7 @@
                     (high - low) * block_rows,
                     keep,
                     (lives_before if held is before else lives_after)[k],
+                    block_rows // 2,
                     width,
                 )
 
@@ -335,6 +336,7 @@
                     block_rows,
                     keep,
                     live,
+                    block_rows // 2,
                     width,
                 )
 
@@ -363,7 +365,7 @@
     )
 
 
-def make_slots(group, block_rows, capacity):
+def make_slots(group, head_rows, block_rows, capacity):
     lanes = 128
     strips = block_rows // lanes
 
@@ -379,7 +381,7 @@
         expert = lax.broadcasted_iota(I32, (8, block_rows), 0)
         for piece, offset in zip(pieces, (0, group - 1, 1, 2)):
             block = lax.rem(me + offset, group)
-            code = piece[pl.ds(block_rows, TAIL), :].astype(F32)
+            code = piece[pl.ds(head_rows, TAIL), :].astype(F32)
             domain = jnp.concatenate([code[r : r + 1, :] for r in range(strips)], axis=1)
             turn = domain.astype(I32) - me
             turn = jnp.where(turn < 0, turn + group, turn)
@@ -559,8 +561,9 @@
         )
     ).astype(BF16)
     cut = chunks[0][1] * rows
-    opening = jnp.concatenate((table[item_ids[:cut]], code))
-    rest = table[item_ids[cut:]]
+    fetch = lambda ids: table.at[ids].get(mode="promise_in_bounds", wrap_negative_indices=False)
+    opening = jnp.concatenate((fetch(item_ids[:cut]), code))
+    rest = fetch(item_ids[cut:])
     mine = [opening] + [rest[a * rows - cut : b * rows - cut] for a, b in chunks[1:]]
     low, high, far = [], [], []
     for c, piece in enumerate(mine):
@@ -578,7 +581,7 @@
         q, kv, emb, *more = project(me, *known, *pieces, norm_gains, weights)
         if c == 0:
             lives = more[0]
-            slots, slot_col = make_slots(group, rows, capacity)(me, lives, *pieces)
+            slots, slot_col = make_slots(group, cut, rows, capacity)(me, lives, *pieces)
         queries.append(q)
         own.append(kv)
         embedded.append(emb)

time: 140 us -> 141 us (level)
  starting transfers between devices: 54.9 us -> 49.4 us
  waiting for transfers between devices: 18.5 us -> 23.7 us
  local copies, waits for them, and re-layouts: 14.4 us -> 16.8 us
    ppermute x15 -> x12, waiting for transfers between devices: 4.71 us -> 11.8 us  [rotated(): lax.ppermute(value, axis, [(source, (source + steps) % count) for source...]
    ppermute x6 -> x4, starting transfers between devices: 16 us -> 11.1 us  [shifted(): lax.ppermute(value, axis, [(source, source + steps) for source in range(f...]
    gather x2, local copies, waits for them, and re-layouts: 12.6 us -> 14.8 us  [by_heads(): table.at[ids].get(mode='promise_in_bounds', wrap_negative_indices=False)]
    ppermute x6, waiting for transfers between devices: 13.8 us -> 11.8 us  [by_heads(): finished.append(lax.ppermute(made[j], 'emb', pairs))]
    ppermute x15 -> x12, starting transfers between devices: 24.4 us -> 23.8 us  [rotated(): lax.ppermute(value, axis, [(source, (source + steps) % count) for source...]
    pallas_call x3 -> x2, Pallas kernels: 4.08 us -> 3.96 us  [by_heads(): q, kv, emb, *more = project(me, *known, *pieces, norm_gains, weights)]
    pallas_call x2 -> x1, Pallas kernels: 5.39 us -> 5.28 us  [by_heads(): make_near(c, chunks, rows, width)(before[c], after[c], *heads, q_all, acc)]
  transfers between devices with their start and end apart: 27 -> 22, of which waited for: 3 -> 4; matrix products, arithmetic and copies ran while one was open for 5% -> 5% of each run, Pallas kernels for 29% -> 28%
where the time goes in v2:
time: 141 us; the launch traced here: 140 us
  starting transfers between devices  49.4 us (35%)
  Pallas kernels  47.7 us (34%)
  waiting for transfers between devices  23.7 us (17%)
  local copies, waits for them, and re-layouts  16.8 us (12%)
  other arithmetic  1.47 us (1%)
    ppermute x12, starting transfers between devices, rotated(): lax.ppermute(value, axis, [(source, (source + steps) % count) for source...  23.8 us
    gather x2, local copies, waits for them, and re-layouts, by_heads(): table.at[ids].get(mode='promise_in_bounds', wrap_negative_indices=False)  14.8 us
    ppermute x6, starting transfers between devices, by_heads(): finished.append(lax.ppermute(made[j], 'emb', pairs))  14.6 us
    pallas_call x2, Pallas kernels, by_heads(): shares = last(*after, before[-1], before[0], q_all, acc, slots)  13.4 us
    ppermute x6, waiting for transfers between devices, by_heads(): finished.append(lax.ppermute(made[j], 'emb', pairs))  11.8 us
    ppermute x12, waiting for transfers between devices, rotated(): lax.ppermute(value, axis, [(source, (source + steps) % count) for source...  11.8 us
    ppermute x4, starting transfers between devices, shifted(): lax.ppermute(value, axis, [(source, source + steps) for source in range(f...  11.1 us
    pallas_call x2, Pallas kernels, by_heads(): serve(me, *sent[n], emb, gating, norm_gains, proj_out, expert_in, expert_...  9.29 us
  transfers between devices with their start and end apart: 22, of which 4 were waited for; matrix products, arithmetic and copies ran while one was open for 5% of the time, Pallas kernels for 28%

profile of v2, /device:TPU:2, one launch (start us, length us, event | category | flops | bytes accessed | tf_op | source)
XLA Modules:
  0.0 140.0 jit_solution(8378935720285542319)
XLA Ops:
  0.7 0.7 convert_bitcast_fusion
  1.4 0.7 slice_clamp_fusion
  2.1 0.1 add_convert_fusion
  2.2 7.5 %gather_fusion = bf16[1024,128]{1,0:T(8,128)(2,1)S(1)} fusion(bf16[32768,128]{1,0:T(8,128)(2,1)} %param.12, s32[1024]{0:T(1024)S(1)} %get-tuple-element.72), kind=kCustom, calls=%fused_computation | custom fusion | bytes 528384 | tf_op jit(solution)/shard_map/gather | solution.py:564
  9.6 0.1 broadcast_in_dim.21
  9.7 0.3 concatenate.6.refs_0_
  10.0 1.6 %collective-permute-start = (bf16[1040,128]{1,0:T(8,128)(2,1)S(1)}, bf16[1040,128]{1,0:T(8,128)(2,1)S(1)}, u32[]{:S(2)}, u32[]{:S(2)}) collective-permute-start(bf16[1040,128]{1,0:T(8,128)(2,1)S(1)} %concatenate.6.refs_0_), channel_id=1, source_target_pairs={{0,1},{1,2},{2,3},{3,0},{4,5},{5,6},{6,7},{7,4},{8,9},{9,10},{10,1... | collective-permute-start | bytes 798728 | tf_op jit(solution)/shard_map/ppermute | solution.py:33
  11.6 7.3 %gather_fusion.1 = bf16[1024,128]{1,0:T(8,128)(2,1)S(1)} fusion(bf16[32768,128]{1,0:T(8,128)(2,1)} %param.12, s32[1024]{0:T(1024)S(1)} %get-tuple-element.71), kind=kCustom, calls=%fused_computation.1 | custom fusion | bytes 528384 | tf_op jit(solution)/shard_map/gather | solution.py:564
  18.9 1.6 %collective-permute-start.4 = (bf16[1024,128]{1,0:T(8,128)(2,1)S(1)}, bf16[1024,128]{1,0:T(8,128)(2,1)}, u32[]{:S(2)}, u32[]{:S(2)}) collective-permute-start(bf16[1024,128]{1,0:T(8,128)(2,1)S(1)} %gather_fusion.1), channel_id=1, source_target_pairs={{0,1},{1,2},{2,3},{3,0},{4,5},{5,6},{6,7},{7,4},{8,9},{9,10},{10,1... | collective-permute-start | bytes 786440 | tf_op jit(solution)/shard_map/ppermute | solution.py:33
  20.6 2.2 %collective-permute-start.1 = (bf16[1040,128]{1,0:T(8,128)(2,1)S(1)}, bf16[1040,128]{1,0:T(8,128)(2,1)S(1)}, u32[]{:S(2)}, u32[]{:S(2)}) collective-permute-start(bf16[1040,128]{1,0:T(8,128)(2,1)S(1)} %concatenate.6.refs_0_), channel_id=1, source_target_pairs={{0,3},{1,0},{2,1},{3,2},{4,7},{5,4},{6,5},{7,6},{8,11},{9,8},{10,9... | collective-permute-start | bytes 798728 | tf_op jit(solution)/shard_map/ppermute | solution.py:33
  22.8 3.8 %collective-permute-start.5 = (bf16[1024,128]{1,0:T(8,128)(2,1)S(1)}, bf16[1024,128]{1,0:T(8,128)(2,1)}, u32[]{:S(2)}, u32[]{:S(2)}) collective-permute-start(bf16[1024,128]{1,0:T(8,128)(2,1)S(1)} %gather_fusion.1), channel_id=1, source_target_pairs={{0,3},{1,0},{2,1},{3,2},{4,7},{5,4},{6,5},{7,6},{8,11},{9,8},{10,9... | collective-permute-start | bytes 786440 | tf_op jit(solution)/shard_map/ppermute | solution.py:33
  26.6 3.5 %collective-permute-done.4.refs_2_ = bf16[1024,128]{1,0:T(8,128)(2,1)} collective-permute-done((bf16[1024,128]{1,0:T(8,128)(2,1)S(1)}, bf16[1024,128]{1,0:T(8,128)(2,1)}, u32[]{:S(2)}, u32[]{:S(2)}) %collective-permute-start.4) | collective-permute-done | bytes 262176 | tf_op jit(solution)/shard_map/ppermute | solution.py:33
  30.1 4.0 %collective-permute-start.6 = (bf16[1024,128]{1,0:T(8,128)(2,1)}, bf16[1024,128]{1,0:T(8,128)(2,1)}, u32[]{:S(2)}, u32[]{:S(2)}) collective-permute-start(bf16[1024,128]{1,0:T(8,128)(2,1)} %collective-permute-done.4.refs_2_), channel_id=1, source_target_pairs={{0,1},{1,2},{2,3},{3,0},{4,5},{5,6},{6,7},{7,4},{8,9},{9,10},{10,1... | collective-permute-start | bytes 786440 | tf_op jit(solution)/shard_map/ppermute | solution.py:33
  34.1 1.6 %copy-done = bf16[512,2048]{1,0:T(8,128)(2,1)S(1)} copy-done((bf16[512,2048]{1,0:T(8,128)(2,1)S(1)}, bf16[512,2048]{1,0:T(8,128)(2,1)}, u32[]{:S(2)}) %copy-start) | copy-done | bytes 2097176
  35.7 0.2 weights.1.refs_5_.refs_6_
  35.9 5.6 %collective-permute-done.2.refs_3_ = bf16[1040,128]{1,0:T(8,128)(2,1)S(1)} collective-permute-done((bf16[1040,128]{1,0:T(8,128)(2,1)S(1)}, bf16[1040,128]{1,0:T(8,128)(2,1)S(1)}, u32[]{:S(2)}, u32[]{:S(2)}) %collective-permute-start.2) | collective-permute-done | bytes 266272 | tf_op jit(solution)/shard_map/ppermute | solution.py:33
  41.5 1.6 %shard_map.91 = (bf16[1024,256]{1,0:T(8,128)(2,1)S(1)}, bf16[1040,256]{1,0:T(8,128)(2,1)S(1)}, bf16[1024,512]{1,0:T(8,128)(2,1)S(1)}, s32[4]{0:T(128)S(1)}) custom-call(s32[1]{0:T(128)} %bitcast.me.me_ref, bf16[1040,128]{1,0:T(8,128)(2,1)S(1)} %concatenate.6.refs_0_, bf16[1040,128]{1,0:T(8,128)(2,1)S(1)} %collective-permute-done.refs_1_, ...), custom_call_target="tpu_custom_call" | custom-call | flops 536870912 | bytes 2097152 | tf_op jit(solution)/shard_map/pallas_call | solution.py:581
  43.1 1.9 %collective-permute-start.9 = (bf16[1040,256]{1,0:T(8,128)(2,1)S(1)}, bf16[1040,256]{1,0:T(8,128)(2,1)S(1)}, u32[]{:S(2)}, u32[]{:S(2)}) collective-permute-start(bf16[1040,256]{1,0:T(8,128)(2,1)S(1)} %get-tuple-element.38.refs_1_.refs_2_), channel_id=1, source_target_pairs={{0,4},{4,8},{8,12},{12,16},{16,20},{20,24},{24,28},{1,5},{5,9},{9,... | collective-permute-start | bytes 1597448 | tf_op jit(solution)/shard_map/ppermute | solution.py:28
  45.0 3.6 %collective-permute-start.3 = (bf16[1040,256]{1,0:T(8,128)(2,1)S(1)}, bf16[1040,256]{1,0:T(8,128)(2,1)S(1)}, u32[]{:S(2)}, u32[]{:S(2)}) collective-permute-start(bf16[1040,256]{1,0:T(8,128)(2,1)S(1)} %get-tuple-element.38.refs_1_.refs_2_), channel_id=1, source_target_pairs={{4,0},{8,4},{12,8},{16,12},{20,16},{24,20},{28,24},{5,1},{9,5},{13... | collective-permute-start | bytes 1597448 | tf_op jit(solution)/shard_map/ppermute | solution.py:28
  48.7 2.7 %collective-permute-done.6.refs_4_ = bf16[1024,128]{1,0:T(8,128)(2,1)} collective-permute-done((bf16[1024,128]{1,0:T(8,128)(2,1)}, bf16[1024,128]{1,0:T(8,128)(2,1)}, u32[]{:S(2)}, u32[]{:S(2)}) %collective-permute-start.6) | collective-permute-done | bytes 262176 | tf_op jit(solution)/shard_map/ppermute | solution.py:33
  51.4 2.4 %shard_map.92 = (bf16[1024,256]{1,0:T(8,128)(2,1)S(1)}, bf16[1024,256]{1,0:T(8,128)(2,1)S(1)}, bf16[1024,512]{1,0:T(8,128)(2,1)S(1)}) custom-call(s32[1]{0:T(128)} %bitcast.me.me_ref, s32[4]{0:T(128)S(1)} %get-tuple-element.39.refs_0_.lives_ref, bf16[1024,128]{1,0:T(8,128)(2,1)S(1)} %gather_fusion.1, bf16[1024,128]{1,0:T(8,128)(2,1)} %collective-permute-done.4.refs_2_, ...), custom_call_target="tpu_custom_call" | custom-call | flops 536870912 | bytes 2097152 | tf_op jit(solution)/shard_map/pallas_call | solution.py:581
  53.8 1.9 %collective-permute-start.8 = (bf16[1024,256]{1,0:T(8,128)(2,1)S(1)}, bf16[1024,256]{1,0:T(8,128)(2,1)S(1)}, u32[]{:S(2)}, u32[]{:S(2)}) collective-permute-start(bf16[1024,256]{1,0:T(8,128)(2,1)S(1)} %get-tuple-element.40.refs_3_), channel_id=1, source_target_pairs={{0,4},{4,8},{8,12},{12,16},{16,20},{20,24},{24,28},{1,5},{5,9},{9,... | collective-permute-start | bytes 1572872 | tf_op jit(solution)/shard_map/ppermute | solution.py:28
  55.7 3.6 %collective-permute-start.7 = (bf16[1024,256]{1,0:T(8,128)(2,1)S(1)}, bf16[1024,256]{1,0:T(8,128)(2,1)S(1)}, u32[]{:S(2)}, u32[]{:S(2)}) collective-permute-start(bf16[1024,256]{1,0:T(8,128)(2,1)S(1)} %get-tuple-element.40.refs_3_), channel_id=1, source_target_pairs={{4,0},{8,4},{12,8},{16,12},{20,16},{24,20},{28,24},{5,1},{9,5},{13... | collective-permute-start | bytes 1572872 | tf_op jit(solution)/shard_map/ppermute | solution.py:28
  59.4 0.9 slots.1
  60.3 0.8 shard_map.98
  61.1 0.8 shard_map.95
  62.0 3.1 %own0.1 = (f32[1024,128]{1,0:T(8,128)S(1)}, bf16[1024,256]{1,0:T(8,128)(2,1)S(1)}) custom-call(s32[4]{0:T(128)S(1)} %get-tuple-element.39.refs_0_.lives_ref, bf16[1024,256]{1,0:T(8,128)(2,1)S(1)} %get-tuple-element.41.refs_0_, bf16[1040,256]{1,0:T(8,128)(2,1)S(1)} %get-tuple-element.38.refs_1_.refs_2_), custom_call_target="tpu_custom_call" | custom-call | flops 2147483648 | bytes 1048576 | tf_op jit(solution)/shard_map/own0/pallas_call | solution.py:591
  65.1 5.3 %shard_map.93.refs_4_ = f32[1024,128]{1,0:T(8,128)S(1)} custom-call(bf16[1040,256]{1,0:T(8,128)(2,1)S(1)} %collective-permute-done.9.refs_0_.refs_3_, bf16[1040,256]{1,0:T(8,128)(2,1)S(1)} %collective-permute-done.3.refs_1_.refs_0_, bf16[1024,256]{1,0:T(8,128)(2,1)S(1)} %get-tuple-element.42.refs_2_.refs_0_, ...), custom_call_target="tpu_custom_call", output_to_operand_aliasing={{}: (3, {})} | custom-call | flops 1610612736 | bytes 1048576 | tf_op jit(solution)/shard_map/pallas_call | solution.py:594
  70.4 8.3 %own1.1 = (f32[2048,128]{1,0:T(8,128)S(1)}, bf16[2048,256]{1,0:T(8,128)(2,1)S(1)}) custom-call(s32[4]{0:T(128)S(1)} %get-tuple-element.39.refs_0_.lives_ref, bf16[1024,256]{1,0:T(8,128)(2,1)S(1)} %get-tuple-element.42.refs_2_.refs_0_, bf16[1024,256]{1,0:T(8,128)(2,1)S(1)} %get-tuple-element.43.refs_1_, ...), custom_call_target="tpu_custom_call" | custom-call | flops 6442450944 | bytes 2097152 | tf_op jit(solution)/shard_map/own1/pallas_call | solution.py:595
  78.7 6.4 %shard_map.97 = (bf16[512,128]{1,0:T(8,128)(2,1)S(1)}, bf16[512,128]{1,0:T(8,128)(2,1)S(1)}, bf16[512,128]{1,0:T(8,128)(2,1)S(1)}, bf16[512,128]{1,0:T(8,128)(2,1)S(1)}) custom-call(bf16[1040,256]{1,0:T(8,128)(2,1)S(1)} %collective-permute-done.3.refs_1_.refs_0_, bf16[1024,256]{1,0:T(8,128)(2,1)S(1)} %collective-permute-done.7.refs_1_, ...), custom_call_target="tpu_custom_call" | custom-call | flops 3758096384 | bytes 1048576 | tf_op jit(solution)/shard_map/pallas_call | solution.py:600
  85.1 0.0 copy-start.3
  85.1 1.3 collective-permute-start.16
  86.4 2.5 %collective-permute-start.17 = (bf16[512,128]{1,0:T(8,128)(2,1)S(1)}, bf16[512,128]{1,0:T(8,128)(2,1)S(1)}, u32[]{:S(2)}, u32[]{:S(2)}) collective-permute-start(bf16[512,128]{1,0:T(8,128)(2,1)S(1)} %get-tuple-element.62), channel_id=1, source_target_pairs={{0,2},{1,3},{2,0},{3,1},{4,6},{5,7},{6,4},{7,5},{8,10},{9,11},{10,... | collective-permute-start | bytes 393224 | tf_op jit(solution)/shard_map/ppermute | solution.py:33
  88.9 2.8 %collective-permute-start.18 = (bf16[512,128]{1,0:T(8,128)(2,1)S(1)}, bf16[512,128]{1,0:T(8,128)(2,1)S(1)}, u32[]{:S(2)}, u32[]{:S(2)}) collective-permute-start(bf16[512,128]{1,0:T(8,128)(2,1)S(1)} %get-tuple-element.63), channel_id=1, source_target_pairs={{0,3},{1,0},{2,1},{3,2},{4,7},{5,4},{6,5},{7,6},{8,11},{9,8},{10,9... | collective-permute-start | bytes 393224 | tf_op jit(solution)/shard_map/ppermute | solution.py:33
  91.7 7.0 %shard_map.94 = (bf16[512,128]{1,0:T(8,128)(2,1)S(1)}, bf16[512,128]{1,0:T(8,128)(2,1)S(1)}, bf16[512,128]{1,0:T(8,128)(2,1)S(1)}, bf16[512,128]{1,0:T(8,128)(2,1)S(1)}) custom-call(bf16[1040,256]{1,0:T(8,128)(2,1)S(1)} %collective-permute-done.3.refs_1_.refs_0_, bf16[1024,256]{1,0:T(8,128)(2,1)S(1)} %collective-permute-done.7.refs_1_, ...), custom_call_target="tpu_custom_call" | custom-call | flops 3758096384 | bytes 1048576 | tf_op jit(solution)/shard_map/pallas_call | solution.py:600
  98.8 0.1 collective-permute-start.10
  98.8 0.6 collective-permute-start.11
  99.4 3.3 %collective-permute-start.12 = (bf16[512,128]{1,0:T(8,128)(2,1)S(1)}, bf16[512,128]{1,0:T(8,128)(2,1)S(1)}, u32[]{:S(2)}, u32[]{:S(2)}) collective-permute-start(bf16[512,128]{1,0:T(8,128)(2,1)S(1)} %get-tuple-element.51), channel_id=1, source_target_pairs={{0,3},{1,0},{2,1},{3,2},{4,7},{5,4},{6,5},{7,6},{8,11},{9,8},{10,9... | collective-permute-start | bytes 393224 | tf_op jit(solution)/shard_map/ppermute | solution.py:33
  102.7 4.6 %shard_map.99 = (bf16[256,512]{1,0:T(8,128)(2,1)S(1)}, bf16[256,512]{1,0:T(8,128)(2,1)S(1)}, bf16[256,512]{1,0:T(8,128)(2,1)S(1)}, bf16[256,512]{1,0:T(8,128)(2,1)S(1)}) custom-call(s32[1]{0:T(128)} %bitcast.me.me_ref, bf16[512,128]{1,0:T(8,128)(2,1)S(1)} %get-tuple-element.60.refs_0_, bf16[512,128]{1,0:T(8,128)(2,1)S(1)} %collective-permute-done.16.refs_1_, ...), custom_call_target="tpu_custom_call" | custom-call | flops 3221225472 | bytes 2097152 | tf_op jit(solution)/shard_map/pallas_call | solution.py:611
  107.3 2.5 %collective-permute-start.19 = (bf16[256,512]{1,0:T(8,128)(2,1)S(1)}, bf16[256,512]{1,0:T(8,128)(2,1)S(1)}, u32[]{:S(2)}, u32[]{:S(2)}) collective-permute-start(bf16[256,512]{1,0:T(8,128)(2,1)S(1)} %get-tuple-element.66), channel_id=1, source_target_pairs={{0,1},{3,2},{4,5},{7,6},{8,9},{11,10},{12,13},{15,14},{16,17},{19,... | collective-permute-start | bytes 786440 | tf_op jit(solution)/shard_map/ppermute | solution.py:615
  109.8 0.7 collective-permute-start.20
  110.5 4.0 %collective-permute-start.21 = (bf16[256,512]{1,0:T(8,128)(2,1)S(1)}, bf16[256,512]{1,0:T(8,128)(2,1)S(1)}, u32[]{:S(2)}, u32[]{:S(2)}) collective-permute-start(bf16[256,512]{1,0:T(8,128)(2,1)S(1)} %get-tuple-element.68), channel_id=1, source_target_pairs={{3,1},{0,2},{7,5},{4,6},{11,9},{8,10},{15,13},{12,14},{19,17},{16,... | collective-permute-start | bytes 786440 | tf_op jit(solution)/shard_map/ppermute | solution.py:615
  114.6 4.6 %shard_map.96 = (bf16[256,512]{1,0:T(8,128)(2,1)S(1)}, bf16[256,512]{1,0:T(8,128)(2,1)S(1)}, bf16[256,512]{1,0:T(8,128)(2,1)S(1)}, bf16[256,512]{1,0:T(8,128)(2,1)S(1)}) custom-call(s32[1]{0:T(128)} %bitcast.me.me_ref, bf16[512,128]{1,0:T(8,128)(2,1)S(1)} %get-tuple-element.48.refs_0_, bf16[512,128]{1,0:T(8,128)(2,1)S(1)} %collective-permute-done.10.refs_1_, ...), custom_call_target="tpu_custom_call" | custom-call | flops 3221225472 | bytes 2097152 | tf_op jit(solution)/shard_map/pallas_call | solution.py:611
  119.2 1.3 collective-permute-start.13
  120.5 1.3 collective-permute-start.14
  121.8 4.8 %collective-permute-start.15 = (bf16[256,512]{1,0:T(8,128)(2,1)S(1)}, bf16[256,512]{1,0:T(8,128)(2,1)S(1)}, u32[]{:S(2)}, u32[]{:S(2)}) collective-permute-start(bf16[256,512]{1,0:T(8,128)(2,1)S(1)} %get-tuple-element.58), channel_id=1, source_target_pairs={{3,0},{0,3},{7,4},{4,7},{11,8},{8,11},{15,12},{12,15},{19,16},{16,... | collective-permute-start | bytes 786440 | tf_op jit(solution)/shard_map/ppermute | solution.py:615
  126.7 11.8 %collective-permute-done.13.refs_0_ = bf16[256,512]{1,0:T(8,128)(2,1)S(1)} collective-permute-done((bf16[256,512]{1,0:T(8,128)(2,1)S(1)}, bf16[256,512]{1,0:T(8,128)(2,1)S(1)}, u32[]{:S(2)}, u32[]{:S(2)}) %collective-permute-start.13) | collective-permute-done | bytes 262176 | tf_op jit(solution)/shard_map/ppermute | solution.py:615
  138.5 1.6 %mix.1 = bf16[512,512]{1,0:T(8,128)(2,1)} custom-call(s32[1]{0:T(128)} %bitcast.me.me_ref, bf16[256,512]{1,0:T(8,128)(2,1)S(1)} %collective-permute-done.13.refs_0_, bf16[256,512]{1,0:T(8,128)(2,1)S(1)} %collective-permute-done.14.refs_1_, bf16[256,512]{1,0:T(8,128)(2,1)S(1)} %collective-permute-done.15.refs_2_, ...), custom_call_target="tpu_custom_call" | custom-call | flops 536870912 | bytes 2097152 | tf_op jit(solution)/shard_map/mix/pallas_call | solution.py:618
  (30 shorter events, 0.1 us)
Async XLA Ops:
  0.0 41.5 %copy-start.2 = (f32[3,512]{1,0:T(4,128)S(1)}, f32[3,512]{1,0:T(4,128)}, u32[]{:S(2)}) copy-start(f32[3,512]{1,0:T(4,128)} %refs_6_.3) | copy-start | bytes 18436
  2.1 58.1 %copy-start.1 = (bf16[512,2048]{1,0:T(8,128)(2,1)S(1)}, bf16[512,2048]{1,0:T(8,128)(2,1)}, u32[]{:S(2)}) copy-start(bf16[512,2048]{1,0:T(8,128)(2,1)} %refs_4_.5) | copy-start | bytes 6291460
  10.0 12.8 %collective-permute-start = (bf16[1040,128]{1,0:T(8,128)(2,1)S(1)}, bf16[1040,128]{1,0:T(8,128)(2,1)S(1)}, u32[]{:S(2)}, u32[]{:S(2)}) collective-permute-start(bf16[1040,128]{1,0:T(8,128)(2,1)S(1)} %concatenate.6.refs_0_), channel_id=1, source_target_pairs={{0,1},{1,2},{2,3},{3,0},{4,5},{5,6},{6,7},{7,4},{8,9},{9,10},{10,1... | collective-permute-start | bytes 798728 | tf_op jit(solution)/shard_map/ppermute | solution.py:33
  18.9 11.2 %collective-permute-start.4 = (bf16[1024,128]{1,0:T(8,128)(2,1)S(1)}, bf16[1024,128]{1,0:T(8,128)(2,1)}, u32[]{:S(2)}, u32[]{:S(2)}) collective-permute-start(bf16[1024,128]{1,0:T(8,128)(2,1)S(1)} %gather_fusion.1), channel_id=1, source_target_pairs={{0,1},{1,2},{2,3},{3,0},{4,5},{5,6},{6,7},{7,4},{8,9},{9,10},{10,1... | collective-permute-start | bytes 786440 | tf_op jit(solution)/shard_map/ppermute | solution.py:33
  20.6 15.3 %collective-permute-start.1 = (bf16[1040,128]{1,0:T(8,128)(2,1)S(1)}, bf16[1040,128]{1,0:T(8,128)(2,1)S(1)}, u32[]{:S(2)}, u32[]{:S(2)}) collective-permute-start(bf16[1040,128]{1,0:T(8,128)(2,1)S(1)} %concatenate.6.refs_0_), channel_id=1, source_target_pairs={{0,3},{1,0},{2,1},{3,2},{4,7},{5,4},{6,5},{7,6},{8,11},{9,8},{10,9... | collective-permute-start | bytes 798728 | tf_op jit(solution)/shard_map/ppermute | solution.py:33
  22.8 18.7 %collective-permute-start.2 = (bf16[1040,128]{1,0:T(8,128)(2,1)S(1)}, bf16[1040,128]{1,0:T(8,128)(2,1)S(1)}, u32[]{:S(2)}, u32[]{:S(2)}) collective-permute-start(bf16[1040,128]{1,0:T(8,128)(2,1)S(1)} %collective-permute-done.refs_1_), channel_id=1, source_target_pairs={{0,1},{1,2},{2,3},{3,0},{4,5},{5,6},{6,7},{7,4},{8,9},{9,10},{10,1... | collective-permute-start | bytes 798728 | tf_op jit(solution)/shard_map/ppermute | solution.py:33
  22.8 25.8 %collective-permute-start.5 = (bf16[1024,128]{1,0:T(8,128)(2,1)S(1)}, bf16[1024,128]{1,0:T(8,128)(2,1)}, u32[]{:S(2)}, u32[]{:S(2)}) collective-permute-start(bf16[1024,128]{1,0:T(8,128)(2,1)S(1)} %gather_fusion.1), channel_id=1, source_target_pairs={{0,3},{1,0},{2,1},{3,2},{4,7},{5,4},{6,5},{7,6},{8,11},{9,8},{10,9... | collective-permute-start | bytes 786440 | tf_op jit(solution)/shard_map/ppermute | solution.py:33
  30.1 21.3 %collective-permute-start.6 = (bf16[1024,128]{1,0:T(8,128)(2,1)}, bf16[1024,128]{1,0:T(8,128)(2,1)}, u32[]{:S(2)}, u32[]{:S(2)}) collective-permute-start(bf16[1024,128]{1,0:T(8,128)(2,1)} %collective-permute-done.4.refs_2_), channel_id=1, source_target_pairs={{0,1},{1,2},{2,3},{3,0},{4,5},{5,6},{6,7},{7,4},{8,9},{9,10},{10,1... | collective-permute-start | bytes 786440 | tf_op jit(solution)/shard_map/ppermute | solution.py:33
  34.1 1.6 %copy-start = (bf16[512,2048]{1,0:T(8,128)(2,1)S(1)}, bf16[512,2048]{1,0:T(8,128)(2,1)}, u32[]{:S(2)}) copy-start(bf16[512,2048]{1,0:T(8,128)(2,1)} %refs_4_.5) | copy-start | bytes 6291460
  43.1 22.0 %collective-permute-start.9 = (bf16[1040,256]{1,0:T(8,128)(2,1)S(1)}, bf16[1040,256]{1,0:T(8,128)(2,1)S(1)}, u32[]{:S(2)}, u32[]{:S(2)}) collective-permute-start(bf16[1040,256]{1,0:T(8,128)(2,1)S(1)} %get-tuple-element.38.refs_1_.refs_2_), channel_id=1, source_target_pairs={{0,4},{4,8},{8,12},{12,16},{16,20},{20,24},{24,28},{1,5},{5,9},{9,... | collective-permute-start | bytes 1597448 | tf_op jit(solution)/shard_map/ppermute | solution.py:28
  45.0 20.1 %collective-permute-start.3 = (bf16[1040,256]{1,0:T(8,128)(2,1)S(1)}, bf16[1040,256]{1,0:T(8,128)(2,1)S(1)}, u32[]{:S(2)}, u32[]{:S(2)}) collective-permute-start(bf16[1040,256]{1,0:T(8,128)(2,1)S(1)} %get-tuple-element.38.refs_1_.refs_2_), channel_id=1, source_target_pairs={{4,0},{8,4},{12,8},{16,12},{20,16},{24,20},{28,24},{5,1},{9,5},{13... | collective-permute-start | bytes 1597448 | tf_op jit(solution)/shard_map/ppermute | solution.py:28
  53.8 24.9 %collective-permute-start.8 = (bf16[1024,256]{1,0:T(8,128)(2,1)S(1)}, bf16[1024,256]{1,0:T(8,128)(2,1)S(1)}, u32[]{:S(2)}, u32[]{:S(2)}) collective-permute-start(bf16[1024,256]{1,0:T(8,128)(2,1)S(1)} %get-tuple-element.40.refs_3_), channel_id=1, source_target_pairs={{0,4},{4,8},{8,12},{12,16},{16,20},{20,24},{24,28},{1,5},{5,9},{9,... | collective-permute-start | bytes 1572872 | tf_op jit(solution)/shard_map/ppermute | solution.py:28
  55.7 23.0 %collective-permute-start.7 = (bf16[1024,256]{1,0:T(8,128)(2,1)S(1)}, bf16[1024,256]{1,0:T(8,128)(2,1)S(1)}, u32[]{:S(2)}, u32[]{:S(2)}) collective-permute-start(bf16[1024,256]{1,0:T(8,128)(2,1)S(1)} %get-tuple-element.40.refs_3_), channel_id=1, source_target_pairs={{4,0},{8,4},{12,8},{16,12},{20,16},{24,20},{28,24},{5,1},{9,5},{13... | collective-permute-start | bytes 1572872 | tf_op jit(solution)/shard_map/ppermute | solution.py:28
  85.1 17.6 %copy-start.3 = (bf16[1,512,4096]{2,1,0:T(8,128)(2,1)S(1)}, bf16[1,512,4096]{2,1,0:T(8,128)(2,1)}, u32[]{:S(2)}) copy-start(bf16[1,512,4096]{2,1,0:T(8,128)(2,1)} %refs_8_.3) | copy-start | bytes 12582916
  85.1 17.5 %copy-start.4 = (bf16[1,2048,512]{2,1,0:T(8,128)(2,1)S(1)}, bf16[1,2048,512]{2,1,0:T(8,128)(2,1)}, u32[]{:S(2)}) copy-start(bf16[1,2048,512]{2,1,0:T(8,128)(2,1)} %refs_9_.3) | copy-start | bytes 6291460
  85.1 17.5 %copy-start.5 = (bf16[512,512]{1,0:T(8,128)(2,1)S(1)}, bf16[512,512]{1,0:T(8,128)(2,1)}, u32[]{:S(2)}) copy-start(bf16[512,512]{1,0:T(8,128)(2,1)} %refs_7_.3) | copy-start | bytes 1572868
  85.1 14.2 %collective-permute-start.16 = (bf16[512,128]{1,0:T(8,128)(2,1)S(1)}, bf16[512,128]{1,0:T(8,128)(2,1)S(1)}, u32[]{:S(2)}, u32[]{:S(2)}) collective-permute-start(bf16[512,128]{1,0:T(8,128)(2,1)S(1)} %get-tuple-element.61), channel_id=1, source_target_pairs={{0,1},{1,2},{2,3},{3,0},{4,5},{5,6},{6,7},{7,4},{8,9},{9,10},{10,1... | collective-permute-start | bytes 393224 | tf_op jit(solution)/shard_map/ppermute | solution.py:33
  86.4 16.3 %collective-permute-start.17 = (bf16[512,128]{1,0:T(8,128)(2,1)S(1)}, bf16[512,128]{1,0:T(8,128)(2,1)S(1)}, u32[]{:S(2)}, u32[]{:S(2)}) collective-permute-start(bf16[512,128]{1,0:T(8,128)(2,1)S(1)} %get-tuple-element.62), channel_id=1, source_target_pairs={{0,2},{1,3},{2,0},{3,1},{4,6},{5,7},{6,4},{7,5},{8,10},{9,11},{10,... | collective-permute-start | bytes 393224 | tf_op jit(solution)/shard_map/ppermute | solution.py:33
  88.9 13.8 %collective-permute-start.18 = (bf16[512,128]{1,0:T(8,128)(2,1)S(1)}, bf16[512,128]{1,0:T(8,128)(2,1)S(1)}, u32[]{:S(2)}, u32[]{:S(2)}) collective-permute-start(bf16[512,128]{1,0:T(8,128)(2,1)S(1)} %get-tuple-element.63), channel_id=1, source_target_pairs={{0,3},{1,0},{2,1},{3,2},{4,7},{5,4},{6,5},{7,6},{8,11},{9,8},{10,9... | collective-permute-start | bytes 393224 | tf_op jit(solution)/shard_map/ppermute | solution.py:33
  98.8 11.8 %collective-permute-start.10 = (bf16[512,128]{1,0:T(8,128)(2,1)S(1)}, bf16[512,128]{1,0:T(8,128)(2,1)S(1)}, u32[]{:S(2)}, u32[]{:S(2)}) collective-permute-start(bf16[512,128]{1,0:T(8,128)(2,1)S(1)} %get-tuple-element.49), channel_id=1, source_target_pairs={{0,1},{1,2},{2,3},{3,0},{4,5},{5,6},{6,7},{7,4},{8,9},{9,10},{10,1... | collective-permute-start | bytes 393224 | tf_op jit(solution)/shard_map/ppermute | solution.py:33
  98.8 15.7 %collective-permute-start.11 = (bf16[512,128]{1,0:T(8,128)(2,1)S(1)}, bf16[512,128]{1,0:T(8,128)(2,1)S(1)}, u32[]{:S(2)}, u32[]{:S(2)}) collective-permute-start(bf16[512,128]{1,0:T(8,128)(2,1)S(1)} %get-tuple-element.50), channel_id=1, source_target_pairs={{0,2},{1,3},{2,0},{3,1},{4,6},{5,7},{6,4},{7,5},{8,10},{9,11},{10,... | collective-permute-start | bytes 393224 | tf_op jit(solution)/shard_map/ppermute | solution.py:33
  99.4 15.2 %collective-permute-start.12 = (bf16[512,128]{1,0:T(8,128)(2,1)S(1)}, bf16[512,128]{1,0:T(8,128)(2,1)S(1)}, u32[]{:S(2)}, u32[]{:S(2)}) collective-permute-start(bf16[512,128]{1,0:T(8,128)(2,1)S(1)} %get-tuple-element.51), channel_id=1, source_target_pairs={{0,3},{1,0},{2,1},{3,2},{4,7},{5,4},{6,5},{7,6},{8,11},{9,8},{10,9... | collective-permute-start | bytes 393224 | tf_op jit(solution)/shard_map/ppermute | solution.py:33
  107.3 14.5 %collective-permute-start.19 = (bf16[256,512]{1,0:T(8,128)(2,1)S(1)}, bf16[256,512]{1,0:T(8,128)(2,1)S(1)}, u32[]{:S(2)}, u32[]{:S(2)}) collective-permute-start(bf16[256,512]{1,0:T(8,128)(2,1)S(1)} %get-tuple-element.66), channel_id=1, source_target_pairs={{0,1},{3,2},{4,5},{7,6},{8,9},{11,10},{12,13},{15,14},{16,17},{19,... | collective-permute-start | bytes 786440 | tf_op jit(solution)/shard_map/ppermute | solution.py:615
  109.8 16.8 %collective-permute-start.20 = (bf16[256,512]{1,0:T(8,128)(2,1)S(1)}, bf16[256,512]{1,0:T(8,128)(2,1)S(1)}, u32[]{:S(2)}, u32[]{:S(2)}) collective-permute-start(bf16[256,512]{1,0:T(8,128)(2,1)S(1)} %get-tuple-element.67), channel_id=1, source_target_pairs={{2,1},{1,2},{6,5},{5,6},{10,9},{9,10},{14,13},{13,14},{18,17},{17,... | collective-permute-start | bytes 786440 | tf_op jit(solution)/shard_map/ppermute | solution.py:615
  110.5 16.1 %collective-permute-start.21 = (bf16[256,512]{1,0:T(8,128)(2,1)S(1)}, bf16[256,512]{1,0:T(8,128)(2,1)S(1)}, u32[]{:S(2)}, u32[]{:S(2)}) collective-permute-start(bf16[256,512]{1,0:T(8,128)(2,1)S(1)} %get-tuple-element.68), channel_id=1, source_target_pairs={{3,1},{0,2},{7,5},{4,6},{11,9},{8,10},{15,13},{12,14},{19,17},{16,... | collective-permute-start | bytes 786440 | tf_op jit(solution)/shard_map/ppermute | solution.py:615
  119.2 19.3 %collective-permute-start.13 = (bf16[256,512]{1,0:T(8,128)(2,1)S(1)}, bf16[256,512]{1,0:T(8,128)(2,1)S(1)}, u32[]{:S(2)}, u32[]{:S(2)}) collective-permute-start(bf16[256,512]{1,0:T(8,128)(2,1)S(1)} %get-tuple-element.56), channel_id=1, source_target_pairs={{1,0},{2,3},{5,4},{6,7},{9,8},{10,11},{13,12},{14,15},{17,16},{18,... | collective-permute-start | bytes 786440 | tf_op jit(solution)/shard_map/ppermute | solution.py:615
  120.5 18.0 %collective-permute-start.14 = (bf16[256,512]{1,0:T(8,128)(2,1)S(1)}, bf16[256,512]{1,0:T(8,128)(2,1)S(1)}, u32[]{:S(2)}, u32[]{:S(2)}) collective-permute-start(bf16[256,512]{1,0:T(8,128)(2,1)S(1)} %get-tuple-element.57), channel_id=1, source_target_pairs={{2,0},{1,3},{6,4},{5,7},{10,8},{9,11},{14,12},{13,15},{18,16},{17,... | collective-permute-start | bytes 786440 | tf_op jit(solution)/shard_map/ppermute | solution.py:615
  121.8 16.7 %collective-permute-start.15 = (bf16[256,512]{1,0:T(8,128)(2,1)S(1)}, bf16[256,512]{1,0:T(8,128)(2,1)S(1)}, u32[]{:S(2)}, u32[]{:S(2)}) collective-permute-start(bf16[256,512]{1,0:T(8,128)(2,1)S(1)} %get-tuple-element.58), channel_id=1, source_target_pairs={{3,0},{0,3},{7,4},{4,7},{11,8},{8,11},{15,12},{12,15},{19,16},{16,... | collective-permute-start | bytes 786440 | tf_op jit(solution)/shard_map/ppermute | solution.py:615

commit v3 on v2

--- a/solution.py
+++ b/solution.py
@@ -220,27 +220,33 @@
         acc[pl.ds(done, total - done), :] = jnp.zeros((total - done, width), F32)
         for (low, high), ref in zip(parts, queries):
             q_all[pl.ds(low * block_rows, (high - low) * block_rows), :] = ref[...]
-        for k in range(blocks):
-            home = next(spans(k, k + 1, chunks))[0]
-            start = 0 if opening or k >= first_end else first_end
-            while start < blocks:
-                past = min(start + 2, blocks)
+        span = 2
+        for home, (low, high) in enumerate(chunks[: len(keys)]):
+            start = 0 if opening or low >= first_end else first_end
+            strides = (blocks - start) // span
+
+            def step(job, carry):
+                k = low + lax.div(job, strides)
+                at = (start + lax.rem(job, strides) * span) * block_rows
+                at = pl.multiple_of(at, block_rows)
                 pair(
                     q_all,
-                    start * block_rows,
-                    start * block_rows,
+                    at,
+                    at,
                     keys[home],
-                    (k - chunks[home][0]) * block_rows,
+                    pl.multiple_of((k - low) * block_rows, block_rows),
                     k * block_rows,
                     acc,
-                    start * block_rows,
-                    (past - start) * block_rows,
+                    at,
+                    span * block_rows,
                     None,
                     lives_ref[k],
                     block_rows,
                     width,
                 )
-                start = past
+                return carry
+
+            lax.fori_loop(0, (high - low) * strides, step, 0)
 
     inputs = len(parts) + (len(chunks) - 1 if opening else len(chunks) + 1)
     pairs = first_end**2 if opening else group**2 - first_end**2
@@ -365,7 +371,7 @@
     )
 
 
-def make_slots(group, head_rows, block_rows, capacity):
+def make_slots(group, tail_at, block_rows, capacity):
     lanes = 128
     strips = block_rows // lanes
 
@@ -379,21 +385,24 @@
         earlier = jnp.where(earlier, 1.0, 0.0).astype(BF16)
         position = lax.broadcasted_iota(I32, (1, block_rows), 1)
         expert = lax.broadcasted_iota(I32, (8, block_rows), 0)
-        for piece, offset in zip(pieces, (0, group - 1, 1, 2)):
-            block = lax.rem(me + offset, group)
-            code = piece[pl.ds(head_rows, TAIL), :].astype(F32)
+        onehots, alives = [], []
+        order = [lax.rem(me + offset, group) for offset in (0, group - 1, 1, 2)]
+        for piece, block in zip(pieces, order):
+            code = piece[pl.ds(tail_at, TAIL), :].astype(F32)
             domain = jnp.concatenate([code[r : r + 1, :] for r in range(strips)], axis=1)
             turn = domain.astype(I32) - me
             turn = jnp.where(turn < 0, turn + group, turn)
-            alive = position < lives_ref[block]
-            onehot = jnp.where((expert == turn) & alive, 1.0, 0.0)
-            rank = jnp.dot(onehot.astype(BF16), earlier, preferred_element_type=F32)
-            slot = jnp.sum(
-                onehot * (rank + (expert * capacity).astype(F32)), axis=0, keepdims=True
-            )
-            slot = jnp.where(alive, slot, -1.0)
+            alives.append(position < lives_ref[block])
+            onehots.append(jnp.where((expert == turn) & alives[-1], 1.0, 0.0))
+        ranks = jnp.dot(
+            jnp.concatenate(onehots).astype(BF16), earlier, preferred_element_type=F32
+        )
+        for n, block in enumerate(order):
+            rank = ranks[8 * n : 8 * n + 8] + (expert * capacity).astype(F32)
+            slot = jnp.sum(onehots[n] * rank, axis=0, keepdims=True)
+            slot = jnp.where(alives[n], slot, -1.0)
             slots[pl.ds(block, 1), :] = slot.astype(I32)
-            if offset == 0:
+            if n == 0:
                 slot_col[...] = jnp.transpose(jnp.broadcast_to(slot, (lanes, block_rows))).astype(
                     I32
                 )
@@ -534,7 +543,7 @@
 BATCHES = ((0, 3), (1, 2))
 HOMEWARD = (
     (((1, 0), (2, 3)), ((2, 0), (1, 3)), ((3, 0), (0, 3))),
-    (((0, 1), (3, 2)), ((2, 1), (1, 2)), ((3, 1), (0, 2))),
+    (((3, 1), (0, 2)), ((0, 1), (3, 2)), ((2, 1), (1, 2))),
 )
 
 
@@ -552,19 +561,17 @@
     chunks = list(zip([0, *ends[:-1]], ends))
 
     high = lax.div(live_counts[0], TAIL)
-    count_code = jnp.stack((high, live_counts[0] - high * TAIL))
-    code = jnp.concatenate(
-        (
-            domains.reshape(rows // width, width),
-            jnp.zeros((TAIL - 2 - rows // width, width), I32),
-            jnp.broadcast_to(count_code[:, None], (2, width)),
-        )
+    tail = jnp.arange(TAIL, dtype=I32) < TAIL - 1
+    tail = jnp.where(tail, high, live_counts[0] - high * TAIL).astype(BF16)
+    count_code = jnp.broadcast_to(tail[:, None], (TAIL, width))
+    domain_code = jnp.pad(
+        domains.reshape(rows // width, width), ((0, TAIL - rows // width), (0, 0))
     ).astype(BF16)
     cut = chunks[0][1] * rows
     fetch = lambda ids: table.at[ids].get(mode="promise_in_bounds", wrap_negative_indices=False)
-    opening = jnp.concatenate((fetch(item_ids[:cut]), code))
+    opening = jnp.concatenate((fetch(item_ids[:cut]), count_code))
     rest = fetch(item_ids[cut:])
-    mine = [opening] + [rest[a * rows - cut : b * rows - cut] for a, b in chunks[1:]]
+    mine = [opening, jnp.concatenate((rest, domain_code))]
     low, high, far = [], [], []
     for c, piece in enumerate(mine):
         low.append(rotated(piece, "emb", 1))
@@ -581,7 +588,6 @@
         q, kv, emb, *more = project(me, *known, *pieces, norm_gains, weights)
         if c == 0:
             lives = more[0]
-            slots, slot_col = make_slots(group, cut, rows, capacity)(me, lives, *pieces)
         queries.append(q)
         own.append(kv)
         embedded.append(emb)
@@ -594,6 +600,9 @@
         acc = make_near(c, chunks, rows, width)(before[c], after[c], *heads, q_all, acc)
     acc, q_all = make_own(chunks, False, rows, width)(lives, q_all, queries[-1], *own, acc)
 
+    slots, slot_col = make_slots(group, mine[1].shape[0] - TAIL, rows, capacity)(
+        me, lives, mine[1], low[1], high[1], far[1]
+    )
     sent = []
     for batch in BATCHES:
         last = make_last(batch, chunks, rows, width, capacity)

time: 141 us -> 146 us (1.035); the launches traced: 140 us -> 144 us
  starting transfers between devices: 49.4 us -> 53.9 us
    ppermute x6, starting transfers between devices: 14.6 us -> 17.9 us  [by_heads(): finished.append(lax.ppermute(made[j], 'emb', pairs))]
  transfers between devices with their start and end apart: 22 -> 22, of which waited for: 4 -> 4; matrix products, arithmetic and copies ran while one was open for 5% -> 6% of each run, Pallas kernels for 28% -> 28%
where the time goes in v3:
time: 146 us; the launch traced here: 144 us
  starting transfers between devices  53.9 us (37%)
  Pallas kernels  47.8 us (33%)
  waiting for transfers between devices  22.7 us (16%)
  local copies, waits for them, and re-layouts  16.4 us (11%)
  other arithmetic  1.62 us (1%)
    ppermute x12, starting transfers between devices, rotated(): lax.ppermute(value, axis, [(source, (source + steps) % count) for source...  24.9 us
    ppermute x6, starting transfers between devices, by_heads(): finished.append(lax.ppermute(made[j], 'emb', pairs))  17.9 us
    gather x2, local copies, waits for them, and re-layouts, by_heads(): table.at[ids].get(mode='promise_in_bounds', wrap_negative_indices=False)  14.8 us
    pallas_call x2, Pallas kernels, by_heads(): shares = last(*after, before[-1], before[0], q_all, acc, slots)  13.2 us
    ppermute x6, waiting for transfers between devices, by_heads(): finished.append(lax.ppermute(made[j], 'emb', pairs))  11.7 us
    ppermute x4, starting transfers between devices, shifted(): lax.ppermute(value, axis, [(source, source + steps) for source in range(f...  11.1 us
    ppermute x12, waiting for transfers between devices, rotated(): lax.ppermute(value, axis, [(source, (source + steps) % count) for source...  11 us
    pallas_call x2, Pallas kernels, by_heads(): serve(me, *sent[n], emb, gating, norm_gains, proj_out, expert_in, expert_...  9.28 us
  transfers between devices with their start and end apart: 22, of which 4 were waited for; matrix products, arithmetic and copies ran while one was open for 6% of the time, Pallas kernels for 28%

profile of v3, /device:TPU:2, one launch (start us, length us, event | category | flops | bytes accessed | tf_op | source)
XLA Modules:
  0.0 143.6 jit_solution(8455910741874132664)
XLA Ops:
  0.7 0.7 slice_clamp_fusion
  1.4 7.5 %gather_fusion = bf16[1024,128]{1,0:T(8,128)(2,1)S(1)} fusion(bf16[32768,128]{1,0:T(8,128)(2,1)} %param.12, s32[1024]{0:T(1024)S(1)} %get-tuple-element.72), kind=kCustom, calls=%fused_computation | custom fusion | bytes 528384 | tf_op jit(solution)/shard_map/gather | solution.py:571
  8.9 0.2 pad_maximum_fusion.refs_0_
  9.1 1.6 %collective-permute-start = (bf16[1040,128]{1,0:T(8,128)(2,1)S(1)}, bf16[1040,128]{1,0:T(8,128)(2,1)}, u32[]{:S(2)}, u32[]{:S(2)}) collective-permute-start(bf16[1040,128]{1,0:T(8,128)(2,1)S(1)} %pad_maximum_fusion.refs_0_), channel_id=1, source_target_pairs={{0,1},{1,2},{2,3},{3,0},{4,5},{5,6},{6,7},{7,4},{8,9},{9,10},{10,1... | collective-permute-start | bytes 798728 | tf_op jit(solution)/shard_map/ppermute | solution.py:33
  10.7 0.7 convert_bitcast_fusion
  11.4 7.3 %gather_fusion.1 = bf16[1024,128]{1,0:T(8,128)(2,1)S(1)} fusion(bf16[32768,128]{1,0:T(8,128)(2,1)} %param.12, s32[1024]{0:T(1024)S(1)} %get-tuple-element.71), kind=kCustom, calls=%fused_computation.1 | custom fusion | bytes 528384 | tf_op jit(solution)/shard_map/gather | solution.py:571
  18.8 1.6 %collective-permute-start.4 = (bf16[1040,128]{1,0:T(8,128)(2,1)S(1)}, bf16[1040,128]{1,0:T(8,128)(2,1)S(1)}, u32[]{:S(2)}, u32[]{:S(2)}) collective-permute-start(bf16[1040,128]{1,0:T(8,128)(2,1)S(1)} %fusion.1.refs_1_.refs_0_), channel_id=1, source_target_pairs={{0,1},{1,2},{2,3},{3,0},{4,5},{5,6},{6,7},{7,4},{8,9},{9,10},{10,1... | collective-permute-start | bytes 798728 | tf_op jit(solution)/shard_map/ppermute | solution.py:33
  20.4 2.2 %collective-permute-start.1 = (bf16[1040,128]{1,0:T(8,128)(2,1)S(1)}, bf16[1040,128]{1,0:T(8,128)(2,1)}, u32[]{:S(2)}, u32[]{:S(2)}) collective-permute-start(bf16[1040,128]{1,0:T(8,128)(2,1)S(1)} %pad_maximum_fusion.refs_0_), channel_id=1, source_target_pairs={{0,3},{1,0},{2,1},{3,2},{4,7},{5,4},{6,5},{7,6},{8,11},{9,8},{10,9... | collective-permute-start | bytes 798728 | tf_op jit(solution)/shard_map/ppermute | solution.py:33
  22.7 3.8 %collective-permute-start.5 = (bf16[1040,128]{1,0:T(8,128)(2,1)S(1)}, bf16[1040,128]{1,0:T(8,128)(2,1)S(1)}, u32[]{:S(2)}, u32[]{:S(2)}) collective-permute-start(bf16[1040,128]{1,0:T(8,128)(2,1)S(1)} %fusion.1.refs_1_.refs_0_), channel_id=1, source_target_pairs={{0,3},{1,0},{2,1},{3,2},{4,7},{5,4},{6,5},{7,6},{8,11},{9,8},{10,9... | collective-permute-start | bytes 798728 | tf_op jit(solution)/shard_map/ppermute | solution.py:33
  26.5 3.5 %collective-permute-done.4.refs_2_.refs_1_ = bf16[1040,128]{1,0:T(8,128)(2,1)S(1)} collective-permute-done((bf16[1040,128]{1,0:T(8,128)(2,1)S(1)}, bf16[1040,128]{1,0:T(8,128)(2,1)S(1)}, u32[]{:S(2)}, u32[]{:S(2)}) %collective-permute-start.4) | collective-permute-done | bytes 266272 | tf_op jit(solution)/shard_map/ppermute | solution.py:33
  30.0 4.1 %collective-permute-start.6 = (bf16[1040,128]{1,0:T(8,128)(2,1)S(1)}, bf16[1040,128]{1,0:T(8,128)(2,1)S(1)}, u32[]{:S(2)}, u32[]{:S(2)}) collective-permute-start(bf16[1040,128]{1,0:T(8,128)(2,1)S(1)} %collective-permute-done.4.refs_2_.refs_1_), channel_id=1, source_target_pairs={{0,1},{1,2},{2,3},{3,0},{4,5},{5,6},{6,7},{7,4},{8,9},{9,10},{10,1... | collective-permute-start | bytes 798728 | tf_op jit(solution)/shard_map/ppermute | solution.py:33
  34.1 1.6 %copy-done = bf16[512,2048]{1,0:T(8,128)(2,1)S(1)} copy-done((bf16[512,2048]{1,0:T(8,128)(2,1)S(1)}, bf16[512,2048]{1,0:T(8,128)(2,1)}, u32[]{:S(2)}) %copy-start) | copy-done | bytes 2097176
  35.7 0.2 weights.1.refs_5_.refs_6_
  35.8 0.0 collective-permute-done.1.refs_2_
  35.8 5.7 %collective-permute-done.2.refs_3_ = bf16[1040,128]{1,0:T(8,128)(2,1)} collective-permute-done((bf16[1040,128]{1,0:T(8,128)(2,1)}, bf16[1040,128]{1,0:T(8,128)(2,1)}, u32[]{:S(2)}, u32[]{:S(2)}) %collective-permute-start.2) | collective-permute-done | bytes 266272 | tf_op jit(solution)/shard_map/ppermute | solution.py:33
  41.5 2.5 %shard_map.91 = (bf16[1024,256]{1,0:T(8,128)(2,1)S(1)}, bf16[1040,256]{1,0:T(8,128)(2,1)S(1)}, bf16[1024,512]{1,0:T(8,128)(2,1)S(1)}, s32[4]{0:T(128)S(1)}) custom-call(s32[1]{0:T(128)} %bitcast.me.me_ref, bf16[1040,128]{1,0:T(8,128)(2,1)S(1)} %pad_maximum_fusion.refs_0_, bf16[1040,128]{1,0:T(8,128)(2,1)} %collective-permute-done.refs_1_, ...), custom_call_target="tpu_custom_call" | custom-call | flops 536870912 | bytes 2097152 | tf_op jit(solution)/shard_map/pallas_call | solution.py:588
  44.1 1.9 %collective-permute-start.9 = (bf16[1040,256]{1,0:T(8,128)(2,1)S(1)}, bf16[1040,256]{1,0:T(8,128)(2,1)S(1)}, u32[]{:S(2)}, u32[]{:S(2)}) collective-permute-start(bf16[1040,256]{1,0:T(8,128)(2,1)S(1)} %get-tuple-element.38.refs_1_.refs_2_), channel_id=1, source_target_pairs={{0,4},{4,8},{8,12},{12,16},{16,20},{20,24},{24,28},{1,5},{5,9},{9,... | collective-permute-start | bytes 1597448 | tf_op jit(solution)/shard_map/ppermute | solution.py:28
  46.0 3.6 %collective-permute-start.3 = (bf16[1040,256]{1,0:T(8,128)(2,1)S(1)}, bf16[1040,256]{1,0:T(8,128)(2,1)S(1)}, u32[]{:S(2)}, u32[]{:S(2)}) collective-permute-start(bf16[1040,256]{1,0:T(8,128)(2,1)S(1)} %get-tuple-element.38.refs_1_.refs_2_), channel_id=1, source_target_pairs={{4,0},{8,4},{12,8},{16,12},{20,16},{24,20},{28,24},{5,1},{9,5},{13... | collective-permute-start | bytes 1597448 | tf_op jit(solution)/shard_map/ppermute | solution.py:28
  49.7 1.8 %collective-permute-done.6.refs_4_.refs_3_ = bf16[1040,128]{1,0:T(8,128)(2,1)S(1)} collective-permute-done((bf16[1040,128]{1,0:T(8,128)(2,1)S(1)}, bf16[1040,128]{1,0:T(8,128)(2,1)S(1)}, u32[]{:S(2)}, u32[]{:S(2)}) %collective-permute-start.6) | collective-permute-done | bytes 266272 | tf_op jit(solution)/shard_map/ppermute | solution.py:33
  51.4 1.8 %shard_map.92 = (bf16[1024,256]{1,0:T(8,128)(2,1)S(1)}, bf16[1024,256]{1,0:T(8,128)(2,1)S(1)}, bf16[1024,512]{1,0:T(8,128)(2,1)S(1)}) custom-call(s32[1]{0:T(128)} %bitcast.me.me_ref, s32[4]{0:T(128)S(1)} %get-tuple-element.39.refs_0_.lives_ref, bf16[1040,128]{1,0:T(8,128)(2,1)S(1)} %fusion.1.refs_1_.refs_0_, ...), custom_call_target="tpu_custom_call" | custom-call | flops 536870912 | bytes 2097152 | tf_op jit(solution)/shard_map/pallas_call | solution.py:588
  53.2 1.9 %collective-permute-start.8 = (bf16[1024,256]{1,0:T(8,128)(2,1)S(1)}, bf16[1024,256]{1,0:T(8,128)(2,1)S(1)}, u32[]{:S(2)}, u32[]{:S(2)}) collective-permute-start(bf16[1024,256]{1,0:T(8,128)(2,1)S(1)} %get-tuple-element.40.refs_3_), channel_id=1, source_target_pairs={{0,4},{4,8},{8,12},{12,16},{16,20},{20,24},{24,28},{1,5},{5,9},{9,... | collective-permute-start | bytes 1572872 | tf_op jit(solution)/shard_map/ppermute | solution.py:28
  55.2 3.6 %collective-permute-start.7 = (bf16[1024,256]{1,0:T(8,128)(2,1)S(1)}, bf16[1024,256]{1,0:T(8,128)(2,1)S(1)}, u32[]{:S(2)}, u32[]{:S(2)}) collective-permute-start(bf16[1024,256]{1,0:T(8,128)(2,1)S(1)} %get-tuple-element.40.refs_3_), channel_id=1, source_target_pairs={{4,0},{8,4},{12,8},{16,12},{20,16},{24,20},{28,24},{5,1},{9,5},{13... | collective-permute-start | bytes 1572872 | tf_op jit(solution)/shard_map/ppermute | solution.py:28
  58.8 0.8 slots.1
  59.7 0.8 shard_map.98
  60.5 0.8 shard_map.95
  61.4 3.2 %own0.1 = (f32[1024,128]{1,0:T(8,128)S(1)}, bf16[1024,256]{1,0:T(8,128)(2,1)S(1)}) custom-call(s32[4]{0:T(128)S(1)} %get-tuple-element.39.refs_0_.lives_ref, bf16[1024,256]{1,0:T(8,128)(2,1)S(1)} %get-tuple-element.41.refs_0_, bf16[1040,256]{1,0:T(8,128)(2,1)S(1)} %get-tuple-element.38.refs_1_.refs_2_), custom_call_target="tpu_custom_call" | custom-call | flops 2147483648 | bytes 1048576 | tf_op jit(solution)/shard_map/own0/pallas_call | solution.py:597
  64.6 5.3 %shard_map.93.refs_4_ = f32[1024,128]{1,0:T(8,128)S(1)} custom-call(bf16[1040,256]{1,0:T(8,128)(2,1)S(1)} %collective-permute-done.9.refs_0_.refs_3_, bf16[1040,256]{1,0:T(8,128)(2,1)S(1)} %collective-permute-done.3.refs_1_.refs_0_, bf16[1024,256]{1,0:T(8,128)(2,1)S(1)} %get-tuple-element.42.refs_2_.refs_0_, ...), custom_call_target="tpu_custom_call", output_to_operand_aliasing={{}: (3, {})} | custom-call | flops 1610612736 | bytes 1048576 | tf_op jit(solution)/shard_map/pallas_call | solution.py:600
  69.8 8.3 %own1.1 = (f32[2048,128]{1,0:T(8,128)S(1)}, bf16[2048,256]{1,0:T(8,128)(2,1)S(1)}) custom-call(s32[4]{0:T(128)S(1)} %get-tuple-element.39.refs_0_.lives_ref, bf16[1024,256]{1,0:T(8,128)(2,1)S(1)} %get-tuple-element.42.refs_2_.refs_0_, bf16[1024,256]{1,0:T(8,128)(2,1)S(1)} %get-tuple-element.43.refs_1_, ...), custom_call_target="tpu_custom_call" | custom-call | flops 6442450944 | bytes 2097152 | tf_op jit(solution)/shard_map/own1/pallas_call | solution.py:601
  78.2 6.4 %shard_map.97 = (bf16[512,128]{1,0:T(8,128)(2,1)S(1)}, bf16[512,128]{1,0:T(8,128)(2,1)S(1)}, bf16[512,128]{1,0:T(8,128)(2,1)S(1)}, bf16[512,128]{1,0:T(8,128)(2,1)S(1)}) custom-call(bf16[1040,256]{1,0:T(8,128)(2,1)S(1)} %collective-permute-done.3.refs_1_.refs_0_, bf16[1024,256]{1,0:T(8,128)(2,1)S(1)} %collective-permute-done.7.refs_1_, ...), custom_call_target="tpu_custom_call" | custom-call | flops 3758096384 | bytes 1048576 | tf_op jit(solution)/shard_map/pallas_call | solution.py:609
  84.6 0.0 copy-start.4
  84.6 0.0 copy-start.5
  84.6 2.3 %collective-permute-start.16 = (bf16[512,128]{1,0:T(8,128)(2,1)S(1)}, bf16[512,128]{1,0:T(8,128)(2,1)S(1)}, u32[]{:S(2)}, u32[]{:S(2)}) collective-permute-start(bf16[512,128]{1,0:T(8,128)(2,1)S(1)} %get-tuple-element.61), channel_id=1, source_target_pairs={{0,1},{1,2},{2,3},{3,0},{4,5},{5,6},{6,7},{7,4},{8,9},{9,10},{10,1... | collective-permute-start | bytes 393224 | tf_op jit(solution)/shard_map/ppermute | solution.py:33
  86.9 2.5 %collective-permute-start.17 = (bf16[512,128]{1,0:T(8,128)(2,1)S(1)}, bf16[512,128]{1,0:T(8,128)(2,1)S(1)}, u32[]{:S(2)}, u32[]{:S(2)}) collective-permute-start(bf16[512,128]{1,0:T(8,128)(2,1)S(1)} %get-tuple-element.62), channel_id=1, source_target_pairs={{0,2},{1,3},{2,0},{3,1},{4,6},{5,7},{6,4},{7,5},{8,10},{9,11},{10,... | collective-permute-start | bytes 393224 | tf_op jit(solution)/shard_map/ppermute | solution.py:33
  89.4 2.8 %collective-permute-start.18 = (bf16[512,128]{1,0:T(8,128)(2,1)S(1)}, bf16[512,128]{1,0:T(8,128)(2,1)S(1)}, u32[]{:S(2)}, u32[]{:S(2)}) collective-permute-start(bf16[512,128]{1,0:T(8,128)(2,1)S(1)} %get-tuple-element.63), channel_id=1, source_target_pairs={{0,3},{1,0},{2,1},{3,2},{4,7},{5,4},{6,5},{7,6},{8,11},{9,8},{10,9... | collective-permute-start | bytes 393224 | tf_op jit(solution)/shard_map/ppermute | solution.py:33
  92.3 6.8 %shard_map.94 = (bf16[512,128]{1,0:T(8,128)(2,1)S(1)}, bf16[512,128]{1,0:T(8,128)(2,1)S(1)}, bf16[512,128]{1,0:T(8,128)(2,1)S(1)}, bf16[512,128]{1,0:T(8,128)(2,1)S(1)}) custom-call(bf16[1040,256]{1,0:T(8,128)(2,1)S(1)} %collective-permute-done.3.refs_1_.refs_0_, bf16[1024,256]{1,0:T(8,128)(2,1)S(1)} %collective-permute-done.7.refs_1_, ...), custom_call_target="tpu_custom_call" | custom-call | flops 3758096384 | bytes 1048576 | tf_op jit(solution)/shard_map/pallas_call | solution.py:609
  99.1 0.1 collective-permute-start.10
  99.2 0.6 collective-permute-start.11
  99.7 3.3 %collective-permute-start.12 = (bf16[512,128]{1,0:T(8,128)(2,1)S(1)}, bf16[512,128]{1,0:T(8,128)(2,1)S(1)}, u32[]{:S(2)}, u32[]{:S(2)}) collective-permute-start(bf16[512,128]{1,0:T(8,128)(2,1)S(1)} %get-tuple-element.51), channel_id=1, source_target_pairs={{0,3},{1,0},{2,1},{3,2},{4,7},{5,4},{6,5},{7,6},{8,11},{9,8},{10,9... | collective-permute-start | bytes 393224 | tf_op jit(solution)/shard_map/ppermute | solution.py:33
  103.0 4.6 %shard_map.99 = (bf16[256,512]{1,0:T(8,128)(2,1)S(1)}, bf16[256,512]{1,0:T(8,128)(2,1)S(1)}, bf16[256,512]{1,0:T(8,128)(2,1)S(1)}, bf16[256,512]{1,0:T(8,128)(2,1)S(1)}) custom-call(s32[1]{0:T(128)} %bitcast.me.me_ref, bf16[512,128]{1,0:T(8,128)(2,1)S(1)} %get-tuple-element.60.refs_0_, bf16[512,128]{1,0:T(8,128)(2,1)S(1)} %collective-permute-done.16.refs_1_, ...), custom_call_target="tpu_custom_call" | custom-call | flops 3221225472 | bytes 2097152 | tf_op jit(solution)/shard_map/pallas_call | solution.py:620
  107.7 3.9 %collective-permute-start.19 = (bf16[256,512]{1,0:T(8,128)(2,1)S(1)}, bf16[256,512]{1,0:T(8,128)(2,1)S(1)}, u32[]{:S(2)}, u32[]{:S(2)}) collective-permute-start(bf16[256,512]{1,0:T(8,128)(2,1)S(1)} %get-tuple-element.66), channel_id=1, source_target_pairs={{3,1},{0,2},{7,5},{4,6},{11,9},{8,10},{15,13},{12,14},{19,17},{16,... | collective-permute-start | bytes 786440 | tf_op jit(solution)/shard_map/ppermute | solution.py:624
  111.6 1.3 collective-permute-start.20
  112.9 0.7 collective-permute-start.21
  113.6 4.6 %shard_map.96 = (bf16[256,512]{1,0:T(8,128)(2,1)S(1)}, bf16[256,512]{1,0:T(8,128)(2,1)S(1)}, bf16[256,512]{1,0:T(8,128)(2,1)S(1)}, bf16[256,512]{1,0:T(8,128)(2,1)S(1)}) custom-call(s32[1]{0:T(128)} %bitcast.me.me_ref, bf16[512,128]{1,0:T(8,128)(2,1)S(1)} %get-tuple-element.48.refs_0_, bf16[512,128]{1,0:T(8,128)(2,1)S(1)} %collective-permute-done.10.refs_1_, ...), custom_call_target="tpu_custom_call" | custom-call | flops 3221225472 | bytes 2097152 | tf_op jit(solution)/shard_map/pallas_call | solution.py:620
  118.3 1.3 collective-permute-start.13
  119.6 1.3 collective-permute-start.14
  120.9 9.3 %collective-permute-start.15 = (bf16[256,512]{1,0:T(8,128)(2,1)S(1)}, bf16[256,512]{1,0:T(8,128)(2,1)S(1)}, u32[]{:S(2)}, u32[]{:S(2)}) collective-permute-start(bf16[256,512]{1,0:T(8,128)(2,1)S(1)} %get-tuple-element.58), channel_id=1, source_target_pairs={{3,0},{0,3},{7,4},{4,7},{11,8},{8,11},{15,12},{12,15},{19,16},{16,... | collective-permute-start | bytes 786440 | tf_op jit(solution)/shard_map/ppermute | solution.py:624
  130.3 11.7 %collective-permute-done.13.refs_0_ = bf16[256,512]{1,0:T(8,128)(2,1)S(1)} collective-permute-done((bf16[256,512]{1,0:T(8,128)(2,1)S(1)}, bf16[256,512]{1,0:T(8,128)(2,1)S(1)}, u32[]{:S(2)}, u32[]{:S(2)}) %collective-permute-start.13) | collective-permute-done | bytes 262176 | tf_op jit(solution)/shard_map/ppermute | solution.py:624
  142.0 1.6 %mix.1 = bf16[512,512]{1,0:T(8,128)(2,1)} custom-call(s32[1]{0:T(128)} %bitcast.me.me_ref, bf16[256,512]{1,0:T(8,128)(2,1)S(1)} %collective-permute-done.13.refs_0_, bf16[256,512]{1,0:T(8,128)(2,1)S(1)} %collective-permute-done.14.refs_1_, bf16[256,512]{1,0:T(8,128)(2,1)S(1)} %collective-permute-done.15.refs_2_, ...), custom_call_target="tpu_custom_call" | custom-call | flops 536870912 | bytes 2097152 | tf_op jit(solution)/shard_map/mix/pallas_call | solution.py:627
  (30 shorter events, 0.1 us)
Async XLA Ops:
  0.0 41.5 %copy-start.2 = (f32[3,512]{1,0:T(4,128)S(1)}, f32[3,512]{1,0:T(4,128)}, u32[]{:S(2)}) copy-start(f32[3,512]{1,0:T(4,128)} %refs_6_.3) | copy-start | bytes 18436
  1.4 58.3 %copy-start.1 = (bf16[512,2048]{1,0:T(8,128)(2,1)S(1)}, bf16[512,2048]{1,0:T(8,128)(2,1)}, u32[]{:S(2)}) copy-start(bf16[512,2048]{1,0:T(8,128)(2,1)} %refs_4_.5) | copy-start | bytes 6291460
  9.1 13.6 %collective-permute-start = (bf16[1040,128]{1,0:T(8,128)(2,1)S(1)}, bf16[1040,128]{1,0:T(8,128)(2,1)}, u32[]{:S(2)}, u32[]{:S(2)}) collective-permute-start(bf16[1040,128]{1,0:T(8,128)(2,1)S(1)} %pad_maximum_fusion.refs_0_), channel_id=1, source_target_pairs={{0,1},{1,2},{2,3},{3,0},{4,5},{5,6},{6,7},{7,4},{8,9},{9,10},{10,1... | collective-permute-start | bytes 798728 | tf_op jit(solution)/shard_map/ppermute | solution.py:33
  18.8 11.2 %collective-permute-start.4 = (bf16[1040,128]{1,0:T(8,128)(2,1)S(1)}, bf16[1040,128]{1,0:T(8,128)(2,1)S(1)}, u32[]{:S(2)}, u32[]{:S(2)}) collective-permute-start(bf16[1040,128]{1,0:T(8,128)(2,1)S(1)} %fusion.1.refs_1_.refs_0_), channel_id=1, source_target_pairs={{0,1},{1,2},{2,3},{3,0},{4,5},{5,6},{6,7},{7,4},{8,9},{9,10},{10,1... | collective-permute-start | bytes 798728 | tf_op jit(solution)/shard_map/ppermute | solution.py:33
  20.4 15.4 %collective-permute-start.1 = (bf16[1040,128]{1,0:T(8,128)(2,1)S(1)}, bf16[1040,128]{1,0:T(8,128)(2,1)}, u32[]{:S(2)}, u32[]{:S(2)}) collective-permute-start(bf16[1040,128]{1,0:T(8,128)(2,1)S(1)} %pad_maximum_fusion.refs_0_), channel_id=1, source_target_pairs={{0,3},{1,0},{2,1},{3,2},{4,7},{5,4},{6,5},{7,6},{8,11},{9,8},{10,9... | collective-permute-start | bytes 798728 | tf_op jit(solution)/shard_map/ppermute | solution.py:33
  22.7 18.8 %collective-permute-start.2 = (bf16[1040,128]{1,0:T(8,128)(2,1)}, bf16[1040,128]{1,0:T(8,128)(2,1)}, u32[]{:S(2)}, u32[]{:S(2)}) collective-permute-start(bf16[1040,128]{1,0:T(8,128)(2,1)} %collective-permute-done.refs_1_), channel_id=1, source_target_pairs={{0,1},{1,2},{2,3},{3,0},{4,5},{5,6},{6,7},{7,4},{8,9},{9,10},{10,1... | collective-permute-start | bytes 798728 | tf_op jit(solution)/shard_map/ppermute | solution.py:33
  22.7 27.0 %collective-permute-start.5 = (bf16[1040,128]{1,0:T(8,128)(2,1)S(1)}, bf16[1040,128]{1,0:T(8,128)(2,1)S(1)}, u32[]{:S(2)}, u32[]{:S(2)}) collective-permute-start(bf16[1040,128]{1,0:T(8,128)(2,1)S(1)} %fusion.1.refs_1_.refs_0_), channel_id=1, source_target_pairs={{0,3},{1,0},{2,1},{3,2},{4,7},{5,4},{6,5},{7,6},{8,11},{9,8},{10,9... | collective-permute-start | bytes 798728 | tf_op jit(solution)/shard_map/ppermute | solution.py:33
  30.0 21.5 %collective-permute-start.6 = (bf16[1040,128]{1,0:T(8,128)(2,1)S(1)}, bf16[1040,128]{1,0:T(8,128)(2,1)S(1)}, u32[]{:S(2)}, u32[]{:S(2)}) collective-permute-start(bf16[1040,128]{1,0:T(8,128)(2,1)S(1)} %collective-permute-done.4.refs_2_.refs_1_), channel_id=1, source_target_pairs={{0,1},{1,2},{2,3},{3,0},{4,5},{5,6},{6,7},{7,4},{8,9},{9,10},{10,1... | collective-permute-start | bytes 798728 | tf_op jit(solution)/shard_map/ppermute | solution.py:33
  34.1 1.6 %copy-start = (bf16[512,2048]{1,0:T(8,128)(2,1)S(1)}, bf16[512,2048]{1,0:T(8,128)(2,1)}, u32[]{:S(2)}) copy-start(bf16[512,2048]{1,0:T(8,128)(2,1)} %refs_4_.5) | copy-start | bytes 6291460
  44.1 20.5 %collective-permute-start.9 = (bf16[1040,256]{1,0:T(8,128)(2,1)S(1)}, bf16[1040,256]{1,0:T(8,128)(2,1)S(1)}, u32[]{:S(2)}, u32[]{:S(2)}) collective-permute-start(bf16[1040,256]{1,0:T(8,128)(2,1)S(1)} %get-tuple-element.38.refs_1_.refs_2_), channel_id=1, source_target_pairs={{0,4},{4,8},{8,12},{12,16},{16,20},{20,24},{24,28},{1,5},{5,9},{9,... | collective-permute-start | bytes 1597448 | tf_op jit(solution)/shard_map/ppermute | solution.py:28
  46.0 18.6 %collective-permute-start.3 = (bf16[1040,256]{1,0:T(8,128)(2,1)S(1)}, bf16[1040,256]{1,0:T(8,128)(2,1)S(1)}, u32[]{:S(2)}, u32[]{:S(2)}) collective-permute-start(bf16[1040,256]{1,0:T(8,128)(2,1)S(1)} %get-tuple-element.38.refs_1_.refs_2_), channel_id=1, source_target_pairs={{4,0},{8,4},{12,8},{16,12},{20,16},{24,20},{28,24},{5,1},{9,5},{13... | collective-permute-start | bytes 1597448 | tf_op jit(solution)/shard_map/ppermute | solution.py:28
  53.2 25.0 %collective-permute-start.8 = (bf16[1024,256]{1,0:T(8,128)(2,1)S(1)}, bf16[1024,256]{1,0:T(8,128)(2,1)S(1)}, u32[]{:S(2)}, u32[]{:S(2)}) collective-permute-start(bf16[1024,256]{1,0:T(8,128)(2,1)S(1)} %get-tuple-element.40.refs_3_), channel_id=1, source_target_pairs={{0,4},{4,8},{8,12},{12,16},{16,20},{20,24},{24,28},{1,5},{5,9},{9,... | collective-permute-start | bytes 1572872 | tf_op jit(solution)/shard_map/ppermute | solution.py:28
  55.2 23.1 %collective-permute-start.7 = (bf16[1024,256]{1,0:T(8,128)(2,1)S(1)}, bf16[1024,256]{1,0:T(8,128)(2,1)S(1)}, u32[]{:S(2)}, u32[]{:S(2)}) collective-permute-start(bf16[1024,256]{1,0:T(8,128)(2,1)S(1)} %get-tuple-element.40.refs_3_), channel_id=1, source_target_pairs={{4,0},{8,4},{12,8},{16,12},{20,16},{24,20},{28,24},{5,1},{9,5},{13... | collective-permute-start | bytes 1572872 | tf_op jit(solution)/shard_map/ppermute | solution.py:28
  84.6 18.4 %copy-start.3 = (bf16[1,512,4096]{2,1,0:T(8,128)(2,1)S(1)}, bf16[1,512,4096]{2,1,0:T(8,128)(2,1)}, u32[]{:S(2)}) copy-start(bf16[1,512,4096]{2,1,0:T(8,128)(2,1)} %refs_8_.3) | copy-start | bytes 12582916
  84.6 18.4 %copy-start.4 = (bf16[1,2048,512]{2,1,0:T(8,128)(2,1)S(1)}, bf16[1,2048,512]{2,1,0:T(8,128)(2,1)}, u32[]{:S(2)}) copy-start(bf16[1,2048,512]{2,1,0:T(8,128)(2,1)} %refs_9_.3) | copy-start | bytes 6291460
  84.6 18.4 %copy-start.5 = (bf16[512,512]{1,0:T(8,128)(2,1)S(1)}, bf16[512,512]{1,0:T(8,128)(2,1)}, u32[]{:S(2)}) copy-start(bf16[512,512]{1,0:T(8,128)(2,1)} %refs_7_.3) | copy-start | bytes 1572868
  84.6 15.1 %collective-permute-start.16 = (bf16[512,128]{1,0:T(8,128)(2,1)S(1)}, bf16[512,128]{1,0:T(8,128)(2,1)S(1)}, u32[]{:S(2)}, u32[]{:S(2)}) collective-permute-start(bf16[512,128]{1,0:T(8,128)(2,1)S(1)} %get-tuple-element.61), channel_id=1, source_target_pairs={{0,1},{1,2},{2,3},{3,0},{4,5},{5,6},{6,7},{7,4},{8,9},{9,10},{10,1... | collective-permute-start | bytes 393224 | tf_op jit(solution)/shard_map/ppermute | solution.py:33
  86.9 16.0 %collective-permute-start.17 = (bf16[512,128]{1,0:T(8,128)(2,1)S(1)}, bf16[512,128]{1,0:T(8,128)(2,1)S(1)}, u32[]{:S(2)}, u32[]{:S(2)}) collective-permute-start(bf16[512,128]{1,0:T(8,128)(2,1)S(1)} %get-tuple-element.62), channel_id=1, source_target_pairs={{0,2},{1,3},{2,0},{3,1},{4,6},{5,7},{6,4},{7,5},{8,10},{9,11},{10,... | collective-permute-start | bytes 393224 | tf_op jit(solution)/shard_map/ppermute | solution.py:33
  89.4 13.6 %collective-permute-start.18 = (bf16[512,128]{1,0:T(8,128)(2,1)S(1)}, bf16[512,128]{1,0:T(8,128)(2,1)S(1)}, u32[]{:S(2)}, u32[]{:S(2)}) collective-permute-start(bf16[512,128]{1,0:T(8,128)(2,1)S(1)} %get-tuple-element.63), channel_id=1, source_target_pairs={{0,3},{1,0},{2,1},{3,2},{4,7},{5,4},{6,5},{7,6},{8,11},{9,8},{10,9... | collective-permute-start | bytes 393224 | tf_op jit(solution)/shard_map/ppermute | solution.py:33
  99.1 13.8 %collective-permute-start.10 = (bf16[512,128]{1,0:T(8,128)(2,1)S(1)}, bf16[512,128]{1,0:T(8,128)(2,1)S(1)}, u32[]{:S(2)}, u32[]{:S(2)}) collective-permute-start(bf16[512,128]{1,0:T(8,128)(2,1)S(1)} %get-tuple-element.49), channel_id=1, source_target_pairs={{0,1},{1,2},{2,3},{3,0},{4,5},{5,6},{6,7},{7,4},{8,9},{9,10},{10,1... | collective-permute-start | bytes 393224 | tf_op jit(solution)/shard_map/ppermute | solution.py:33
  99.2 14.5 %collective-permute-start.11 = (bf16[512,128]{1,0:T(8,128)(2,1)S(1)}, bf16[512,128]{1,0:T(8,128)(2,1)S(1)}, u32[]{:S(2)}, u32[]{:S(2)}) collective-permute-start(bf16[512,128]{1,0:T(8,128)(2,1)S(1)} %get-tuple-element.50), channel_id=1, source_target_pairs={{0,2},{1,3},{2,0},{3,1},{4,6},{5,7},{6,4},{7,5},{8,10},{9,11},{10,... | collective-permute-start | bytes 393224 | tf_op jit(solution)/shard_map/ppermute | solution.py:33
  99.7 13.9 %collective-permute-start.12 = (bf16[512,128]{1,0:T(8,128)(2,1)S(1)}, bf16[512,128]{1,0:T(8,128)(2,1)S(1)}, u32[]{:S(2)}, u32[]{:S(2)}) collective-permute-start(bf16[512,128]{1,0:T(8,128)(2,1)S(1)} %get-tuple-element.51), channel_id=1, source_target_pairs={{0,3},{1,0},{2,1},{3,2},{4,7},{5,4},{6,5},{7,6},{8,11},{9,8},{10,9... | collective-permute-start | bytes 393224 | tf_op jit(solution)/shard_map/ppermute | solution.py:33
  107.7 13.2 %collective-permute-start.19 = (bf16[256,512]{1,0:T(8,128)(2,1)S(1)}, bf16[256,512]{1,0:T(8,128)(2,1)S(1)}, u32[]{:S(2)}, u32[]{:S(2)}) collective-permute-start(bf16[256,512]{1,0:T(8,128)(2,1)S(1)} %get-tuple-element.66), channel_id=1, source_target_pairs={{3,1},{0,2},{7,5},{4,6},{11,9},{8,10},{15,13},{12,14},{19,17},{16,... | collective-permute-start | bytes 786440 | tf_op jit(solution)/shard_map/ppermute | solution.py:624
  111.6 18.6 %collective-permute-start.20 = (bf16[256,512]{1,0:T(8,128)(2,1)S(1)}, bf16[256,512]{1,0:T(8,128)(2,1)S(1)}, u32[]{:S(2)}, u32[]{:S(2)}) collective-permute-start(bf16[256,512]{1,0:T(8,128)(2,1)S(1)} %get-tuple-element.67), channel_id=1, source_target_pairs={{0,1},{3,2},{4,5},{7,6},{8,9},{11,10},{12,13},{15,14},{16,17},{19,... | collective-permute-start | bytes 786440 | tf_op jit(solution)/shard_map/ppermute | solution.py:624
  112.9 17.3 %collective-permute-start.21 = (bf16[256,512]{1,0:T(8,128)(2,1)S(1)}, bf16[256,512]{1,0:T(8,128)(2,1)S(1)}, u32[]{:S(2)}, u32[]{:S(2)}) collective-permute-start(bf16[256,512]{1,0:T(8,128)(2,1)S(1)} %get-tuple-element.68), channel_id=1, source_target_pairs={{2,1},{1,2},{6,5},{5,6},{10,9},{9,10},{14,13},{13,14},{18,17},{17,... | collective-permute-start | bytes 786440 | tf_op jit(solution)/shard_map/ppermute | solution.py:624
  118.3 23.7 %collective-permute-start.13 = (bf16[256,512]{1,0:T(8,128)(2,1)S(1)}, bf16[256,512]{1,0:T(8,128)(2,1)S(1)}, u32[]{:S(2)}, u32[]{:S(2)}) collective-permute-start(bf16[256,512]{1,0:T(8,128)(2,1)S(1)} %get-tuple-element.56), channel_id=1, source_target_pairs={{1,0},{2,3},{5,4},{6,7},{9,8},{10,11},{13,12},{14,15},{17,16},{18,... | collective-permute-start | bytes 786440 | tf_op jit(solution)/shard_map/ppermute | solution.py:624
  119.6 22.4 %collective-permute-start.14 = (bf16[256,512]{1,0:T(8,128)(2,1)S(1)}, bf16[256,512]{1,0:T(8,128)(2,1)S(1)}, u32[]{:S(2)}, u32[]{:S(2)}) collective-permute-start(bf16[256,512]{1,0:T(8,128)(2,1)S(1)} %get-tuple-element.57), channel_id=1, source_target_pairs={{2,0},{1,3},{6,4},{5,7},{10,8},{9,11},{14,12},{13,15},{18,16},{17,... | collective-permute-start | bytes 786440 | tf_op jit(solution)/shard_map/ppermute | solution.py:624
  120.9 21.1 %collective-permute-start.15 = (bf16[256,512]{1,0:T(8,128)(2,1)S(1)}, bf16[256,512]{1,0:T(8,128)(2,1)S(1)}, u32[]{:S(2)}, u32[]{:S(2)}) collective-permute-start(bf16[256,512]{1,0:T(8,128)(2,1)S(1)} %get-tuple-element.58), channel_id=1, source_target_pairs={{3,0},{0,3},{7,4},{4,7},{11,8},{8,11},{15,12},{12,15},{19,16},{16,... | collective-permute-start | bytes 786440 | tf_op jit(solution)/shard_map/ppermute | solution.py:624
